TPU v7x, 32 devices: a whole 2x2x4 slice. The times are simulated.
32 devices in a mesh: tab: 4 (over y, x), blk: 8 (over z, core).
Axes of the slice: x: 2, y: 2, z: 4, core: 2. Of those that a mesh axis runs over, the one named last changes fastest.
Arguments:
- tokens: bfloat16 [8, 2048, 768], P('tab', 'blk'), may hold values from -6 to 6
- lengths: int32 [8], P('tab'), may hold values from 128 to 2048, as said below
- qkv_weight: bfloat16 [768, 2304], replicated, may hold values from -0.21875 to 0.21875
- qkv_bias: bfloat16 [1536], replicated, may hold values from -1 to 1
- out_weight: bfloat16 [768, 768], replicated, may hold values from -0.75 to 0.75
- out_bias: bfloat16 [768], replicated, may hold values from -3 to 3
- attn_gain: bfloat16 [768], replicated, may hold values from 0.5 to 1.5
- attn_shift: bfloat16 [768], replicated, may hold values from -3 to 3
- up_weight: bfloat16 [768, 3072], replicated, may hold values from -0.21875 to 0.21875
- up_bias: bfloat16 [3072], replicated, may hold values from -3 to 3
- down_weight: bfloat16 [3072, 768], replicated, may hold values from -0.109375 to 0.109375
- down_bias: bfloat16 [768], replicated, may hold values from -3 to 3
- ffn_gain: bfloat16 [768], replicated, may hold values from 0.5 to 1.5
- ffn_shift: bfloat16 [768], replicated, may hold values from -3 to 3
- cotangent: bfloat16 [8, 2048, 768], P('tab', 'blk'), may hold values from -6 to 6
Outputs:
- layer_out: bfloat16 [8, 2048, 768], P('tab', 'blk')
- token_grad: bfloat16 [8, 2048, 768], P('tab', 'blk')
- wgrad_qkv: float32 [768, 2304], P(('tab', 'blk'))
- bgrad_qkv: float32 [1536], P(('tab', 'blk'))
- wgrad_out: float32 [768, 768], P(('tab', 'blk'))
- bgrad_out: float32 [768], P(('tab', 'blk'))
- ggrad_attn: float32 [768], P(('tab', 'blk'))
- sgrad_attn: float32 [768], P(('tab', 'blk'))
- wgrad_up: float32 [768, 3072], P(('tab', 'blk'))
- bgrad_up: float32 [3072], P(('tab', 'blk'))
- wgrad_down: float32 [3072, 768], P(('tab', 'blk'))
- bgrad_down: float32 [768], P(('tab', 'blk'))
- ggrad_ffn: float32 [768], P(('tab', 'blk'))
- sgrad_ffn: float32 [768], P(('tab', 'blk'))
Inputs may be any that keep to these rules, and one draw needn't show every extreme that they name: `lengths`: among each 2 consecutive tables one, drawn from the seed, has exactly 2048 tokens.
All inputs are finite; a program needn't handle non-finite values.
Results may differ from a plain program's by a relative error of at most 0.023.
Values may be sent and summed in bfloat16 or wider, within the bound.
A program may use at most 192 MiB of HBM per device.

v0:
```python
import jax
import jax.numpy as jnp
from jax import lax
from jax.sharding import PartitionSpec as P

HD = 64


EPSILON = 1e-05
NEGATIVE = -1e30


def from_behind(block, axis, distance):
    devices = range(lax.axis_size(axis))
    route = [((i - distance) % len(devices), i) for i in devices]
    return lax.ppermute(block, axis, route)


def norm_rows(inputs, gains, shifts):
    row_mean = jnp.mean(inputs, axis=-1, keepdims=True)
    centred = inputs - row_mean
    row_var = jnp.mean(centred * centred, axis=-1, keepdims=True)
    return centred * lax.rsqrt(row_var + EPSILON) * gains + shifts


def gelu_exact(inputs):
    return jax.nn.gelu(inputs, approximate=False)


def times_back(left, right):
    return lax.dot_general(
        left, right, (((1,), (1,)), ((), ())), preferred_element_type=jnp.float32
    )


def over_rows(left, right):
    return lax.dot_general(
        left, right, (((0,), (0,)), ((), ())), preferred_element_type=jnp.float32
    )


def shards(
    tokens,
    lengths,
    qkv_weight,
    qkv_bias,
    out_weight,
    out_bias,
    attn_gain,
    attn_shift,
    up_weight,
    up_bias,
    down_weight,
    down_bias,
    ffn_gain,
    ffn_shift,
    cotangent,
):
    table_count, row_count, model_width = tokens.shape
    head_count = model_width // HD
    cycle_size = lax.axis_size("blk")
    cycle_place = lax.axis_index("blk")
    score_scale = HD ** (-0.5)
    flat_tokens = tokens.reshape(table_count * row_count, model_width)
    bias_full = jnp.concatenate(
        [
            qkv_bias[:model_width].astype(jnp.float32),
            jnp.zeros((model_width,), jnp.float32),
            qkv_bias[model_width:].astype(jnp.float32),
        ]
    )
    qkv_low = (
        jnp.dot(flat_tokens, qkv_weight, preferred_element_type=jnp.float32) + bias_full
    ).astype(jnp.bfloat16)
    queries = qkv_low[:, :model_width].reshape(table_count, row_count, head_count, HD)
    key_values = qkv_low[:, model_width:].reshape(table_count, row_count, 2 * model_width)

    def key_mask(first_row, key_count):
        positions = first_row + jnp.arange(key_count, dtype=jnp.int32)
        return (positions[None, :] < lengths[:, None])[:, None, None, :]

    def split_pair(pair_block):
        key_count = pair_block.shape[1]
        keys_part = pair_block[:, :, :model_width].reshape(table_count, key_count, head_count, HD)
        values_part = pair_block[:, :, model_width:].reshape(table_count, key_count, head_count, HD)
        return (keys_part, values_part)

    pair_block = lax.all_gather(key_values, "blk", axis=1, tiled=True)
    running_max = jnp.full((table_count, row_count, head_count), NEGATIVE, jnp.float32)
    keys_part, values_part = split_pair(pair_block)
    is_valid = key_mask(jnp.int32(0), pair_block.shape[1])
    raw_scores = jnp.einsum(
        "trhd,tkhd->trhk", queries, keys_part, preferred_element_type=jnp.float32
    )
    scores = jnp.where(is_valid, raw_scores * score_scale, NEGATIVE)
    peak_new = jnp.maximum(running_max, jnp.max(scores, axis=-1))
    exponent = jnp.where(is_valid, jnp.exp(scores - peak_new[..., None]), 0.0)
    running_sum = jnp.sum(exponent, axis=-1)
    weighted = jnp.einsum(
        "trhk,tkhd->trhd",
        exponent.astype(jnp.bfloat16),
        values_part,
        preferred_element_type=jnp.float32,
    )
    running_max, running_sum, weighted = (peak_new, running_sum, weighted)
    context = weighted / running_sum[..., None]
    log_total = running_max + jnp.log(running_sum)
    context_low = context.reshape(table_count * row_count, model_width).astype(jnp.bfloat16)
    attended = jnp.dot(
        context_low, out_weight, preferred_element_type=jnp.float32
    ) + out_bias.astype(jnp.float32)
    pre_one = flat_tokens.astype(jnp.float32) + attended
    gain_one = attn_gain.astype(jnp.float32)
    shift_one = attn_shift.astype(jnp.float32)
    hidden = norm_rows(pre_one, gain_one, shift_one)
    hidden_low = hidden.astype(jnp.bfloat16)
    upper = jnp.dot(hidden_low, up_weight, preferred_element_type=jnp.float32) + up_bias.astype(
        jnp.float32
    )
    active = gelu_exact(upper).astype(jnp.bfloat16)
    pre_two = (
        hidden
        + jnp.dot(active, down_weight, preferred_element_type=jnp.float32)
        + down_bias.astype(jnp.float32)
    )
    gain_two = ffn_gain.astype(jnp.float32)
    shift_two = ffn_shift.astype(jnp.float32)
    layer_out = norm_rows(pre_two, gain_two, shift_two).astype(jnp.bfloat16).reshape(tokens.shape)
    grad_out = cotangent.reshape(table_count * row_count, model_width).astype(jnp.float32)
    _, norm_two_back = jax.vjp(norm_rows, pre_two, gain_two, shift_two)
    grad_pre_two, ggrad_ffn, sgrad_ffn = norm_two_back(grad_out)
    grad_branch = grad_pre_two.astype(jnp.bfloat16)
    wgrad_down = over_rows(active, grad_branch)
    bgrad_down = jnp.sum(grad_branch, axis=0, dtype=jnp.float32)
    grad_active = times_back(grad_branch, down_weight)
    _, gelu_back = jax.vjp(gelu_exact, upper)
    grad_upper = gelu_back(grad_active)[0].astype(jnp.bfloat16)
    wgrad_up = over_rows(hidden_low, grad_upper)
    bgrad_up = jnp.sum(grad_upper, axis=0, dtype=jnp.float32)
    grad_hidden = grad_pre_two + times_back(grad_upper, up_weight)
    _, norm_one_back = jax.vjp(norm_rows, pre_one, gain_one, shift_one)
    grad_pre_one, ggrad_attn, sgrad_attn = norm_one_back(grad_hidden)
    grad_attended = grad_pre_one.astype(jnp.bfloat16)
    wgrad_out = over_rows(context_low, grad_attended)
    bgrad_out = jnp.sum(grad_attended, axis=0, dtype=jnp.float32)
    grad_context = times_back(grad_attended, out_weight).astype(jnp.bfloat16)
    grad_heads = grad_context.reshape(table_count, row_count, head_count, HD)
    row_delta = jnp.sum(grad_heads.astype(jnp.float32) * context, axis=-1)

    def cycle_turn_step(cycle_turn, cycle_state):
        pair_now, pair_grads, grad_queries = cycle_state
        owner_index = (cycle_place - cycle_turn) % cycle_size
        keys_part, values_part = split_pair(pair_now)
        is_valid = key_mask(owner_index * row_count, row_count)
        raw_scores = jnp.einsum(
            "trhd,tkhd->trhk", queries, keys_part, preferred_element_type=jnp.float32
        )
        scores = jnp.where(is_valid, raw_scores * score_scale, NEGATIVE)
        probs = jnp.where(is_valid, jnp.exp(scores - log_total[..., None]), 0.0)
        grad_probs = jnp.einsum(
            "trhd,tkhd->trhk", grad_heads, values_part, preferred_element_type=jnp.float32
        )
        grad_raw = (probs * (grad_probs - row_delta[..., None]) * score_scale).astype(jnp.bfloat16)
        grad_queries = grad_queries + jnp.einsum(
            "trhk,tkhd->trhd", grad_raw, keys_part, preferred_element_type=jnp.float32
        )
        grad_keys = jnp.einsum(
            "trhk,trhd->tkhd", grad_raw, queries, preferred_element_type=jnp.float32
        )
        grad_values = jnp.einsum(
            "trhk,trhd->tkhd",
            probs.astype(jnp.bfloat16),
            grad_heads,
            preferred_element_type=jnp.float32,
        )
        pair_grads = pair_grads + jnp.concatenate(
            [
                grad_keys.reshape(table_count, row_count, model_width),
                grad_values.reshape(table_count, row_count, model_width),
            ],
            axis=-1,
        )
        pair_next = from_behind(pair_now, "blk", 1)
        grads_next = from_behind(pair_grads.astype(jnp.bfloat16), "blk", 1).astype(pair_grads.dtype)
        return (pair_next, grads_next, grad_queries)

    cycle_start = (
        key_values,
        jnp.zeros((table_count, row_count, 2 * model_width), jnp.float32),
        jnp.zeros((table_count, row_count, head_count, HD), jnp.float32),
    )
    _, pair_home, grad_queries = lax.fori_loop(0, cycle_size, cycle_turn_step, cycle_start)
    grad_qkv = jnp.concatenate(
        [
            grad_queries.reshape(table_count * row_count, model_width),
            pair_home.reshape(table_count * row_count, 2 * model_width),
        ],
        axis=-1,
    ).astype(jnp.bfloat16)
    wgrad_qkv = over_rows(flat_tokens, grad_qkv)
    column_sums = jnp.sum(grad_qkv, axis=0, dtype=jnp.float32)
    bgrad_qkv = jnp.concatenate([column_sums[:model_width], column_sums[2 * model_width :]])
    token_grad = (
        (grad_pre_one + times_back(grad_qkv, qkv_weight)).astype(jnp.bfloat16).reshape(tokens.shape)
    )
    (
        wgrad_qkv,
        bgrad_qkv,
        wgrad_out,
        bgrad_out,
        ggrad_attn,
        sgrad_attn,
        wgrad_up,
        bgrad_up,
        wgrad_down,
        bgrad_down,
        ggrad_ffn,
        sgrad_ffn,
    ) = (
        lax.psum_scatter(
            wgrad_qkv.astype(jnp.bfloat16), "tab", scatter_dimension=0, tiled=True
        ).astype(jnp.float32),
        lax.psum_scatter(
            bgrad_qkv.astype(jnp.bfloat16), "tab", scatter_dimension=0, tiled=True
        ).astype(jnp.float32),
        lax.psum_scatter(
            wgrad_out.astype(jnp.bfloat16), "tab", scatter_dimension=0, tiled=True
        ).astype(jnp.float32),
        lax.psum_scatter(
            bgrad_out.astype(jnp.bfloat16), "tab", scatter_dimension=0, tiled=True
        ).astype(jnp.float32),
        lax.psum_scatter(
            ggrad_attn.astype(jnp.bfloat16), "tab", scatter_dimension=0, tiled=True
        ).astype(jnp.float32),
        lax.psum_scatter(
            sgrad_attn.astype(jnp.bfloat16), "tab", scatter_dimension=0, tiled=True
        ).astype(jnp.float32),
        lax.psum_scatter(
            wgrad_up.astype(jnp.bfloat16), "tab", scatter_dimension=0, tiled=True
        ).astype(jnp.float32),
        lax.psum_scatter(
            bgrad_up.astype(jnp.bfloat16), "tab", scatter_dimension=0, tiled=True
        ).astype(jnp.float32),
        lax.psum_scatter(
            wgrad_down.astype(jnp.bfloat16), "tab", scatter_dimension=0, tiled=True
        ).astype(jnp.float32),
        lax.psum_scatter(
            bgrad_down.astype(jnp.bfloat16), "tab", scatter_dimension=0, tiled=True
        ).astype(jnp.float32),
        lax.psum_scatter(
            ggrad_ffn.astype(jnp.bfloat16), "tab", scatter_dimension=0, tiled=True
        ).astype(jnp.float32),
        lax.psum_scatter(
            sgrad_ffn.astype(jnp.bfloat16), "tab", scatter_dimension=0, tiled=True
        ).astype(jnp.float32),
    )
    (
        wgrad_qkv,
        bgrad_qkv,
        wgrad_out,
        bgrad_out,
        ggrad_attn,
        sgrad_attn,
        wgrad_up,
        bgrad_up,
        wgrad_down,
        bgrad_down,
        ggrad_ffn,
        sgrad_ffn,
    ) = (
        lax.psum_scatter(
            wgrad_qkv.astype(jnp.bfloat16), "blk", scatter_dimension=0, tiled=True
        ).astype(jnp.float32),
        lax.psum_scatter(
            bgrad_qkv.astype(jnp.bfloat16), "blk", scatter_dimension=0, tiled=True
        ).astype(jnp.float32),
        lax.psum_scatter(
            wgrad_out.astype(jnp.bfloat16), "blk", scatter_dimension=0, tiled=True
        ).astype(jnp.float32),
        lax.psum_scatter(
            bgrad_out.astype(jnp.bfloat16), "blk", scatter_dimension=0, tiled=True
        ).astype(jnp.float32),
        lax.psum_scatter(
            ggrad_attn.astype(jnp.bfloat16), "blk", scatter_dimension=0, tiled=True
        ).astype(jnp.float32),
        lax.psum_scatter(
            sgrad_attn.astype(jnp.bfloat16), "blk", scatter_dimension=0, tiled=True
        ).astype(jnp.float32),
        lax.psum_scatter(
            wgrad_up.astype(jnp.bfloat16), "blk", scatter_dimension=0, tiled=True
        ).astype(jnp.float32),
        lax.psum_scatter(
            bgrad_up.astype(jnp.bfloat16), "blk", scatter_dimension=0, tiled=True
        ).astype(jnp.float32),
        lax.psum_scatter(
            wgrad_down.astype(jnp.bfloat16), "blk", scatter_dimension=0, tiled=True
        ).astype(jnp.float32),
        lax.psum_scatter(
            bgrad_down.astype(jnp.bfloat16), "blk", scatter_dimension=0, tiled=True
        ).astype(jnp.float32),
        lax.psum_scatter(
            ggrad_ffn.astype(jnp.bfloat16), "blk", scatter_dimension=0, tiled=True
        ).astype(jnp.float32),
        lax.psum_scatter(
            sgrad_ffn.astype(jnp.bfloat16), "blk", scatter_dimension=0, tiled=True
        ).astype(jnp.float32),
    )
    return (
        layer_out,
        token_grad,
        wgrad_qkv,
        bgrad_qkv,
        wgrad_out,
        bgrad_out,
        ggrad_attn,
        sgrad_attn,
        wgrad_up,
        bgrad_up,
        wgrad_down,
        bgrad_down,
        ggrad_ffn,
        sgrad_ffn,
    )


def solution(mesh):
    in_specs = (
        P("tab", "blk", None),
        P("tab"),
        P(),
        P(),
        P(),
        P(),
        P(),
        P(),
        P(),
        P(),
        P(),
        P(),
        P(),
        P(),
        P("tab", "blk", None),
    )
    out_specs = (
        P("tab", "blk", None),
        P("tab", "blk", None),
        P(("tab", "blk"), None),
        P(("tab", "blk")),
        P(("tab", "blk"), None),
        P(("tab", "blk")),
        P(("tab", "blk")),
        P(("tab", "blk")),
        P(("tab", "blk"), None),
        P(("tab", "blk")),
        P(("tab", "blk"), None),
        P(("tab", "blk")),
        P(("tab", "blk")),
        P(("tab", "blk")),
    )
    return jax.shard_map(shards, mesh=mesh, in_specs=in_specs, out_specs=out_specs, check_vma=False)
```

profile of v0, /device:TPU:0, one launch (start us, length us, event | category | flops | bytes accessed | tf_op | source)
XLA Modules:
  0.0 1047.5 jit_solution(7722632652528159522)
XLA Ops:
  9.2 3.1 fusion.28
  34.3 100.4 %all-gather.2.cloned.1.call-done = bf16[2,2048,1536]{2,1,0:T(8,128)(2,1)} async-done(((bf16[2,256,1536]{2,1,0:T(8,128)(2,1)}), bf16[2,2048,1536]{2,1,0:T(8,128)(2,1)}) %all-gather.2.cloned.1.call-update) | async-done | bytes 12582928 | tf_op jit(solution)/shard_map/all_gather | solution.py:88
  134.7 10.5 fusion.57
  145.1 8.6 copy.61
  153.8 21.1 %bitcast_reduce_fusion = (f32[2,256,12]{1,2,0:T(8,128)S(1)}, f32[2,12,2048,256]{3,2,1,0:T(8,128)}) fusion(pred[2,2048]{1,0:T(4,128)(4,1)S(1)} %iota_compare_fusion, bf16[2,2048,12,64]{1,3,2,0:T(8,128)(2,1)} %bitcast.149, bf16[2,256,12,64]{1,0,3,2:T(2,128)(2,1)} %reshape.230), kind=kOutput, calls=%fused_computation.20 | convolution fusion | flops 1648355328 | bytes 57438208 | tf_op jit(solution)/shard_map/trhd,tkhd->trhk/dot_general | solution.py:92
  176.1 8.6 copy.60
  184.8 24.1 %fusion.16 = f32[2,256,12]{1,2,0:T(8,128)S(1)} fusion(f32[2,12,2048,256]{3,2,1,0:T(8,128)} %get-tuple-element.428, f32[2,256,12]{1,2,0:T(8,128)} %broadcast_maximum_fusion, pred[2,2048]{1,0:T(4,128)(4,1)S(1)} %iota_compare_fusion), kind=kLoop, calls=%fused_computation.24 | loop fusion | flops 62908416 | bytes 50384896 | tf_op jit(solution)/shard_map/reduce_sum | solution.py:98
  209.6 20.6 %fusion.59 = (bf16[2,256,12,64]{1,3,2,0:T(8,128)(2,1)S(1)}, f32[2,256,12,64]{1,3,2,0:T(8,128)}) fusion(f32[2,256,12]{1,2,0:T(8,128)S(1)} %fusion.16, bf16[2,2048,12,64]{1,3,2,0:T(8,128)(2,1)S(1)} %bitcast.153, f32[2,12,2048,256]{3,2,1,0:T(8,128)} %get-tuple-element.428, f32[2,256,12]{1,2,0:T(8,128)S(1)} %copy-done.14, pred[2,2048]{1,0:T(4,128)(4,1)S(1)} %iota_compare_fusion), kind=kOutput, calls=%fused_computation.120 | convolution fusion | flops 1674313728 | bytes 59035648 | tf_op jit(solution)/shard_map/trhk,tkhd->trhd/dot_general | solution.py:99
  233.8 18.3 %multiply_convert_fusion = (bf16[512,3072]{1,0:T(8,128)(2,1)S(1)}, f32[512,3072]{1,0:T(8,128)}, f32[512,3072]{1,0:T(8,128)}) fusion(f32[3072]{0:T(1024)S(1)} %copy-done.21, bf16[768,3072]{1,0:T(8,128)(2,1)S(1)} %bitcast.166, f32[512,768]{1,0:T(8,128)S(1)} %get-tuple-element.432, f32[768]{0:T(1024)S(1)} %copy-done.27, f32[768]{0:T(1024)S(1)} %copy-done.20, ...), kind=kOutput, calls=%fused_computation.32 | convolution fusion | flops 2521694208 | bytes 22042624 | tf_op jit(solution)/shard_map/dot_general | solution.py:117
  259.1 9.7 fusion.51
  268.9 5.6 multiply_reduce_fusion
  282.9 2.9 reshape.232
  290.6 430.9 %while.20 = (s32[]{:T(128)}, bf16[2,256,1536]{1,2,0:T(8,128)(2,1)}, f32[2,256,1536]{1,2,0:T(8,128)}, f32[2,256,12,64]{1,3,2,0:T(8,128)}, s32[]{:T(128)}, /*index...) while((s32[]{:T(128)}, bf16[2,256,1536]{1,2,0:T(8,128)(2,1)}, ...), condition=%wide.region_12.13_spmd.clone, body=%wide.region_11.12_spmd.clone.sunk | while | flops 1031799552 | bytes 106442808 | solution.py:192
  306.2 3.9 bitcast_add_fusion.2
  310.1 17.8 %collective-permute-done.1 = bf16[2,256,1536]{1,2,0:T(8,128)(2,1)} collective-permute-done((bf16[2,256,1536]{1,2,0:T(8,128)(2,1)}, bf16[2,256,1536]{1,2,0:T(8,128)(2,1)}, u32[]{:S(2)}, u32[]{:S(2)}) %collective-permute-start.1) | collective-permute-done | bytes 1572896 | tf_op jit(solution)/shard_map/while/body/eval_jaxpr/ppermute | solution.py:16
  327.9 3.3 convert_element_type.315
  331.2 13.6 %collective-permute-done = bf16[2,256,1536]{1,2,0:T(8,128)(2,1)} collective-permute-done((bf16[2,256,1536]{1,2,0:T(8,128)(2,1)}, bf16[2,256,1536]{1,2,0:T(8,128)(2,1)}, u32[]{:S(2)}, u32[]{:S(2)}) %collective-permute-start) | collective-permute-done | bytes 1572896 | tf_op jit(solution)/shard_map/while/body/eval_jaxpr/ppermute | solution.py:16
  359.7 4.4 bitcast_add_fusion.2
  364.1 17.6 %collective-permute-done.1 = bf16[2,256,1536]{1,2,0:T(8,128)(2,1)} collective-permute-done((bf16[2,256,1536]{1,2,0:T(8,128)(2,1)}, bf16[2,256,1536]{1,2,0:T(8,128)(2,1)}, u32[]{:S(2)}, u32[]{:S(2)}) %collective-permute-start.1) | collective-permute-done | bytes 1572896 | tf_op jit(solution)/shard_map/while/body/eval_jaxpr/ppermute | solution.py:16
  381.7 3.3 convert_element_type.315
  385.0 13.6 %collective-permute-done = bf16[2,256,1536]{1,2,0:T(8,128)(2,1)} collective-permute-done((bf16[2,256,1536]{1,2,0:T(8,128)(2,1)}, bf16[2,256,1536]{1,2,0:T(8,128)(2,1)}, u32[]{:S(2)}, u32[]{:S(2)}) %collective-permute-start) | collective-permute-done | bytes 1572896 | tf_op jit(solution)/shard_map/while/body/eval_jaxpr/ppermute | solution.py:16
  405.9 2.9 fusion.124
  413.6 4.4 bitcast_add_fusion.2
  418.0 17.5 %collective-permute-done.1 = bf16[2,256,1536]{1,2,0:T(8,128)(2,1)} collective-permute-done((bf16[2,256,1536]{1,2,0:T(8,128)(2,1)}, bf16[2,256,1536]{1,2,0:T(8,128)(2,1)}, u32[]{:S(2)}, u32[]{:S(2)}) %collective-permute-start.1) | collective-permute-done | bytes 1572896 | tf_op jit(solution)/shard_map/while/body/eval_jaxpr/ppermute | solution.py:16
  435.5 3.3 convert_element_type.315
  438.8 13.6 %collective-permute-done = bf16[2,256,1536]{1,2,0:T(8,128)(2,1)} collective-permute-done((bf16[2,256,1536]{1,2,0:T(8,128)(2,1)}, bf16[2,256,1536]{1,2,0:T(8,128)(2,1)}, u32[]{:S(2)}, u32[]{:S(2)}) %collective-permute-start) | collective-permute-done | bytes 1572896 | tf_op jit(solution)/shard_map/while/body/eval_jaxpr/ppermute | solution.py:16
  459.8 2.9 fusion.124
  467.4 4.4 bitcast_add_fusion.2
  471.8 17.5 %collective-permute-done.1 = bf16[2,256,1536]{1,2,0:T(8,128)(2,1)} collective-permute-done((bf16[2,256,1536]{1,2,0:T(8,128)(2,1)}, bf16[2,256,1536]{1,2,0:T(8,128)(2,1)}, u32[]{:S(2)}, u32[]{:S(2)}) %collective-permute-start.1) | collective-permute-done | bytes 1572896 | tf_op jit(solution)/shard_map/while/body/eval_jaxpr/ppermute | solution.py:16
  489.3 3.3 convert_element_type.315
  492.6 13.6 %collective-permute-done = bf16[2,256,1536]{1,2,0:T(8,128)(2,1)} collective-permute-done((bf16[2,256,1536]{1,2,0:T(8,128)(2,1)}, bf16[2,256,1536]{1,2,0:T(8,128)(2,1)}, u32[]{:S(2)}, u32[]{:S(2)}) %collective-permute-start) | collective-permute-done | bytes 1572896 | tf_op jit(solution)/shard_map/while/body/eval_jaxpr/ppermute | solution.py:16
  513.6 2.9 fusion.124
  521.2 4.4 bitcast_add_fusion.2
  525.6 17.5 %collective-permute-done.1 = bf16[2,256,1536]{1,2,0:T(8,128)(2,1)} collective-permute-done((bf16[2,256,1536]{1,2,0:T(8,128)(2,1)}, bf16[2,256,1536]{1,2,0:T(8,128)(2,1)}, u32[]{:S(2)}, u32[]{:S(2)}) %collective-permute-start.1) | collective-permute-done | bytes 1572896 | tf_op jit(solution)/shard_map/while/body/eval_jaxpr/ppermute | solution.py:16
  543.2 3.3 convert_element_type.315
  546.5 13.6 %collective-permute-done = bf16[2,256,1536]{1,2,0:T(8,128)(2,1)} collective-permute-done((bf16[2,256,1536]{1,2,0:T(8,128)(2,1)}, bf16[2,256,1536]{1,2,0:T(8,128)(2,1)}, u32[]{:S(2)}, u32[]{:S(2)}) %collective-permute-start) | collective-permute-done | bytes 1572896 | tf_op jit(solution)/shard_map/while/body/eval_jaxpr/ppermute | solution.py:16
  567.4 2.9 fusion.124
  575.1 4.4 bitcast_add_fusion.2
  579.5 17.5 %collective-permute-done.1 = bf16[2,256,1536]{1,2,0:T(8,128)(2,1)} collective-permute-done((bf16[2,256,1536]{1,2,0:T(8,128)(2,1)}, bf16[2,256,1536]{1,2,0:T(8,128)(2,1)}, u32[]{:S(2)}, u32[]{:S(2)}) %collective-permute-start.1) | collective-permute-done | bytes 1572896 | tf_op jit(solution)/shard_map/while/body/eval_jaxpr/ppermute | solution.py:16
  597.0 3.3 convert_element_type.315
  600.3 13.6 %collective-permute-done = bf16[2,256,1536]{1,2,0:T(8,128)(2,1)} collective-permute-done((bf16[2,256,1536]{1,2,0:T(8,128)(2,1)}, bf16[2,256,1536]{1,2,0:T(8,128)(2,1)}, u32[]{:S(2)}, u32[]{:S(2)}) %collective-permute-start) | collective-permute-done | bytes 1572896 | tf_op jit(solution)/shard_map/while/body/eval_jaxpr/ppermute | solution.py:16
  621.2 2.9 fusion.124
  628.9 4.4 bitcast_add_fusion.2
  633.3 17.5 %collective-permute-done.1 = bf16[2,256,1536]{1,2,0:T(8,128)(2,1)} collective-permute-done((bf16[2,256,1536]{1,2,0:T(8,128)(2,1)}, bf16[2,256,1536]{1,2,0:T(8,128)(2,1)}, u32[]{:S(2)}, u32[]{:S(2)}) %collective-permute-start.1) | collective-permute-done | bytes 1572896 | tf_op jit(solution)/shard_map/while/body/eval_jaxpr/ppermute | solution.py:16
  650.8 3.3 convert_element_type.315
  654.1 13.6 %collective-permute-done = bf16[2,256,1536]{1,2,0:T(8,128)(2,1)} collective-permute-done((bf16[2,256,1536]{1,2,0:T(8,128)(2,1)}, bf16[2,256,1536]{1,2,0:T(8,128)(2,1)}, u32[]{:S(2)}, u32[]{:S(2)}) %collective-permute-start) | collective-permute-done | bytes 1572896 | tf_op jit(solution)/shard_map/while/body/eval_jaxpr/ppermute | solution.py:16
  675.1 2.9 fusion.124
  682.7 4.4 bitcast_add_fusion.2
  687.1 17.5 %collective-permute-done.1 = bf16[2,256,1536]{1,2,0:T(8,128)(2,1)} collective-permute-done((bf16[2,256,1536]{1,2,0:T(8,128)(2,1)}, bf16[2,256,1536]{1,2,0:T(8,128)(2,1)}, u32[]{:S(2)}, u32[]{:S(2)}) %collective-permute-start.1) | collective-permute-done | bytes 1572896 | tf_op jit(solution)/shard_map/while/body/eval_jaxpr/ppermute | solution.py:16
  704.7 3.3 convert_element_type.315
  707.9 13.6 %collective-permute-done = bf16[2,256,1536]{1,2,0:T(8,128)(2,1)} collective-permute-done((bf16[2,256,1536]{1,2,0:T(8,128)(2,1)}, bf16[2,256,1536]{1,2,0:T(8,128)(2,1)}, u32[]{:S(2)}, u32[]{:S(2)}) %collective-permute-start) | collective-permute-done | bytes 1572896 | tf_op jit(solution)/shard_map/while/body/eval_jaxpr/ppermute | solution.py:16
  727.2 3.1 copy.72
  730.3 5.6 fusion.29
  735.9 5.8 copy.79
  741.8 6.9 convolution_convert_fusion
  749.3 7.4 convolution_convert_fusion.1
  757.3 29.9 %reduce-scatter.25.cloned.1.call-done = bf16[192,2304]{1,0:T(8,128)(2,1)} async-done(((bf16[768,2304]{1,0:T(8,128)(2,1)}), bf16[192,2304]{1,0:T(8,128)(2,1)}) %reduce-scatter.25.cloned.1.call-update) | async-done | bytes 884752
  787.3 59.9 %reduce-scatter.21.cloned.1.call-done = bf16[768,768]{1,0:T(8,128)(2,1)} async-done(((bf16[3072,768]{1,0:T(8,128)(2,1)}), bf16[768,768]{1,0:T(8,128)(2,1)}) %reduce-scatter.21.cloned.1.call-update) | async-done | bytes 1179664 | tf_op jit(solution)/shard_map/reduce_scatter | solution.py:244
  847.3 59.9 %reduce-scatter.17.cloned.1.call-done = bf16[192,3072]{1,0:T(8,128)(2,1)} async-done(((bf16[768,3072]{1,0:T(8,128)(2,1)}), bf16[192,3072]{1,0:T(8,128)(2,1)}) %reduce-scatter.17.cloned.1.call-update) | async-done | bytes 1179664 | tf_op jit(solution)/shard_map/reduce_scatter | solution.py:238
  916.9 16.5 %all-reduce.17 = (bf16[1536]{0:T(1024)(128)(2,1)}, bf16[768]{0:T(1024)(128)(2,1)}, bf16[768]{0:T(1024)(128)(2,1)}, bf16[768]{0:T(1024)(128)(2,1)}, bf16[3072]{0:...) all-reduce(bf16[1536]{0:T(1024)(128)(2,1)S(1)} %pad_maximum_fusion., ...), channel_id=4, replica_groups=mesh['tab'=4,'blk'=8] {'tab'}, use_global_device_ids=true, to_apply=%region_16.17.clone | all-reduce | flops 9216 | bytes 36864
  942.5 14.7 %all-reduce.16 = (bf16[384]{0:T(512)(128)(2,1)}, bf16[192]{0:T(256)(128)(2,1)S(1)}, bf16[192]{0:T(256)(128)(2,1)}, bf16[192]{0:T(256)(128)(2,1)}, bf16[768]{0:T(...) all-reduce(bf16[384]{0:T(512)(128)(2,1)S(1)} %dynamic-slice.1, ...), channel_id=5, replica_groups=mesh['tab'=4,'blk'=8] {'blk'}, use_global_device_ids=true, to_apply=%region_17.18.clone | all-reduce | flops 2304 | bytes 9216
  963.5 5.1 add_convert_fusion.1
  976.3 29.5 %reduce-scatter.23.cloned.1.call-done = bf16[96,768]{1,0:T(8,128)(2,1)} async-done(((bf16[768,768]{1,0:T(8,128)(2,1)}), bf16[96,768]{1,0:T(8,128)(2,1)}) %reduce-scatter.23.cloned.1.call-update) | async-done | bytes 147472 | tf_op jit(solution)/shard_map/reduce_scatter | solution.py:295
  1007.4 31.5 %reduce-scatter.19.cloned.1.call-done = bf16[24,3072]{1,0:T(8,128)(2,1)} async-done(((bf16[192,3072]{1,0:T(8,128)(2,1)}), bf16[24,3072]{1,0:T(8,128)(2,1)}) %reduce-scatter.19.cloned.1.call-update) | async-done | bytes 147472 | tf_op jit(solution)/shard_map/reduce_scatter | solution.py:289
  (352 shorter events, 190.8 us)
Async XLA Ops:
  7.2 127.5 %all-gather.2.cloned.1.call-start = ((), (), s32[]{:S(2)}) async-start(), calls=%async_computation.8 | async-start | bytes 14155776 | tf_op jit(solution)/shard_map/all_gather | solution.py:88
  15.1 741.7 %reduce-scatter.13.cloned.1.call-start = ((), (), s32[]{:S(2)}) async-start(), calls=%async_computation.9 | async-start | bytes 1474560 | tf_op jit(solution)/shard_map/reduce_scatter | solution.py:226
  17.2 7.8 copy-start.30
  17.2 11.0 %copy-start.26 = (bf16[3072]{0:T(1024)(128)(2,1)S(1)}, bf16[3072]{0:T(1024)(128)(2,1)}, u32[]{:S(2)}) copy-start(bf16[3072]{0:T(1024)(128)(2,1)} %param.26) | copy-start | bytes 18436
  17.2 17.0 %copy-start.17 = (s32[2]{0:T(128)S(1)}, s32[2]{0:T(128)}, u32[]{:S(2)}) copy-start(s32[2]{0:T(128)} %param.18) | copy-start | bytes 28
  184.8 24.2 %copy-start.13 = (f32[2,256,12]{1,2,0:T(8,128)S(1)}, f32[2,256,12]{1,2,0:T(8,128)}, u32[]{:S(2)}) copy-start(f32[2,256,12]{1,2,0:T(8,128)} %copy-done.12) | copy-start | bytes 73732
  184.8 24.8 %copy-start.6 = (bf16[2,2048,768]{1,2,0:T(8,128)(2,1)S(1)}, bf16[2,2048,768]{1,2,0:T(8,128)(2,1)}, u32[]{:S(2)}) copy-start(bf16[2,2048,768]{1,2,0:T(8,128)(2,1)} %copy.60) | copy-start | bytes 18874372
  184.8 24.8 %copy-start.14 = (f32[2,256,12]{1,2,0:T(8,128)S(1)}, f32[2,256,12]{1,2,0:T(8,128)}, u32[]{:S(2)}) copy-start(f32[2,256,12]{1,2,0:T(8,128)} %broadcast_maximum_fusion) | copy-start | bytes 73732
  184.8 49.0 %slice-start.2 = ((s8[4718592]{0:T(1024)(128)(4,1)}), s8[4194304]{0:T(1024)(128)(4,1)S(1)}, s32[]{:S(2)}) async-start(s8[4718592]{0:T(1024)(128)(4,1)} %bitcast.165), calls=%async_computation.19 | async-start | bytes 8388608
  209.6 21.7 %copy-start.29 = (f32[768]{0:T(1024)S(1)}, f32[768]{0:T(1024)}, u32[]{:S(2)}) copy-start(f32[768]{0:T(1024)} %convert_element_type.219) | copy-start | bytes 9220
  209.6 21.7 %copy-start.31 = (bf16[768,768]{1,0:T(8,128)(2,1)S(1)}, bf16[768,768]{1,0:T(8,128)(2,1)}, u32[]{:S(2)}) copy-start(bf16[768,768]{1,0:T(8,128)(2,1)} %param.21) | copy-start | bytes 3538948
  209.6 24.2 %slice-start.3 = ((s8[4718592]{0:T(1024)(128)(4,1)}), s8[524288]{0:T(1024)(128)(4,1)S(1)}, s32[]{:S(2)}) async-start(s8[4718592]{0:T(1024)(128)(4,1)} %bitcast.165), calls=%async_computation.20 | async-start | bytes 1048576
  231.3 20.9 %slice-start = ((s8[4718592]{0:T(1024)(128)(4,1)}), s8[524288]{0:T(1024)(128)(4,1)S(1)}, s32[]{:S(2)}) async-start(s8[4718592]{0:T(1024)(128)(4,1)} %bitcast.163), calls=%async_computation.17 | async-start | bytes 1048576
  233.4 41.1 %copy-start.8 = (f32[512,768]{1,0:T(8,128)}, f32[512,768]{1,0:T(8,128)S(1)}, u32[]{:S(2)}) copy-start(f32[512,768]{1,0:T(8,128)S(1)} %get-tuple-element.432) | copy-start | bytes 4718596
  233.8 40.7 %copy-start.22 = (f32[512]{0:T(512)}, f32[512]{0:T(512)S(1)}, u32[]{:S(2)}) copy-start(f32[512]{0:T(512)S(1)} %fusion.38) | copy-start | bytes 6148
  233.8 18.4 %copy-start.28 = (f32[768]{0:T(1024)S(1)}, f32[768]{0:T(1024)}, u32[]{:S(2)}) copy-start(f32[768]{0:T(1024)} %convert_element_type.225) | copy-start | bytes 9220
  233.8 18.4 %slice-start.1 = ((s8[4718592]{0:T(1024)(128)(4,1)}), s8[4194304]{0:T(1024)(128)(4,1)S(1)}, s32[]{:S(2)}) async-start(s8[4718592]{0:T(1024)(128)(4,1)} %bitcast.163), calls=%async_computation.18 | async-start | bytes 8388608
  252.2 3.2 copy-start.5
  259.1 9.8 copy-start.11
  282.9 7.7 copy-start.18
  290.5 496.7 %reduce-scatter.25.cloned.1.call-start = ((), (), s32[]{:S(2)}) async-start(), calls=%async_computation.15 | async-start | bytes 4423680
  290.8 4.3 copy-start.4
  301.2 4.7 copy-start.1
  301.2 3.1 copy-start.3
  305.9 22.0 %collective-permute-start.1 = (bf16[2,256,1536]{1,2,0:T(8,128)(2,1)}, bf16[2,256,1536]{1,2,0:T(8,128)(2,1)}, u32[]{:S(2)}, u32[]{:S(2)}) collective-permute-start(bf16[2,256,1536]{1,2,0:T(8,128)(2,1)} %fusion.126), channel_id=1, source_target_pairs={{7,0},{0,1},{1,2},{2,3},{3,4},{4,5},{5,6},{6,7},{15,8},{8,9},{9,10... | collective-permute-start | bytes 4718600 | tf_op jit(solution)/shard_map/while/body/eval_jaxpr/ppermute | solution.py:16
  306.2 38.6 %collective-permute-start = (bf16[2,256,1536]{1,2,0:T(8,128)(2,1)}, bf16[2,256,1536]{1,2,0:T(8,128)(2,1)}, u32[]{:S(2)}, u32[]{:S(2)}) collective-permute-start(bf16[2,256,1536]{1,2,0:T(8,128)(2,1)} %copy.95), channel_id=1, source_target_pairs={{7,0},{0,1},{1,2},{2,3},{3,4},{4,5},{5,6},{6,7},{15,8},{8,9},{9,10... | collective-permute-start | bytes 4718600 | tf_op jit(solution)/shard_map/while/body/eval_jaxpr/ppermute | solution.py:16
  344.7 4.3 copy-start.4
  355.0 4.7 copy-start.1
  355.0 3.0 copy-start.3
  359.7 22.0 %collective-permute-start.1 = (bf16[2,256,1536]{1,2,0:T(8,128)(2,1)}, bf16[2,256,1536]{1,2,0:T(8,128)(2,1)}, u32[]{:S(2)}, u32[]{:S(2)}) collective-permute-start(bf16[2,256,1536]{1,2,0:T(8,128)(2,1)} %fusion.126), channel_id=1, source_target_pairs={{7,0},{0,1},{1,2},{2,3},{3,4},{4,5},{5,6},{6,7},{15,8},{8,9},{9,10... | collective-permute-start | bytes 4718600 | tf_op jit(solution)/shard_map/while/body/eval_jaxpr/ppermute | solution.py:16
  359.7 38.8 %collective-permute-start = (bf16[2,256,1536]{1,2,0:T(8,128)(2,1)}, bf16[2,256,1536]{1,2,0:T(8,128)(2,1)}, u32[]{:S(2)}, u32[]{:S(2)}) collective-permute-start(bf16[2,256,1536]{1,2,0:T(8,128)(2,1)} %copy.95), channel_id=1, source_target_pairs={{7,0},{0,1},{1,2},{2,3},{3,4},{4,5},{5,6},{6,7},{15,8},{8,9},{9,10... | collective-permute-start | bytes 4718600 | tf_op jit(solution)/shard_map/while/body/eval_jaxpr/ppermute | solution.py:16
  398.5 4.3 copy-start.4
  408.9 4.7 copy-start.1
  413.6 22.0 %collective-permute-start.1 = (bf16[2,256,1536]{1,2,0:T(8,128)(2,1)}, bf16[2,256,1536]{1,2,0:T(8,128)(2,1)}, u32[]{:S(2)}, u32[]{:S(2)}) collective-permute-start(bf16[2,256,1536]{1,2,0:T(8,128)(2,1)} %fusion.126), channel_id=1, source_target_pairs={{7,0},{0,1},{1,2},{2,3},{3,4},{4,5},{5,6},{6,7},{15,8},{8,9},{9,10... | collective-permute-start | bytes 4718600 | tf_op jit(solution)/shard_map/while/body/eval_jaxpr/ppermute | solution.py:16
  413.6 38.8 %collective-permute-start = (bf16[2,256,1536]{1,2,0:T(8,128)(2,1)}, bf16[2,256,1536]{1,2,0:T(8,128)(2,1)}, u32[]{:S(2)}, u32[]{:S(2)}) collective-permute-start(bf16[2,256,1536]{1,2,0:T(8,128)(2,1)} %copy.95), channel_id=1, source_target_pairs={{7,0},{0,1},{1,2},{2,3},{3,4},{4,5},{5,6},{6,7},{15,8},{8,9},{9,10... | collective-permute-start | bytes 4718600 | tf_op jit(solution)/shard_map/while/body/eval_jaxpr/ppermute | solution.py:16
  452.4 4.3 copy-start.4
  462.7 4.7 copy-start.1
  467.4 22.0 %collective-permute-start.1 = (bf16[2,256,1536]{1,2,0:T(8,128)(2,1)}, bf16[2,256,1536]{1,2,0:T(8,128)(2,1)}, u32[]{:S(2)}, u32[]{:S(2)}) collective-permute-start(bf16[2,256,1536]{1,2,0:T(8,128)(2,1)} %fusion.126), channel_id=1, source_target_pairs={{7,0},{0,1},{1,2},{2,3},{3,4},{4,5},{5,6},{6,7},{15,8},{8,9},{9,10... | collective-permute-start | bytes 4718600 | tf_op jit(solution)/shard_map/while/body/eval_jaxpr/ppermute | solution.py:16
  467.4 38.8 %collective-permute-start = (bf16[2,256,1536]{1,2,0:T(8,128)(2,1)}, bf16[2,256,1536]{1,2,0:T(8,128)(2,1)}, u32[]{:S(2)}, u32[]{:S(2)}) collective-permute-start(bf16[2,256,1536]{1,2,0:T(8,128)(2,1)} %copy.95), channel_id=1, source_target_pairs={{7,0},{0,1},{1,2},{2,3},{3,4},{4,5},{5,6},{6,7},{15,8},{8,9},{9,10... | collective-permute-start | bytes 4718600 | tf_op jit(solution)/shard_map/while/body/eval_jaxpr/ppermute | solution.py:16
  506.2 4.3 copy-start.4
  516.5 4.7 copy-start.1
  521.2 22.0 %collective-permute-start.1 = (bf16[2,256,1536]{1,2,0:T(8,128)(2,1)}, bf16[2,256,1536]{1,2,0:T(8,128)(2,1)}, u32[]{:S(2)}, u32[]{:S(2)}) collective-permute-start(bf16[2,256,1536]{1,2,0:T(8,128)(2,1)} %fusion.126), channel_id=1, source_target_pairs={{7,0},{0,1},{1,2},{2,3},{3,4},{4,5},{5,6},{6,7},{15,8},{8,9},{9,10... | collective-permute-start | bytes 4718600 | tf_op jit(solution)/shard_map/while/body/eval_jaxpr/ppermute | solution.py:16
  521.2 38.8 %collective-permute-start = (bf16[2,256,1536]{1,2,0:T(8,128)(2,1)}, bf16[2,256,1536]{1,2,0:T(8,128)(2,1)}, u32[]{:S(2)}, u32[]{:S(2)}) collective-permute-start(bf16[2,256,1536]{1,2,0:T(8,128)(2,1)} %copy.95), channel_id=1, source_target_pairs={{7,0},{0,1},{1,2},{2,3},{3,4},{4,5},{5,6},{6,7},{15,8},{8,9},{9,10... | collective-permute-start | bytes 4718600 | tf_op jit(solution)/shard_map/while/body/eval_jaxpr/ppermute | solution.py:16
  560.0 4.3 copy-start.4
  570.3 4.7 copy-start.1
  575.0 22.0 %collective-permute-start.1 = (bf16[2,256,1536]{1,2,0:T(8,128)(2,1)}, bf16[2,256,1536]{1,2,0:T(8,128)(2,1)}, u32[]{:S(2)}, u32[]{:S(2)}) collective-permute-start(bf16[2,256,1536]{1,2,0:T(8,128)(2,1)} %fusion.126), channel_id=1, source_target_pairs={{7,0},{0,1},{1,2},{2,3},{3,4},{4,5},{5,6},{6,7},{15,8},{8,9},{9,10... | collective-permute-start | bytes 4718600 | tf_op jit(solution)/shard_map/while/body/eval_jaxpr/ppermute | solution.py:16
  575.0 38.8 %collective-permute-start = (bf16[2,256,1536]{1,2,0:T(8,128)(2,1)}, bf16[2,256,1536]{1,2,0:T(8,128)(2,1)}, u32[]{:S(2)}, u32[]{:S(2)}) collective-permute-start(bf16[2,256,1536]{1,2,0:T(8,128)(2,1)} %copy.95), channel_id=1, source_target_pairs={{7,0},{0,1},{1,2},{2,3},{3,4},{4,5},{5,6},{6,7},{15,8},{8,9},{9,10... | collective-permute-start | bytes 4718600 | tf_op jit(solution)/shard_map/while/body/eval_jaxpr/ppermute | solution.py:16
  613.9 4.3 copy-start.4
  624.2 4.7 copy-start.1
  628.9 22.0 %collective-permute-start.1 = (bf16[2,256,1536]{1,2,0:T(8,128)(2,1)}, bf16[2,256,1536]{1,2,0:T(8,128)(2,1)}, u32[]{:S(2)}, u32[]{:S(2)}) collective-permute-start(bf16[2,256,1536]{1,2,0:T(8,128)(2,1)} %fusion.126), channel_id=1, source_target_pairs={{7,0},{0,1},{1,2},{2,3},{3,4},{4,5},{5,6},{6,7},{15,8},{8,9},{9,10... | collective-permute-start | bytes 4718600 | tf_op jit(solution)/shard_map/while/body/eval_jaxpr/ppermute | solution.py:16
  628.9 38.8 %collective-permute-start = (bf16[2,256,1536]{1,2,0:T(8,128)(2,1)}, bf16[2,256,1536]{1,2,0:T(8,128)(2,1)}, u32[]{:S(2)}, u32[]{:S(2)}) collective-permute-start(bf16[2,256,1536]{1,2,0:T(8,128)(2,1)} %copy.95), channel_id=1, source_target_pairs={{7,0},{0,1},{1,2},{2,3},{3,4},{4,5},{5,6},{6,7},{15,8},{8,9},{9,10... | collective-permute-start | bytes 4718600 | tf_op jit(solution)/shard_map/while/body/eval_jaxpr/ppermute | solution.py:16
  667.7 4.3 copy-start.4
  678.0 4.7 copy-start.1
  682.7 22.0 %collective-permute-start.1 = (bf16[2,256,1536]{1,2,0:T(8,128)(2,1)}, bf16[2,256,1536]{1,2,0:T(8,128)(2,1)}, u32[]{:S(2)}, u32[]{:S(2)}) collective-permute-start(bf16[2,256,1536]{1,2,0:T(8,128)(2,1)} %fusion.126), channel_id=1, source_target_pairs={{7,0},{0,1},{1,2},{2,3},{3,4},{4,5},{5,6},{6,7},{15,8},{8,9},{9,10... | collective-permute-start | bytes 4718600 | tf_op jit(solution)/shard_map/while/body/eval_jaxpr/ppermute | solution.py:16
  682.7 38.8 %collective-permute-start = (bf16[2,256,1536]{1,2,0:T(8,128)(2,1)}, bf16[2,256,1536]{1,2,0:T(8,128)(2,1)}, u32[]{:S(2)}, u32[]{:S(2)}) collective-permute-start(bf16[2,256,1536]{1,2,0:T(8,128)(2,1)} %copy.95), channel_id=1, source_target_pairs={{7,0},{0,1},{1,2},{2,3},{3,4},{4,5},{5,6},{6,7},{15,8},{8,9},{9,10... | collective-permute-start | bytes 4718600 | tf_op jit(solution)/shard_map/while/body/eval_jaxpr/ppermute | solution.py:16
  741.7 105.5 %reduce-scatter.21.cloned.1.call-start = ((), (), s32[]{:S(2)}) async-start(), calls=%async_computation.13 | async-start | bytes 5898240 | tf_op jit(solution)/shard_map/reduce_scatter | solution.py:244
  748.7 158.6 %reduce-scatter.17.cloned.1.call-start = ((), (), s32[]{:S(2)}) async-start(), calls=%async_computation.11 | async-start | bytes 5898240 | tf_op jit(solution)/shard_map/reduce_scatter | solution.py:238
  756.7 155.7 %copy-start.32 = (u32[32]{0:T(128)S(1)}, u32[32]{0:T(128)}, u32[]{:S(2)}) copy-start(u32[32]{0:T(128)} %constant.186) | copy-start | bytes 388
  756.7 160.2 %copy-start.24 = (bf16[768]{0:T(1024)(128)(2,1)S(1)}, bf16[768]{0:T(1024)(128)(2,1)}, u32[]{:S(2)}) copy-start(bf16[768]{0:T(1024)(128)(2,1)} %get-tuple-element.367) | copy-start | bytes 4612
  756.7 160.2 %copy-start.25 = (bf16[768]{0:T(1024)(128)(2,1)S(1)}, bf16[768]{0:T(1024)(128)(2,1)}, u32[]{:S(2)}) copy-start(bf16[768]{0:T(1024)(128)(2,1)} %get-tuple-element.406) | copy-start | bytes 4612
  756.7 211.8 %reduce-scatter.15.cloned.1.call-start = ((), (), s32[]{:S(2)}) async-start(), calls=%async_computation.10 | async-start | bytes 331776 | tf_op jit(solution)/shard_map/reduce_scatter | solution.py:277
  757.3 215.1 %reduce-scatter.27.cloned.1.call-start = ((), (), s32[]{:S(2)}) async-start(), calls=%async_computation.16 | async-start | bytes 995328
  787.3 218.5 %reduce-scatter.23.cloned.1.call-start = ((), (), s32[]{:S(2)}) async-start(), calls=%async_computation.14 | async-start | bytes 1327104 | tf_op jit(solution)/shard_map/reduce_scatter | solution.py:295
  847.3 191.6 %reduce-scatter.19.cloned.1.call-start = ((), (), s32[]{:S(2)}) async-start(), calls=%async_computation.12 | async-start | bytes 1327104 | tf_op jit(solution)/shard_map/reduce_scatter | solution.py:289
  (48 other events, 80.5 us)
Sparse Core Ops, SparseCore 0:
  15.2 119.4 all-gather.1
  290.7 26.7 reduce-scatter.12
  741.8 45.3 reduce-scatter.24
  790.1 57.0 reduce-scatter.20
  850.1 57.0 reduce-scatter.16
  909.3 30.5 reduce-scatter.14
  942.3 30.0 reduce-scatter.26
  974.6 31.1 reduce-scatter.22
  1008.1 30.7 reduce-scatter.18
where the time goes:
time: 1060 us; the launch traced here: 1050 us
  waiting for transfers between devices  563 us (53%)
  matrix products  200 us (19%)
  local copies, waits for them, and re-layouts  134 us (13%)
  other arithmetic  98.2 us (9%)
  blocking collectives  31.2 us (3%)
  between operations  18.6 us (2%)
    ppermute x16, waiting for transfers between devices, from_behind(): return lax.ppermute(block, axis, route)  249 us
    all_gather x1, waiting for transfers between devices, shards(): pair_block = lax.all_gather(key_values, 'blk', axis=1, tiled=True)  100 us
    reduce_scatter x1, waiting for transfers between devices, shards(): lax.psum_scatter(wgrad_down.astype(jnp.bfloat16), 'tab', scatter_dimensio...  59.9 us
    reduce_scatter x1, waiting for transfers between devices, shards(): lax.psum_scatter(wgrad_up.astype(jnp.bfloat16), 'tab', scatter_dimension=...  59.9 us
    while x120, local copies, waits for them, and re-layouts  40.2 us
    dot_general x8, matrix products, cycle_turn_step(): jnp.einsum('trhk,tkhd->trhd', grad_raw, keys_part, preferred_element_type...  34.7 us
    unnamed x11, waiting for transfers between devices  33 us
    reduce_scatter x1, waiting for transfers between devices, shards(): lax.psum_scatter(wgrad_up.astype(jnp.bfloat16), 'blk', scatter_dimension=...  31.5 us
  transfers between devices with their start and end apart: 25, of which 23 were waited for; matrix products, arithmetic and copies ran while one was open for 24% of the time, Pallas kernels for 0%

commit v1 on v0

--- a/solution.py
+++ b/solution.py
@@ -1,6 +1,11 @@
+import functools
+import math
+
 import jax
 import jax.numpy as jnp
 from jax import lax
+from jax.experimental import pallas as pl
+from jax.experimental.pallas import tpu as pltpu
 from jax.sharding import PartitionSpec as P
 
 HD = 64
@@ -39,7 +44,7 @@
     )
 
 
-def shards(
+def shards_ring(
     tokens,
     lengths,
     qkv_weight,
@@ -323,6 +328,661 @@
     )
 
 
+GROUPS = 4
+LANES = 128
+LOG2E = math.log2(math.e)
+MESH = pl.DeviceIdType.MESH
+CHUNKS = 2
+
+
+def times_t(left, right):
+    return lax.dot_general(
+        left, right, (((1,), (1,)), ((), ())), preferred_element_type=jnp.float32
+    )
+
+
+def place():
+    tab, blk = lax.axis_index("tab"), lax.axis_index("blk")
+    return tab, blk, blk // 2, blk % 2
+
+
+def meet(tab, blk):
+    barrier = pltpu.get_barrier_semaphore()
+
+    @pl.loop(1, 8)
+    def _(step):
+        pl.semaphore_signal(
+            barrier, inc=1, device_id=(tab, lax.rem(blk + step, 8)), device_id_type=MESH
+        )
+
+    pl.semaphore_wait(barrier, 7)
+
+
+def attend_kernel(
+    heads,
+    tok_ref,
+    len_ref,
+    w_ref,
+    bias_ref,
+    ctx_ref,
+    full_ref,
+    qkv_ref,
+    ot_ref,
+    lse_ref,
+    tokv,
+    qkvv,
+    vtv,
+    otv,
+    lsev,
+    csend,
+    send_a,
+    send_b,
+    send_c,
+    send_d,
+    send_e,
+    recv,
+    csend_sem,
+    crecv_sem,
+    local_sem,
+):
+    tab, blk, chip, core = place()
+    half = chip // 2
+    rows = tok_ref.shape[1]
+    piece = rows // CHUNKS
+    is_near = jnp.logical_or(chip == 1, chip == 2)
+    mate = chip + 1 - 2 * lax.rem(chip, 2)
+    other_near = 2 - half
+    other_far = 3 - 3 * half
+    own_far = 3 * half
+    scale = LOG2E / math.sqrt(HD)
+
+    def remote(src, dst, send_sem, recv_sem, to_chip, to_core):
+        return pltpu.make_async_remote_copy(
+            src_ref=src,
+            dst_ref=dst,
+            send_sem=send_sem,
+            recv_sem=recv_sem,
+            device_id=(tab, 2 * to_chip + to_core),
+            device_id_type=MESH,
+        )
+
+    def own_copies(part):
+        cut = pl.ds(part * piece, piece)
+        here, there = tok_ref.at[half, cut], tok_ref.at[1 - half, cut]
+        dst, done = tokv.at[blk, cut], recv.at[blk, part]
+        return (
+            remote(here, dst, send_a.at[part], done, mate, core),
+            remote(there, dst, send_c.at[part], done, other_near, core),
+            remote(here, dst, send_b.at[part], done, chip, 1 - core),
+        )
+
+    def onward(slot, part, src_chip):
+        cut = pl.ds(part * piece, piece)
+        which = 2 * src_chip + core
+        ref, done = tokv.at[which, cut], recv.at[which, part]
+        return (
+            remote(ref, ref, send_d.at[slot, part], done, own_far, core),
+            remote(ref, ref, send_e.at[slot, part], done, chip, 1 - core),
+        )
+
+    def arrived(which, part):
+        ref = tokv.at[which, pl.ds(part * piece, piece)]
+        pltpu.make_async_copy(ref, ref, recv.at[which, part]).wait()
+
+    meet(tab, blk)
+    for part in range(CHUNKS):
+        for copy in own_copies(part):
+            copy.start()
+    tokv[blk] = tok_ref[half]
+
+    length = len_ref[half]
+    lane = lax.broadcasted_iota(jnp.int32, (rows, LANES), 1)
+    row = lax.broadcasted_iota(jnp.int32, (rows, LANES), 0)
+
+    def project(which):
+        first = pl.multiple_of(which * rows, rows)
+        y = (
+            jnp.dot(tokv[which], w_ref[...], preferred_element_type=jnp.float32)
+            + bias_ref[...]
+        )
+        pad = jnp.where((lane == HD) & (row + first >= length), NEGATIVE, 0.0)
+        for head in range(heads):
+            q, k, v = (
+                y[:, (part * heads + head) * LANES :][:, :LANES] for part in range(3)
+            )
+            qkvv[head, pl.ds(first, rows)] = q.astype(jnp.bfloat16)
+            qkvv[heads + head, pl.ds(first, rows)] = (k + pad).astype(jnp.bfloat16)
+            qkvv[2 * heads + head, pl.ds(first, rows)] = v.astype(jnp.bfloat16)
+            vtv[head, :, pl.ds(first, rows)] = v.T.astype(jnp.bfloat16)
+
+    project(blk)
+    for part in range(CHUNKS):
+        arrived(2 * mate + core, part)
+        onward(0, part, mate)[1].start()
+    project(2 * mate + core)
+    for part in range(CHUNKS):
+        arrived(2 * chip + 1 - core, part)
+    project(2 * chip + 1 - core)
+    for part in range(CHUNKS):
+        arrived(2 * mate + 1 - core, part)
+    project(2 * mate + 1 - core)
+    for part in range(CHUNKS):
+        for slot, src_chip in ((1, other_near), (2, other_far)):
+            arrived(2 * src_chip + core, part)
+            to_far, to_core = onward(slot, part, src_chip)
+            pl.when(is_near)(to_far.start)
+            to_core.start()
+    for src_chip in (other_near, other_far):
+        project(2 * src_chip + core)
+        for part in range(CHUNKS):
+            arrived(2 * src_chip + 1 - core, part)
+        project(2 * src_chip + 1 - core)
+
+    keep = (
+        pltpu.make_async_copy(tokv, full_ref, local_sem.at[0]),
+        pltpu.make_async_copy(qkvv, qkv_ref, local_sem.at[1]),
+    )
+    for copy in keep:
+        copy.start()
+
+    group = 2 * lax.rem(chip, 2) + core
+
+    def context_copy(which):
+        return remote(
+            csend.at[which],
+            ctx_ref.at[half, group],
+            csend_sem.at[which],
+            crecv_sem.at[blk],
+            which // 2,
+            lax.rem(which, 2),
+        )
+
+    own_context = pltpu.make_async_copy(
+        csend.at[blk], ctx_ref.at[half, group], local_sem.at[2]
+    )
+
+    @pl.loop(0, 8)
+    def _(step):
+        which = lax.rem(blk + 1 + step, 8)
+        first = pl.multiple_of(which * rows, rows)
+        for head in range(heads):
+            q = qkvv[head, pl.ds(first, rows)]
+            st = times_t(qkvv[heads + head], q)
+            peak = jnp.max(st, axis=0, keepdims=True)
+            pt = jnp.exp2((st - peak) * scale).astype(jnp.bfloat16)
+            ot = jnp.dot(vtv[head], pt, preferred_element_type=jnp.float32)
+            total = ot[HD : HD + 1]
+            otv[which, head * HD : (head + 1) * HD] = ot[:HD] / total
+            lsev[which, head : head + 1] = peak * scale + jnp.log(total) * LOG2E
+        csend[which] = otv[which].T.astype(jnp.bfloat16)
+
+        @pl.when(step < 7)
+        def _():
+            context_copy(which).start()
+
+        @pl.when(step == 7)
+        def _():
+            own_context.start()
+
+    more = (
+        pltpu.make_async_copy(otv, ot_ref, local_sem.at[3]),
+        pltpu.make_async_copy(lsev, lse_ref, local_sem.at[4]),
+    )
+    for copy in more:
+        copy.start()
+    for part in range(CHUNKS):
+        for copy in own_copies(part):
+            copy.wait_send()
+        onward(0, part, mate)[1].wait_send()
+        for slot, src_chip in ((1, other_near), (2, other_far)):
+            to_far, to_core = onward(slot, part, src_chip)
+            pl.when(is_near)(to_far.wait_send)
+            to_core.wait_send()
+
+    @pl.loop(0, 7)
+    def _(step):
+        which = lax.rem(blk + 1 + step, 8)
+        context_copy(which).wait_send()
+        pltpu.make_async_copy(
+            ctx_ref.at[which // 4, lax.rem(which, 4)],
+            ctx_ref.at[which // 4, lax.rem(which, 4)],
+            crecv_sem.at[which],
+        ).wait()
+
+    own_context.wait()
+    for copy in keep + more:
+        copy.wait()
+
+
+def attend(tokens, lengths, own_weight, own_bias, heads):
+    tables, rows, width = tokens.shape
+    blocks = 8
+    total = blocks * rows
+    any_space = pl.BlockSpec(memory_space=pl.ANY)
+    vmem = pl.BlockSpec(memory_space=pltpu.VMEM)
+    bf16, f32 = jnp.bfloat16, jnp.float32
+    dma = pltpu.SemaphoreType.DMA
+    return pl.pallas_call(
+        functools.partial(attend_kernel, heads),
+        name="attend",
+        out_shape=(
+            jax.ShapeDtypeStruct((tables, GROUPS, rows, heads * HD), bf16),
+            jax.ShapeDtypeStruct((blocks, rows, width), bf16),
+            jax.ShapeDtypeStruct((3 * heads, total, LANES), bf16),
+            jax.ShapeDtypeStruct((blocks, heads * HD, rows), f32),
+            jax.ShapeDtypeStruct((blocks, 8, rows), f32),
+        ),
+        in_specs=[vmem, pl.BlockSpec(memory_space=pltpu.SMEM), vmem, vmem],
+        out_specs=(any_space,) * 5,
+        scratch_shapes=[
+            pltpu.VMEM((blocks, rows, width), bf16),
+            pltpu.VMEM((3 * heads, total, LANES), bf16),
+            pltpu.VMEM((heads, LANES, total), bf16),
+            pltpu.VMEM((blocks, heads * HD, rows), f32),
+            pltpu.VMEM((blocks, 8, rows), f32),
+            pltpu.VMEM((blocks, rows, heads * HD), bf16),
+            dma((CHUNKS,)),
+            dma((CHUNKS,)),
+            dma((CHUNKS,)),
+            dma((3, CHUNKS)),
+            dma((3, CHUNKS)),
+            dma((blocks, CHUNKS)),
+            dma((blocks,)),
+            dma((blocks,)),
+            dma((5,)),
+        ],
+        compiler_params=pltpu.CompilerParams(
+            collective_id=1, has_side_effects=True, vmem_limit_bytes=56 << 20
+        ),
+    )(tokens, lengths, own_weight, own_bias)
+
+
+def attend_back_kernel(
+    heads,
+    dctx_ref,
+    qkv_ref,
+    ot_ref,
+    lse_ref,
+    full_ref,
+    w_ref,
+    pre_ref,
+    tgrad_ref,
+    wgrad_ref,
+    sums_ref,
+    dov,
+    qkvv,
+    otv,
+    lsev,
+    tokv,
+    wv,
+    prev,
+    ktv,
+    dqv,
+    dkv,
+    dvv,
+    dqkv,
+    arrive,
+    dsend_sem,
+    drecv_sem,
+    gsend_sem,
+    grecv_sem,
+    local_sem,
+    own_sem,
+):
+    tab, blk, chip, core = place()
+    half = chip // 2
+    group = 2 * lax.rem(chip, 2) + core
+    blocks, rows = dov.shape[0], dov.shape[1]
+    scale = LOG2E / math.sqrt(HD)
+
+    loads = [
+        pltpu.make_async_copy(src, dst, local_sem.at[at])
+        for at, (src, dst) in enumerate(
+            (
+                (qkv_ref, qkvv),
+                (ot_ref, otv),
+                (lse_ref, lsev),
+                (dctx_ref.at[half, group], dov.at[blk]),
+                (full_ref, tokv),
+                (w_ref, wv),
+                (pre_ref, prev),
+            )
+        )
+    ]
+    for copy in loads:
+        copy.start()
+    meet(tab, blk)
+
+    def context_copy(which):
+        return pltpu.make_async_remote_copy(
+            src_ref=dctx_ref.at[which // 4, lax.rem(which, 4)],
+            dst_ref=dov.at[blk],
+            send_sem=dsend_sem.at[which],
+            recv_sem=drecv_sem.at[blk],
+            device_id=(tab, which),
+            device_id_type=MESH,
+        )
+
+    @pl.loop(1, 8)
+    def _(step):
+        context_copy(lax.rem(blk + 8 - step, 8)).start()
+
+    for copy in loads[:4]:
+        copy.wait()
+    for head in range(heads):
+        ktv[head] = qkvv[heads + head].T
+
+    def gradient_copy(head, which):
+        return pltpu.make_async_remote_copy(
+            src_ref=dqkv.at[head, which],
+            dst_ref=arrive.at[half, group * heads + head],
+            send_sem=gsend_sem.at[head, which],
+            recv_sem=grecv_sem.at[half, group * heads + head],
+            device_id=(tab, which),
+            device_id_type=MESH,
+        )
+
+    def own_gradient(head):
+        return pltpu.make_async_copy(
+            dqkv.at[head, blk], arrive.at[half, group * heads + head], own_sem.at[head]
+        )
+
+    for head in range(heads):
+
+        @pl.loop(0, 8)
+        def _(step, head=head):
+            which = lax.rem(blk + step, 8)
+            first = pl.multiple_of(which * rows, rows)
+            if head == 0:
+
+                @pl.when(step > 0)
+                def _():
+                    pltpu.make_async_copy(
+                        dov.at[which], dov.at[which], drecv_sem.at[which]
+                    ).wait()
+
+            q = qkvv[head, pl.ds(first, rows)][:, :HD]
+            q_full = qkvv[head, pl.ds(first, rows)]
+            do = dov[which][:, head * HD : (head + 1) * HD]
+            ot = otv[which, head * HD : (head + 1) * HD]
+            delta = jnp.sum(ot * do.astype(jnp.float32).T, axis=0, keepdims=True)
+            st = times_t(qkvv[heads + head], q_full)
+            pt = jnp.exp2(st * scale - lsev[which, head : head + 1])
+            dpt = times_t(qkvv[2 * heads + head][:, :HD], do)
+            dst = (pt * (dpt - delta)).astype(jnp.bfloat16)
+            dv = jnp.dot(pt.astype(jnp.bfloat16), do, preferred_element_type=jnp.float32)
+            dk = jnp.dot(dst, q, preferred_element_type=jnp.float32)
+
+            @pl.when(step == 0)
+            def _():
+                dvv[...] = dv
+                dkv[...] = dk
+
+            @pl.when(step > 0)
+            def _():
+                dvv[...] += dv
+                dkv[...] += dk
+
+            dqt = jnp.dot(ktv[head], dst, preferred_element_type=jnp.float32)
+            dqv[which] = dqt[:HD].T * (HD**-0.5)
+
+        @pl.loop(0, 8)
+        def _(step, head=head):
+            which = lax.rem(blk + 1 + step, 8)
+            first = pl.multiple_of(which * rows, rows)
+            dqkv[head, which] = jnp.concatenate(
+                [
+                    dqv[which],
+                    dkv[pl.ds(first, rows)] * (HD**-0.5),
+                    dvv[pl.ds(first, rows)],
+                ],
+                axis=1,
+            ).astype(jnp.bfloat16)
+
+            @pl.when(step < 7)
+            def _():
+                gradient_copy(head, which).start()
+
+            @pl.when(step == 7)
+            def _():
+                own_gradient(head).start()
+
+    for copy in loads[4:]:
+        copy.wait()
+    for head in range(heads):
+        flat = dqkv[head].reshape(blocks * rows, 3 * HD)
+        tok = tokv[...].reshape(blocks * rows, tokv.shape[2])
+        wgrad_ref[head] = lax.dot_general(
+            tok, flat, (((0,), (0,)), ((), ())), preferred_element_type=jnp.float32
+        ).astype(jnp.bfloat16)
+        sums_ref[head : head + 1] = jnp.sum(
+            flat.astype(jnp.float32), axis=0, keepdims=True
+        )
+
+    for head in range(heads):
+        own_gradient(head).wait()
+
+        @pl.loop(1, 8)
+        def _(step, head=head):
+            which = lax.rem(blk + step, 8)
+            slot = lax.rem(which, 4) * heads + head
+            gradient_copy(head, which).wait_send()
+            pltpu.make_async_copy(
+                arrive.at[which // 4, slot],
+                arrive.at[which // 4, slot],
+                grecv_sem.at[which // 4, slot],
+            ).wait()
+
+    for table in range(2):
+
+        def add(at, total, table=table):
+            return total + times_t(arrive[table, at], wv[at])
+
+        total = lax.fori_loop(0, GROUPS * heads, add, prev[table])
+        tgrad_ref[table] = total.astype(jnp.bfloat16)
+
+    @pl.loop(1, 8)
+    def _(step):
+        context_copy(lax.rem(blk + 8 - step, 8)).wait_send()
+
+
+def attend_back(dctx, qkv, ot, lse, full, by_head, pre, heads):
+    blocks, rows, width = full.shape
+    total = blocks * rows
+    any_space = pl.BlockSpec(memory_space=pl.ANY)
+    vmem = pl.BlockSpec(memory_space=pltpu.VMEM)
+    bf16, f32 = jnp.bfloat16, jnp.float32
+    dma = pltpu.SemaphoreType.DMA
+    return pl.pallas_call(
+        functools.partial(attend_back_kernel, heads),
+        name="attend_back",
+        out_shape=(
+            jax.ShapeDtypeStruct((2, rows, width), bf16),
+            jax.ShapeDtypeStruct((heads, width, 3 * HD), bf16),
+            jax.ShapeDtypeStruct((8, 3 * HD), f32),
+        ),
+        in_specs=[any_space] * 7,
+        out_specs=(vmem,) * 3,
+        scratch_shapes=[
+            pltpu.VMEM((blocks, rows, heads * HD), bf16),
+            pltpu.VMEM((3 * heads, total, LANES), bf16),
+            pltpu.VMEM((blocks, heads * HD, rows), f32),
+            pltpu.VMEM((blocks, 8, rows), f32),
+            pltpu.VMEM((blocks, rows, width), bf16),
+            pltpu.VMEM(by_head.shape, bf16),
+            pltpu.VMEM((2, rows, width), f32),
+            pltpu.VMEM((heads, LANES, total), bf16),
+            pltpu.VMEM((blocks, rows, HD), f32),
+            pltpu.VMEM((total, HD), f32),
+            pltpu.VMEM((total, HD), f32),
+            pltpu.VMEM((heads, blocks, rows, 3 * HD), bf16),
+            pltpu.VMEM((2, GROUPS * heads, rows, 3 * HD), bf16),
+            dma((blocks,)),
+            dma((blocks,)),
+            dma((heads, blocks)),
+            dma((2, GROUPS * heads)),
+            dma((7,)),
+            dma((heads,)),
+        ],
+        compiler_params=pltpu.CompilerParams(
+            collective_id=2, has_side_effects=True, vmem_limit_bytes=60 << 20
+        ),
+    )(dctx, qkv, ot, lse, full, by_head, pre)
+
+
+def scatter_sum(grad):
+    return lax.psum_scatter(
+        lax.psum_scatter(
+            grad.astype(jnp.bfloat16), "tab", scatter_dimension=0, tiled=True
+        ),
+        "blk",
+        scatter_dimension=0,
+        tiled=True,
+    ).astype(jnp.float32)
+
+
+def shards_direct(
+    tokens,
+    lengths,
+    qkv_weight,
+    qkv_bias,
+    out_weight,
+    out_bias,
+    attn_gain,
+    attn_shift,
+    up_weight,
+    up_bias,
+    down_weight,
+    down_bias,
+    ffn_gain,
+    ffn_shift,
+    cotangent,
+):
+    tables, rows, width = tokens.shape
+    f32, bf16 = jnp.float32, jnp.bfloat16
+    all_heads = width // HD
+    heads = all_heads // GROUPS
+    blk = lax.axis_index("blk")
+    group = blk % GROUPS
+    flat_tokens = tokens.reshape(tables * rows, width)
+
+    by_group = qkv_weight.reshape(width, 3, GROUPS, heads, HD)
+    own = lax.dynamic_index_in_dim(by_group, group, 2, keepdims=False)
+    own_weight = jnp.pad(own, ((0, 0), (0, 0), (0, 0), (0, LANES - HD))).reshape(width, -1)
+    bias_full = jnp.concatenate(
+        [
+            qkv_bias[:width].astype(f32),
+            jnp.zeros((width,), f32),
+            qkv_bias[width:].astype(f32),
+        ]
+    ).reshape(3, GROUPS, heads, HD)
+    own_bias = jnp.pad(
+        lax.dynamic_index_in_dim(bias_full, group, 1, keepdims=False),
+        ((0, 0), (0, 0), (0, LANES - HD)),
+    )
+    ones = jnp.zeros((3, 1, LANES), f32).at[0::2, :, HD].set(1.0)
+    own_bias = (own_bias + ones).reshape(1, -1)
+    by_head = (
+        qkv_weight.reshape(width, 3, all_heads, HD)
+        .transpose(2, 0, 1, 3)
+        .reshape(all_heads, width, 3 * HD)
+    )
+
+    ctx, full, qkv, ot, lse = attend(tokens, lengths, own_weight, own_bias, heads)
+
+    context_low = ctx.transpose(0, 2, 1, 3).reshape(tables * rows, width)
+    attended = jnp.dot(context_low, out_weight, preferred_element_type=f32) + out_bias.astype(
+        f32
+    )
+    pre_one = flat_tokens.astype(f32) + attended
+    gain_one = attn_gain.astype(f32)
+    shift_one = attn_shift.astype(f32)
+    hidden = norm_rows(pre_one, gain_one, shift_one)
+    hidden_low = hidden.astype(bf16)
+    upper = jnp.dot(hidden_low, up_weight, preferred_element_type=f32) + up_bias.astype(f32)
+    active = gelu_exact(upper).astype(bf16)
+    pre_two = (
+        hidden
+        + jnp.dot(active, down_weight, preferred_element_type=f32)
+        + down_bias.astype(f32)
+    )
+    gain_two = ffn_gain.astype(f32)
+    shift_two = ffn_shift.astype(f32)
+    layer_out = norm_rows(pre_two, gain_two, shift_two).astype(bf16).reshape(tokens.shape)
+    grad_out = cotangent.reshape(tables * rows, width).astype(f32)
+    _, norm_two_back = jax.vjp(norm_rows, pre_two, gain_two, shift_two)
+    grad_pre_two, ggrad_ffn, sgrad_ffn = norm_two_back(grad_out)
+    grad_branch = grad_pre_two.astype(bf16)
+    wgrad_down = over_rows(active, grad_branch)
+    bgrad_down = jnp.sum(grad_branch, axis=0, dtype=f32)
+    grad_active = times_back(grad_branch, down_weight)
+    _, gelu_back = jax.vjp(gelu_exact, upper)
+    grad_upper = gelu_back(grad_active)[0].astype(bf16)
+    wgrad_up = over_rows(hidden_low, grad_upper)
+    bgrad_up = jnp.sum(grad_upper, axis=0, dtype=f32)
+    grad_hidden = grad_pre_two + times_back(grad_upper, up_weight)
+    _, norm_one_back = jax.vjp(norm_rows, pre_one, gain_one, shift_one)
+    grad_pre_one, ggrad_attn, sgrad_attn = norm_one_back(grad_hidden)
+    grad_attended = grad_pre_one.astype(bf16)
+    wgrad_out = over_rows(context_low, grad_attended)
+    bgrad_out = jnp.sum(grad_attended, axis=0, dtype=f32)
+    grad_context = times_back(grad_attended, out_weight).astype(bf16)
+    dctx = grad_context.reshape(tables, rows, GROUPS, heads * HD).transpose(0, 2, 1, 3)
+
+    token_grad, wgrad_part, sums = attend_back(
+        dctx, qkv, ot, lse, full, by_head, grad_pre_one.reshape(tokens.shape), heads
+    )
+
+    part = lax.psum_scatter(
+        wgrad_part.transpose(1, 0, 2), "tab", scatter_dimension=0, tiled=True
+    )
+    part = lax.all_to_all(
+        part.reshape(8, -1, heads, 3 * HD), "blk", split_axis=0, concat_axis=0, tiled=True
+    )
+    part = part.reshape(2, GROUPS, -1, heads, 3, HD).astype(f32).sum(axis=0)
+    wgrad_qkv = part.transpose(1, 3, 0, 2, 4).reshape(-1, 3 * width)
+
+    sums = sums[:heads].reshape(heads, 3, HD)[:, 0::2].transpose(1, 0, 2)
+    placed = jnp.zeros((2, GROUPS, heads, HD), f32)
+    placed = lax.dynamic_update_slice(placed, sums[:, None], (0, group, 0, 0)).reshape(-1)
+    small = (placed, bgrad_out, ggrad_attn, sgrad_attn, bgrad_up, bgrad_down, ggrad_ffn, sgrad_ffn)
+    small = jnp.concatenate([s.reshape(32, -1) for s in small], axis=1).astype(f32)
+    small = lax.psum_scatter(
+        small.reshape(4, -1), "tab", scatter_dimension=0, tiled=True
+    ).reshape(8, -1)
+    small = lax.psum_scatter(small, "blk", scatter_dimension=0, tiled=True).reshape(-1)
+    each = width // 32
+    cuts = [2 * each, 3 * each, 4 * each, 5 * each]
+    cuts += [cuts[-1] + up_bias.shape[0] // 32]
+    cuts += [cuts[-1] + each, cuts[-1] + 2 * each]
+    (
+        bgrad_qkv,
+        bgrad_out,
+        ggrad_attn,
+        sgrad_attn,
+        bgrad_up,
+        bgrad_down,
+        ggrad_ffn,
+        sgrad_ffn,
+    ) = jnp.split(small, cuts)
+    return (
+        layer_out,
+        token_grad,
+        wgrad_qkv,
+        bgrad_qkv,
+        scatter_sum(wgrad_out),
+        bgrad_out,
+        ggrad_attn,
+        sgrad_attn,
+        scatter_sum(wgrad_up),
+        bgrad_up,
+        scatter_sum(wgrad_down),
+        bgrad_down,
+        ggrad_ffn,
+        sgrad_ffn,
+    )
+
+
 def solution(mesh):
     in_specs = (
         P("tab", "blk", None),
@@ -357,4 +1017,15 @@
         P(("tab", "blk")),
         P(("tab", "blk")),
     )
-    return jax.shard_map(shards, mesh=mesh, in_specs=in_specs, out_specs=out_specs, check_vma=False)
+    tab_count, blk_count = mesh.shape["tab"], mesh.shape["blk"]
+
+    def pick(*operands):
+        table_count = operands[0].shape[0] // tab_count
+        head_count = operands[0].shape[2] // HD
+        direct = table_count == 2 and blk_count == 8 and tab_count == 4 and head_count % 4 == 0
+        body = shards_direct if direct else shards_ring
+        return jax.shard_map(
+            body, mesh=mesh, in_specs=in_specs, out_specs=out_specs, check_vma=False
+        )(*operands)
+
+    return pick

time: 1060 us -> 446 us (0.42)
  waiting for transfers between devices: 563 us -> 85.2 us
  Pallas kernels: 0 us -> 181 us
  matrix products: 200 us -> 57.4 us
  local copies, waits for them, and re-layouts: 134 us -> 40.3 us
  other arithmetic: 98.2 us -> 11.8 us
  blocking collectives: 31.2 us -> 42 us
    ppermute x16 -> x0, waiting for transfers between devices: 249 us -> none  [from_behind(): return lax.ppermute(block, axis, route)]
    pallas_call x0 -> x2, Pallas kernels: none -> 181 us  [the longest x1 102 us: attend_back(): pl.pallas_call(functools.partial(attend_back_kernel, heads), name='attend...]
    dot_general x46 -> x3, matrix products: 157 us -> 23.8 us  [the longest x1 20.1 us: shards_direct(): jnp.dot(hidden_low, up_weight, preferred_element_type=f32)]
    all_gather x1 -> x0, waiting for transfers between devices: 100 us -> none  [shards(): pair_block = lax.all_gather(key_values, 'blk', axis=1, tiled=True)]
    reduce_scatter x6 -> x7, waiting for transfers between devices: 181 us -> 84.1 us  [the longest x3 39.3 us: scatter_sum(): lax.psum_scatter(lax.psum_scatter(grad.astype(jnp.bfloat16), 'tab', scatt...]
    convert_element_type x32 -> x11, other arithmetic: 58.4 us -> 6.85 us  [the longest x3 4.69 us: scatter_sum(): return lax.psum_scatter(lax.psum_scatter(grad.astype(jnp.bfloat16), 'tab'...]
    slice x15 -> x2, local copies, waits for them, and re-layouts: 45.1 us -> 0.03 us  [shards_direct(): sums = sums[:heads].reshape(heads, 3, HD)[:, 0::2].transpose(1, 0, 2)]
    while x121 -> x0, local copies, waits for them, and re-layouts: 43.2 us -> none
  transfers between devices with their start and end apart: 25 -> 8, of which waited for: 23 -> 4; matrix products, arithmetic and copies ran while one was open for 24% -> 10% of each run, Pallas kernels for 0% -> 23%
where the time goes in v1:
time: 446 us; the launch traced here: 437 us
  Pallas kernels  181 us (41%)
  waiting for transfers between devices  85.2 us (19%)
  matrix products  57.4 us (13%)
  blocking collectives  42 us (9%)
  local copies, waits for them, and re-layouts  40.3 us (9%)
  between operations  15 us (3%)
  other arithmetic  11.8 us (3%)
  starting transfers between devices  4.89 us (1%)
    pallas_call x1, Pallas kernels, attend_back(): pl.pallas_call(functools.partial(attend_back_kernel, heads), name='attend...  102 us
    pallas_call x1, Pallas kernels, attend(): pl.pallas_call(functools.partial(attend_kernel, heads), name='attend', ou...  78.7 us
    unnamed x2, blocking collectives  42 us
    reduce_scatter x3, waiting for transfers between devices, scatter_sum(): lax.psum_scatter(lax.psum_scatter(grad.astype(jnp.bfloat16), 'tab', scatt...  39.3 us
    reduce_scatter x1, waiting for transfers between devices, shards_direct(): lax.psum_scatter(wgrad_part.transpose(1, 0, 2), 'tab', scatter_dimension=...  31.2 us
    dot_general x1, matrix products, shards_direct(): jnp.dot(hidden_low, up_weight, preferred_element_type=f32)  20.1 us
    dot_general x3, matrix products, times_back(): lax.dot_general(left, right, (((1,), (1,)), ((), ())), preferred_element_...  17.5 us
    dot_general x3, matrix products, over_rows(): lax.dot_general(left, right, (((0,), (0,)), ((), ())), preferred_element_...  16.1 us
  transfers between devices with their start and end apart: 8, of which 4 were waited for; matrix products, arithmetic and copies ran while one was open for 10% of the time, Pallas kernels for 23%

profile of v1, /device:TPU:0, one launch (start us, length us, event | category | flops | bytes accessed | tf_op | source)
XLA Modules:
  0.0 437.4 jit_solution(1565393063580921999)
XLA Ops:
  7.3 0.8 convert_element_type.132
  8.0 0.7 convert_element_type.130
  8.7 0.7 convert_element_type.126
  9.4 5.7 %copy.40 = bf16[768,2304]{0,1:T(8,128)(2,1)} copy(bf16[768,2304]{1,0:T(8,128)(2,1)} %param.17) | data formatting | bytes 7077888 | tf_op args[2]
  15.2 1.2 dynamic-slice_bitcast_fusion
  16.4 0.2 pad.9
  16.6 2.2 copy.41.w_ref
  19.1 0.6 scatter_fusion
  19.8 0.6 reshape.231.bias_ref
  20.4 78.7 %attend.1 = (bf16[2,4,256,192]{3,2,1,0:T(8,128)(2,1)}, bf16[8,256,768]{2,1,0:T(8,128)(2,1)}, bf16[9,2048,128]{2,1,0:T(8,128)(2,1)}, f32[8,192,256]{2,1,0:T(8,128)}, f32[8,8,256]{2,1,0:T(8,128)}) custom-call(bf16[2,256,768]{2,1,0:T(8,128)(2,1)} %tok_ref.1, s32[2]{0:T(128)} %len_ref.1, bf16[768,1152]{1,0:T(8,128)(2,1)} %copy.41.w_ref, f32[1,1152]{1,0:T(1,128)} %reshape.231.bias_ref), custom_call_target="tpu_custom_call" | custom-call | tf_op jit(solution)/shard_map/attend/pallas_call | solution.py:565
  99.0 2.5 copy.42
  101.5 0.2 copy.54
  101.8 0.9 fusion.27
  102.8 0.3 multiply_reduce_fusion.3
  103.1 20.1 %multiply_convert_fusion = (bf16[512,3072]{1,0:T(8,128)(2,1)S(1)}, f32[512,3072]{1,0:T(8,128)}, f32[512,3072]{1,0:T(8,128)}) fusion(f32[3072]{0:T(1024)S(1)} %convert_element_type.130, bf16[768,3072]{1,0:T(8,128)(2,1)} %param.23, f32[512,768]{1,0:T(8,128)S(1)} %get-tuple-element.57, f32[768]{0:T(1024)S(1)} %convert_element_type.128, ...), kind=kOutput, calls=%fused_computation.5 | convolution fusion | flops 2521694208 | bytes 22042624 | tf_op jit(solution)/shard_map/dot_general | solution.py:902
  123.2 2.8 fusion.28
  126.0 0.3 multiply_reduce_fusion.2
  126.4 0.8 fusion.9
  127.2 1.6 fusion.25
  128.8 0.2 convert_reduce_fusion.2
  129.0 10.2 %convert_reduce_fusion = (f32[3072]{0:T(1024)}, bf16[512,3072]{1,0:T(8,128)(2,1)}) fusion(f32[512,3072]{1,0:T(8,128)} %get-tuple-element.46, f32[512,3072]{1,0:T(8,128)} %get-tuple-element.58, f32[3072]{0:T(1024)S(1)} %convert_element_type.130, bf16[512,768]{1,0:T(8,128)(2,1)S(1)} %get-tuple-element.36, bf16[3072,768]{1,0:T(8,128)(2,1)S(1)} %bitcast.101), kind=kOutput, calls=%fused_computation.3 | convolution fusion | flops 2442654720 | bytes 21258240 | tf_op jit(solution)/shard_map/dot_general | solution.py:36
  139.2 5.6 %multiply_reduce_fusion = (f32[768]{0:T(1024)}, f32[512]{0:T(512)S(1)}, f32[768]{0:T(1024)}, f32[512,768]{1,0:T(8,128)S(1)}) fusion(f32[512,768]{1,0:T(8,128)S(1)} %get-tuple-element.57, f32[512]{0:T(512)S(1)} %fusion.15, f32[512]{0:T(512)S(1)} %broadcast_multiply_fusion.1, f32[768]{0:T(1024)S(1)} %convert_element_type.127, ...), kind=kOutput, calls=%fused_computation.32 | convolution fusion | flops 2419849216 | bytes 12600320 | tf_op jit(solution)/shard_map/dot_general | solution.py:36
  144.9 0.6 fusion.24
  145.5 0.2 convert_reduce_fusion.3
  145.8 1.8 convolution_convert_fusion.2
  147.6 7.4 %convolution_convert_fusion.1 = bf16[768,3072]{1,0:T(8,128)(2,1)} fusion(bf16[512,3072]{1,0:T(8,128)(2,1)} %get-tuple-element.38, f32[512,768]{1,0:T(8,128)} %copy-done.3, f32[768]{0:T(1024)} %copy-done.12, f32[768]{0:T(1024)} %copy-done.6, f32[512]{0:T(512)} %copy-done.8, f32[512]{0:T(512)S(1)} %broadcast_multiply_fusion.1), kind=kOutput, calls=%fused_computation.20 | convolution fusion | flops 2420244480 | bytes 9447424 | tf_op jit(solution)/shard_map/dot_general | solution.py:42
  155.1 6.9 %convolution_convert_fusion = bf16[3072,768]{1,0:T(8,128)(2,1)} fusion(bf16[512,3072]{1,0:T(8,128)(2,1)} %copy-done.20, bf16[512,768]{1,0:T(8,128)(2,1)} %copy-done.5), kind=kOutput, calls=%fused_computation.19 | convolution fusion | flops 2418278400 | bytes 8650752 | tf_op jit(solution)/shard_map/dot_general | solution.py:42
  162.1 1.7 convolution_convert_fusion.3
  163.8 2.8 reshape.266
  166.6 1.1 copy.59
  167.8 4.4 %copy.46 = bf16[12,768,3,64]{1,3,2,0:T(8,128)(2,1)} copy(bf16[12,768,3,64]{1,3,0,2:T(8,128)(2,1)} %bitcast.86) | data formatting | bytes 7077888 | tf_op jit(solution)/shard_map/transpose | solution.py:887
  172.1 6.3 %copy.47.w_ref = bf16[12,768,192]{2,1,0:T(8,128)(2,1)} copy(bf16[12,768,192]{1,2,0:T(8,128)(2,1)} %bitcast.88) | data formatting | bytes 7077888 | tf_op jit(solution)/shard_map/reshape | solution.py:888
  178.4 102.2 %attend_back.1 = (bf16[2,256,768]{2,1,0:T(8,128)(2,1)}, bf16[3,768,192]{2,1,0:T(8,128)(2,1)}, f32[8,192]{1,0:T(8,128)}) custom-call(bf16[2,4,256,192]{3,2,1,0:T(8,128)(2,1)} %bitcast.90, bf16[9,2048,128]{2,1,0:T(8,128)(2,1)} %get-tuple-element.23.qkv_ref, f32[8,192,256]{2,1,0:T(8,128)} %get-tuple-element.24.ot_ref, f32[8,8,256]{2,1,0:T(8,128)} %get-tuple-element.25.lse_ref, ...), custom_call_target="tpu_custom_call" | custom-call | tf_op jit(solution)/shard_map/attend_back/pallas_call | solution.py:796
  280.8 0.5 reduce-scatter.12.cloned.1.call-update
  281.4 0.5 reduce-scatter.16.cloned.1.call-update
  282.0 13.7 %reduce-scatter.18.cloned.1.call-done = bf16[768,768]{1,0:T(8,128)(2,1)} async-done(((bf16[3072,768]{1,0:T(8,128)(2,1)}), bf16[768,768]{1,0:T(8,128)(2,1)}) %reduce-scatter.18.cloned.1.call-update) | async-done | bytes 1179664 | tf_op jit(solution)/shard_map/reduce_scatter | solution.py:835
  295.7 0.1 reshape.240
  295.8 31.2 %reduce-scatter.8.cloned.1.call-done = bf16[192,3,192]{2,0,1:T(8,128)(2,1)} async-done(((bf16[768,3,192]{2,0,1:T(8,128)(2,1)}), bf16[192,3,192]{2,0,1:T(8,128)(2,1)}) %reduce-scatter.8.cloned.1.call-update) | async-done | bytes 221200 | tf_op jit(solution)/shard_map/reduce_scatter | solution.py:936
  327.0 1.7 copy.48
  328.7 4.6 %all-to-all-start = ((bf16[8,24,3,192]{3,1,2,0:T(8,128)(2,1)}), bf16[8,24,3,192]{3,1,2,0:T(8,128)(2,1)S(1)}, u32[]{:S(2)}, u32[]{:S(2)}) async-start(bf16[8,24,3,192]{3,1,2,0:T(8,128)(2,1)} %copy.48), calls=%async_computation.1 | async-start | bytes 589824 | tf_op jit(solution)/shard_map/all_to_all | solution.py:939
  333.3 0.1 convert_reduce_fusion.1
  333.4 0.1 reshape_reshape.3
  333.5 0.1 reshape.241
  333.9 0.1 reshape.245
  334.1 0.1 concatenate.12
  334.2 0.1 reshape.248
  334.4 0.6 dynamic-slice
  334.9 15.7 %all-reduce.3 = f32[4,2304]{1,0:T(4,128)S(1)} all-reduce(f32[4,2304]{1,0:T(4,128)S(1)} %reshape.248), channel_id=3, replica_groups=mesh['tab'=4,'blk'=8] {'tab'}, use_global_device_ids=true, to_apply=%region_18.19.clone | all-reduce | flops 9216 | bytes 73728
  350.7 0.7 dynamic-slice_reduce_fusion
  351.5 0.6 dynamic-slice.2
  352.0 26.3 %all-reduce.4 = f32[8,288]{1,0:T(8,128)S(1)} all-reduce(f32[8,288]{1,0:T(8,128)S(1)} %reshape.249), channel_id=4, replica_groups=mesh['tab'=4,'blk'=8] {'blk'}, use_global_device_ids=true, to_apply=%region_19.20.clone | all-reduce | flops 2304 | bytes 18432
  378.3 1.2 dynamic-slice_bitcast_fusion.8
  379.5 1.2 dynamic-slice_bitcast_fusion.4
  380.7 1.3 dynamic-slice_bitcast_fusion.1
  382.0 0.4 reshape.254
  382.3 0.6 reduce_sum.154
  382.9 0.3 copy.49
  383.2 1.1 reshape.239
  384.3 1.4 convert_element_type.149
  385.7 7.4 %reduce-scatter.16.cloned.1.call-done = bf16[24,3072]{1,0:T(8,128)(2,1)} async-done(((bf16[192,3072]{1,0:T(8,128)(2,1)}), bf16[24,3072]{1,0:T(8,128)(2,1)}) %reduce-scatter.16.cloned.1.call-update) | async-done | bytes 147472 | tf_op jit(solution)/shard_map/reduce_scatter | solution.py:834
  393.1 1.6 convert_element_type.151
  394.7 31.9 %reduce-scatter.20.cloned.1.call-done = bf16[96,768]{1,0:T(8,128)(2,1)} async-done(((bf16[768,768]{1,0:T(8,128)(2,1)}), bf16[96,768]{1,0:T(8,128)(2,1)}) %reduce-scatter.20.cloned.1.call-update) | async-done | bytes 147472 | tf_op jit(solution)/shard_map/reduce_scatter | solution.py:834
  426.6 1.6 convert_element_type.153
  428.2 2.1 copy.63
  (99 shorter events, 1.5 us)
Async XLA Ops:
  7.2 94.6 %copy-start = (bf16[768,768]{1,0:T(8,128)(2,1)S(1)}, bf16[768,768]{1,0:T(8,128)(2,1)}, u32[]{:S(2)}) copy-start(bf16[768,768]{1,0:T(8,128)(2,1)} %param.19) | copy-start | bytes 3538948
  7.2 273.6 %reduce-scatter.10.cloned.1.call-start = ((), (), s32[]{:S(2)}) async-start(), calls=%async_computation.9 | async-start | bytes 1474560 | tf_op jit(solution)/shard_map/reduce_scatter | solution.py:835
  16.4 2.4 copy-start.9
  19.7 82.0 %copy-start.13 = (bf16[768]{0:T(1024)(128)(2,1)S(1)}, bf16[768]{0:T(1024)(128)(2,1)}, u32[]{:S(2)}) copy-start(bf16[768]{0:T(1024)(128)(2,1)} %param.22) | copy-start | bytes 4612
  19.7 82.0 %copy-start.14 = (bf16[768]{0:T(1024)(128)(2,1)S(1)}, bf16[768]{0:T(1024)(128)(2,1)}, u32[]{:S(2)}) copy-start(bf16[768]{0:T(1024)(128)(2,1)} %param.21) | copy-start | bytes 4612
  19.8 82.0 %copy-start.4 = (bf16[2,256,768]{2,1,0:T(8,128)(2,1)S(1)}, bf16[2,256,768]{2,1,0:T(8,128)(2,1)}, u32[]{:S(2)}) copy-start(bf16[2,256,768]{2,1,0:T(8,128)(2,1)} %tok_ref.1) | copy-start | bytes 2359300
  101.7 21.4 %copy-start.12 = (f32[768]{0:T(1024)}, f32[768]{0:T(1024)S(1)}, u32[]{:S(2)}) copy-start(f32[768]{0:T(1024)S(1)} %convert_element_type.128) | copy-start | bytes 9220
  101.8 43.1 %copy-start.6 = (f32[768]{0:T(1024)}, f32[768]{0:T(1024)S(1)}, u32[]{:S(2)}) copy-start(f32[768]{0:T(1024)S(1)} %convert_element_type.127) | copy-start | bytes 9220
  101.8 21.4 %slice-start = ((s8[4718592]{0:T(1024)(128)(4,1)}), s8[4194304]{0:T(1024)(128)(4,1)S(1)}, s32[]{:S(2)}) async-start(s8[4718592]{0:T(1024)(128)(4,1)} %bitcast.100), calls=%async_computation.15 | async-start | bytes 8388608
  102.7 42.1 %copy-start.3 = (f32[512,768]{1,0:T(8,128)}, f32[512,768]{1,0:T(8,128)S(1)}, u32[]{:S(2)}) copy-start(f32[512,768]{1,0:T(8,128)S(1)} %get-tuple-element.57) | copy-start | bytes 4718596
  103.1 41.8 %copy-start.8 = (f32[512]{0:T(512)}, f32[512]{0:T(512)S(1)}, u32[]{:S(2)}) copy-start(f32[512]{0:T(512)S(1)} %fusion.15) | copy-start | bytes 6148
  103.1 20.1 %slice-start.1 = ((s8[4718592]{0:T(1024)(128)(4,1)}), s8[524288]{0:T(1024)(128)(4,1)S(1)}, s32[]{:S(2)}) async-start(s8[4718592]{0:T(1024)(128)(4,1)} %bitcast.100), calls=%async_computation.16 | async-start | bytes 1048576
  123.2 2.8 copy-start.20
  123.2 3.1 copy-start.15
  123.2 3.2 copy-start.2
  126.0 1.1 copy-start.16
  127.2 12.0 %slice-start.2 = ((s8[4718592]{0:T(1024)(128)(4,1)}), s8[4194304]{0:T(1024)(128)(4,1)S(1)}, s32[]{:S(2)}) async-start(s8[4718592]{0:T(1024)(128)(4,1)} %bitcast.102), calls=%async_computation.17 | async-start | bytes 8388608
  129.0 10.2 %copy-start.5 = (bf16[512,768]{1,0:T(8,128)(2,1)}, bf16[512,768]{1,0:T(8,128)(2,1)S(1)}, u32[]{:S(2)}) copy-start(bf16[512,768]{1,0:T(8,128)(2,1)S(1)} %get-tuple-element.36) | copy-start | bytes 2359300
  129.0 10.2 %slice-start.3 = ((s8[4718592]{0:T(1024)(128)(4,1)}), s8[524288]{0:T(1024)(128)(4,1)S(1)}, s32[]{:S(2)}) async-start(s8[4718592]{0:T(1024)(128)(4,1)} %bitcast.102), calls=%async_computation.18 | async-start | bytes 1048576
  145.7 16.3 %copy-start.1 = (f32[512,768]{1,0:T(8,128)}, f32[512,768]{1,0:T(8,128)S(1)}, u32[]{:S(2)}) copy-start(f32[512,768]{1,0:T(8,128)S(1)} %get-tuple-element.40) | copy-start | bytes 4718596
  147.6 133.8 %reduce-scatter.14.cloned.1.call-start = ((), (), s32[]{:S(2)}) async-start(), calls=%async_computation.11 | async-start | bytes 5898240 | tf_op jit(solution)/shard_map/reduce_scatter | solution.py:835
  155.1 140.6 %reduce-scatter.18.cloned.1.call-start = ((), (), s32[]{:S(2)}) async-start(), calls=%async_computation.13 | async-start | bytes 5898240 | tf_op jit(solution)/shard_map/reduce_scatter | solution.py:835
  162.0 164.9 %reduce-scatter.8.cloned.1.call-start = ((), (), s32[]{:S(2)}) async-start(), calls=%async_computation.8 | async-start | bytes 1474560 | tf_op jit(solution)/shard_map/reduce_scatter | solution.py:936
  280.7 15.0 %copy-start.17 = (f32[8,192]{1,0:T(8,128)S(1)}, f32[8,192]{1,0:T(8,128)}, u32[]{:S(2)}) copy-start(f32[8,192]{1,0:T(8,128)} %get-tuple-element.29) | copy-start | bytes 18436
  280.7 52.9 %copy-start.11 = (f32[768]{0:T(1024)S(1)}, f32[768]{0:T(1024)}, u32[]{:S(2)}) copy-start(f32[768]{0:T(1024)} %get-tuple-element.30) | copy-start | bytes 9220
  280.7 53.0 %copy-start.10 = (f32[768]{0:T(1024)S(1)}, f32[768]{0:T(1024)}, u32[]{:S(2)}) copy-start(f32[768]{0:T(1024)} %get-tuple-element.34) | copy-start | bytes 9220
  280.7 53.1 %copy-start.7 = (f32[3072]{0:T(1024)S(1)}, f32[3072]{0:T(1024)}, u32[]{:S(2)}) copy-start(f32[3072]{0:T(1024)} %get-tuple-element.37) | copy-start | bytes 36868
  280.7 53.6 %copy-start.19 = (u32[32]{0:T(128)S(1)}, u32[32]{0:T(128)}, u32[]{:S(2)}) copy-start(u32[32]{0:T(128)} %constant.144) | copy-start | bytes 388
  280.7 70.7 %copy-start.18 = (u32[32]{0:T(128)S(1)}, u32[32]{0:T(128)}, u32[]{:S(2)}) copy-start(u32[32]{0:T(128)} %constant.148) | copy-start | bytes 388
  280.8 103.5 %reduce-scatter.12.cloned.1.call-start = ((), (), s32[]{:S(2)}) async-start(), calls=%async_computation.10 | async-start | bytes 331776 | tf_op jit(solution)/shard_map/reduce_scatter | solution.py:834
  281.3 111.7 %reduce-scatter.16.cloned.1.call-start = ((), (), s32[]{:S(2)}) async-start(), calls=%async_computation.12 | async-start | bytes 1327104 | tf_op jit(solution)/shard_map/reduce_scatter | solution.py:834
  281.9 144.7 %reduce-scatter.20.cloned.1.call-start = ((), (), s32[]{:S(2)}) async-start(), calls=%async_computation.14 | async-start | bytes 1327104 | tf_op jit(solution)/shard_map/reduce_scatter | solution.py:834
  328.7 53.3 %all-to-all-start = ((bf16[8,24,3,192]{3,1,2,0:T(8,128)(2,1)}), bf16[8,24,3,192]{3,1,2,0:T(8,128)(2,1)S(1)}, u32[]{:S(2)}, u32[]{:S(2)}) async-start(bf16[8,24,3,192]{3,1,2,0:T(8,128)(2,1)} %copy.48), calls=%async_computation.1 | async-start | bytes 589824 | tf_op jit(solution)/shard_map/all_to_all | solution.py:939
Sparse Core Ops, SparseCore 0:
  147.7 27.6 reduce-scatter.9
  178.3 57.1 reduce-scatter.13
  238.5 57.0 reduce-scatter.17
  298.4 28.5 reduce-scatter.7
  329.1 30.6 reduce-scatter.11
  362.0 31.0 reduce-scatter.15
  395.5 31.0 reduce-scatter.19

commit v2 on v1

--- a/solution.py
+++ b/solution.py
@@ -358,18 +358,32 @@
     pl.semaphore_wait(barrier, 7)
 
 
+def own_window(group, first, rows_ref, out):
+    start = pl.multiple_of(first + LANES * ((3 * group) // 2), LANES)
+    window = rows_ref[:, pl.ds(start, 2 * LANES)].astype(jnp.float32)
+    window = pltpu.roll(window, lax.rem(2 * LANES - HD * lax.rem(group, 2), 2 * LANES), 1)
+    left = window[:, :LANES]
+    low = lax.broadcasted_iota(jnp.int32, left.shape, 1) < HD
+    for head, lanes in enumerate((left, pltpu.roll(left, HD, 1), window[:, LANES:])):
+        out(head, jnp.where(low, lanes, 0.0))
+
+
 def attend_kernel(
     heads,
     tok_ref,
     len_ref,
-    w_ref,
-    bias_ref,
+    par_ref,
+    w_hbm,
     ctx_ref,
-    full_ref,
+    fullt_ref,
     qkv_ref,
     ot_ref,
     lse_ref,
     tokv,
+    toktv,
+    wfull,
+    wown,
+    bown,
     qkvv,
     vtv,
     otv,
@@ -387,7 +401,9 @@
 ):
     tab, blk, chip, core = place()
     half = chip // 2
+    group = 2 * lax.rem(chip, 2) + core
     rows = tok_ref.shape[1]
+    width = tok_ref.shape[2]
     piece = rows // CHUNKS
     is_near = jnp.logical_or(chip == 1, chip == 2)
     mate = chip + 1 - 2 * lax.rem(chip, 2)
@@ -416,35 +432,54 @@
             remote(here, dst, send_b.at[part], done, chip, 1 - core),
         )
 
-    def onward(slot, part, src_chip):
-        cut = pl.ds(part * piece, piece)
+    def to_far(slot, part, src_chip):
         which = 2 * src_chip + core
-        ref, done = tokv.at[which, cut], recv.at[which, part]
-        return (
-            remote(ref, ref, send_d.at[slot, part], done, own_far, core),
-            remote(ref, ref, send_e.at[slot, part], done, chip, 1 - core),
-        )
+        ref = tokv.at[which, pl.ds(part * piece, piece)]
+        return remote(ref, ref, send_d.at[slot, part], recv.at[which, part], own_far, core)
+
+    def to_core(slot, part, src_chip):
+        which = 2 * src_chip + core
+        ref = tokv.at[which, pl.ds(part * piece, piece)]
+        return remote(ref, ref, send_e.at[slot, part], recv.at[which, part], chip, 1 - core)
 
     def arrived(which, part):
         ref = tokv.at[which, pl.ds(part * piece, piece)]
         pltpu.make_async_copy(ref, ref, recv.at[which, part]).wait()
 
+    load = pltpu.make_async_copy(w_hbm, wfull, local_sem.at[5])
+    load.start()
     meet(tab, blk)
     for part in range(CHUNKS):
         for copy in own_copies(part):
             copy.start()
     tokv[blk] = tok_ref[half]
 
+    lane1 = lax.broadcasted_iota(jnp.int32, (8, LANES), 1)
+    for at in (0, 2):
+
+        def keep_bias(head, lanes, at=at):
+            row = jnp.where(lane1 == HD, 1.0, lanes)
+            bown[:, pl.ds((at * heads + head) * LANES, LANES)] = row
+
+        own_window(group, 0, par_ref.at[pl.ds(8 * (1 + at // 2), 8)], keep_bias)
+    for head in range(heads):
+        bown[:, pl.ds((heads + head) * LANES, LANES)] = jnp.zeros((8, LANES), jnp.float32)
+    load.wait()
+    for at in range(3):
+
+        def keep_weight(head, lanes, at=at):
+            wown[:, pl.ds((at * heads + head) * LANES, LANES)] = lanes.astype(jnp.bfloat16)
+
+        own_window(group, at * width, wfull, keep_weight)
+
     length = len_ref[half]
     lane = lax.broadcasted_iota(jnp.int32, (rows, LANES), 1)
     row = lax.broadcasted_iota(jnp.int32, (rows, LANES), 0)
 
     def project(which):
         first = pl.multiple_of(which * rows, rows)
-        y = (
-            jnp.dot(tokv[which], w_ref[...], preferred_element_type=jnp.float32)
-            + bias_ref[...]
-        )
+        tok = tokv[which]
+        y = jnp.dot(tok, wown[...], preferred_element_type=jnp.float32) + bown[:1]
         pad = jnp.where((lane == HD) & (row + first >= length), NEGATIVE, 0.0)
         for head in range(heads):
             q, k, v = (
@@ -454,11 +489,12 @@
             qkvv[heads + head, pl.ds(first, rows)] = (k + pad).astype(jnp.bfloat16)
             qkvv[2 * heads + head, pl.ds(first, rows)] = v.astype(jnp.bfloat16)
             vtv[head, :, pl.ds(first, rows)] = v.T.astype(jnp.bfloat16)
+        toktv[:, pl.ds(first, rows)] = tok.T
 
     project(blk)
     for part in range(CHUNKS):
         arrived(2 * mate + core, part)
-        onward(0, part, mate)[1].start()
+        to_core(0, part, mate).start()
     project(2 * mate + core)
     for part in range(CHUNKS):
         arrived(2 * chip + 1 - core, part)
@@ -469,9 +505,8 @@
     for part in range(CHUNKS):
         for slot, src_chip in ((1, other_near), (2, other_far)):
             arrived(2 * src_chip + core, part)
-            to_far, to_core = onward(slot, part, src_chip)
-            pl.when(is_near)(to_far.start)
-            to_core.start()
+            pl.when(is_near)(to_far(slot, part, src_chip).start)
+            to_core(slot, part, src_chip).start()
     for src_chip in (other_near, other_far):
         project(2 * src_chip + core)
         for part in range(CHUNKS):
@@ -479,13 +514,11 @@
         project(2 * src_chip + 1 - core)
 
     keep = (
-        pltpu.make_async_copy(tokv, full_ref, local_sem.at[0]),
+        pltpu.make_async_copy(toktv, fullt_ref, local_sem.at[0]),
         pltpu.make_async_copy(qkvv, qkv_ref, local_sem.at[1]),
     )
     for copy in keep:
         copy.start()
-
-    group = 2 * lax.rem(chip, 2) + core
 
     def context_copy(which):
         return remote(
@@ -501,12 +534,12 @@
         csend.at[blk], ctx_ref.at[half, group], local_sem.at[2]
     )
 
-    @pl.loop(0, 8)
+    @pl.loop(0, 4)
     def _(step):
-        which = lax.rem(blk + 1 + step, 8)
-        first = pl.multiple_of(which * rows, rows)
+        which = lax.rem(chip + 1 + step, 4)
+        first = pl.multiple_of(which * 2 * rows, 2 * rows)
         for head in range(heads):
-            q = qkvv[head, pl.ds(first, rows)]
+            q = qkvv[head, pl.ds(first, 2 * rows)]
             st = times_t(qkvv[heads + head], q)
             peak = jnp.max(st, axis=0, keepdims=True)
             pt = jnp.exp2((st - peak) * scale).astype(jnp.bfloat16)
@@ -514,14 +547,18 @@
             total = ot[HD : HD + 1]
             otv[which, head * HD : (head + 1) * HD] = ot[:HD] / total
             lsev[which, head : head + 1] = peak * scale + jnp.log(total) * LOG2E
-        csend[which] = otv[which].T.astype(jnp.bfloat16)
-
-        @pl.when(step < 7)
+        out = otv[which].T.astype(jnp.bfloat16)
+        csend[2 * which] = out[:rows]
+        csend[2 * which + 1] = out[rows:]
+
+        @pl.when(step < 3)
         def _():
-            context_copy(which).start()
-
-        @pl.when(step == 7)
+            context_copy(2 * which).start()
+            context_copy(2 * which + 1).start()
+
+        @pl.when(step == 3)
         def _():
+            context_copy(2 * which + 1 - core).start()
             own_context.start()
 
     more = (
@@ -533,15 +570,14 @@
     for part in range(CHUNKS):
         for copy in own_copies(part):
             copy.wait_send()
-        onward(0, part, mate)[1].wait_send()
+        to_core(0, part, mate).wait_send()
         for slot, src_chip in ((1, other_near), (2, other_far)):
-            to_far, to_core = onward(slot, part, src_chip)
-            pl.when(is_near)(to_far.wait_send)
-            to_core.wait_send()
-
-    @pl.loop(0, 7)
+            pl.when(is_near)(to_far(slot, part, src_chip).wait_send)
+            to_core(slot, part, src_chip).wait_send()
+
+    @pl.loop(1, 8)
     def _(step):
-        which = lax.rem(blk + 1 + step, 8)
+        which = lax.rem(blk + step, 8)
         context_copy(which).wait_send()
         pltpu.make_async_copy(
             ctx_ref.at[which // 4, lax.rem(which, 4)],
@@ -554,7 +590,7 @@
         copy.wait()
 
 
-def attend(tokens, lengths, own_weight, own_bias, heads):
+def attend(tokens, lengths, params, qkv_weight, heads):
     tables, rows, width = tokens.shape
     blocks = 8
     total = blocks * rows
@@ -567,19 +603,23 @@
         name="attend",
         out_shape=(
             jax.ShapeDtypeStruct((tables, GROUPS, rows, heads * HD), bf16),
-            jax.ShapeDtypeStruct((blocks, rows, width), bf16),
+            jax.ShapeDtypeStruct((width, total), bf16),
             jax.ShapeDtypeStruct((3 * heads, total, LANES), bf16),
-            jax.ShapeDtypeStruct((blocks, heads * HD, rows), f32),
-            jax.ShapeDtypeStruct((blocks, 8, rows), f32),
+            jax.ShapeDtypeStruct((4, heads * HD, 2 * rows), f32),
+            jax.ShapeDtypeStruct((4, 8, 2 * rows), f32),
         ),
-        in_specs=[vmem, pl.BlockSpec(memory_space=pltpu.SMEM), vmem, vmem],
+        in_specs=[vmem, pl.BlockSpec(memory_space=pltpu.SMEM), vmem, any_space],
         out_specs=(any_space,) * 5,
         scratch_shapes=[
             pltpu.VMEM((blocks, rows, width), bf16),
+            pltpu.VMEM((width, total), bf16),
+            pltpu.VMEM(qkv_weight.shape, bf16),
+            pltpu.VMEM((width, 3 * heads * LANES), bf16),
+            pltpu.VMEM((8, 3 * heads * LANES), f32),
             pltpu.VMEM((3 * heads, total, LANES), bf16),
             pltpu.VMEM((heads, LANES, total), bf16),
-            pltpu.VMEM((blocks, heads * HD, rows), f32),
-            pltpu.VMEM((blocks, 8, rows), f32),
+            pltpu.VMEM((4, heads * HD, 2 * rows), f32),
+            pltpu.VMEM((4, 8, 2 * rows), f32),
             pltpu.VMEM((blocks, rows, heads * HD), bf16),
             dma((CHUNKS,)),
             dma((CHUNKS,)),
@@ -589,12 +629,18 @@
             dma((blocks, CHUNKS)),
             dma((blocks,)),
             dma((blocks,)),
-            dma((5,)),
+            dma((6,)),
         ],
         compiler_params=pltpu.CompilerParams(
-            collective_id=1, has_side_effects=True, vmem_limit_bytes=56 << 20
+            collective_id=1, has_side_effects=True, vmem_limit_bytes=60 << 20
         ),
-    )(tokens, lengths, own_weight, own_bias)
+    )(tokens, lengths, params, qkv_weight)
+
+
+UNITS = 9
+TURNS = 4
+STAGES = 5
+PHASE = (1, 3, 5, 7, 9)
 
 
 def attend_back_kernel(
@@ -603,17 +649,24 @@
     qkv_ref,
     ot_ref,
     lse_ref,
-    full_ref,
+    fullt_ref,
     w_ref,
     pre_ref,
+    parts_ref,
+    small_ref,
     tgrad_ref,
-    wgrad_ref,
-    sums_ref,
+    wqkv_ref,
+    wout_ref,
+    wup_ref,
+    wdown_ref,
+    little_ref,
     dov,
+    doh,
+    deltas,
     qkvv,
     otv,
     lsev,
-    tokv,
+    toktv,
     wv,
     prev,
     ktv,
@@ -622,18 +675,58 @@
     dvv,
     dqkv,
     arrive,
+    joined,
+    mine,
+    sum0,
+    sum1,
+    sum2,
+    sum3,
+    sum4,
+    slab,
+    slab_in,
+    line,
+    line_in,
+    small_in,
+    small_line,
+    small_line_in,
     dsend_sem,
     drecv_sem,
     gsend_sem,
     grecv_sem,
+    ssend_sem,
+    srecv_sem,
+    tsend_sem,
+    trecv_sem,
+    lsend_sem,
+    lrecv_sem,
     local_sem,
     own_sem,
+    mine_sem,
 ):
+    f32, bf16 = jnp.float32, jnp.bfloat16
     tab, blk, chip, core = place()
-    half = chip // 2
-    group = 2 * lax.rem(chip, 2) + core
+    y, x, zh, zl = tab // 2, lax.rem(tab, 2), chip // 2, lax.rem(chip, 2)
+    half = zh
+    group = 2 * zl + core
     blocks, rows = dov.shape[0], dov.shape[1]
+    width = toktv.shape[0]
+    tile = 2 * rows
+    piece = 256
     scale = LOG2E / math.sqrt(HD)
+    shrink = HD**-0.5
+
+    def remote(src, dst, send_sem, recv_sem, device):
+        return pltpu.make_async_remote_copy(
+            src_ref=src,
+            dst_ref=dst,
+            send_sem=send_sem,
+            recv_sem=recv_sem,
+            device_id=device,
+            device_id_type=MESH,
+        )
+
+    def landed(ref, sem):
+        pltpu.make_async_copy(ref, ref, sem).wait()
 
     loads = [
         pltpu.make_async_copy(src, dst, local_sem.at[at])
@@ -643,7 +736,7 @@
                 (ot_ref, otv),
                 (lse_ref, lsev),
                 (dctx_ref.at[half, group], dov.at[blk]),
-                (full_ref, tokv),
+                (fullt_ref, toktv),
                 (w_ref, wv),
                 (pre_ref, prev),
             )
@@ -651,21 +744,206 @@
     ]
     for copy in loads:
         copy.start()
-    meet(tab, blk)
+
+    barrier = pltpu.get_barrier_semaphore()
+    for step in range(1, 8):
+        pl.semaphore_signal(
+            barrier, inc=1, device_id=(tab, lax.rem(blk + step, 8)), device_id_type=MESH
+        )
+    for step in range(1, 4):
+        pl.semaphore_signal(
+            barrier, inc=1, device_id=(lax.rem(tab + step, 4), blk), device_id_type=MESH
+        )
+    pl.semaphore_wait(barrier, 10)
 
     def context_copy(which):
-        return pltpu.make_async_remote_copy(
-            src_ref=dctx_ref.at[which // 4, lax.rem(which, 4)],
-            dst_ref=dov.at[blk],
-            send_sem=dsend_sem.at[which],
-            recv_sem=drecv_sem.at[blk],
-            device_id=(tab, which),
-            device_id_type=MESH,
-        )
-
-    @pl.loop(1, 8)
-    def _(step):
-        context_copy(lax.rem(blk + 8 - step, 8)).start()
+        return remote(
+            dctx_ref.at[which // 4, lax.rem(which, 4)],
+            dov.at[blk],
+            dsend_sem.at[which],
+            drecv_sem.at[blk],
+            (tab, which),
+        )
+
+    for step in range(1, 8):
+        which = 2 * lax.rem(chip + 4 - step // 2, 4) + (
+            (1 - core) if step == 1 else (core if step % 2 == 0 else 1 - core)
+        )
+        context_copy(which).start()
+
+    def stage_copy(stage, unit, order=None):
+        send, done = ssend_sem.at[stage, unit], srecv_sem.at[stage, unit]
+        if stage == 0:
+            src = parts_ref.at[unit, :, :, :, :, 1 - core]
+            return remote(src, sum0.at[unit], send, done, (tab, 2 * chip + 1 - core))
+        if stage == 1 and order == 0:
+            return remote(
+                sum0.at[unit, :, 1 - x], sum1.at[unit], send, done, (2 * y + 1 - x, blk)
+            )
+        if stage == 1:
+            return remote(
+                sum0.at[unit, 1 - y], sum1.at[unit], send, done, (2 * (1 - y) + x, blk)
+            )
+        if stage == 2 and order == 0:
+            return remote(
+                sum1.at[unit, 1 - y], sum2.at[unit], send, done, (2 * (1 - y) + x, blk)
+            )
+        if stage == 2:
+            return remote(
+                sum1.at[unit, 1 - x], sum2.at[unit], send, done, (2 * y + 1 - x, blk)
+            )
+        if stage == 3:
+            src, there = sum2.at[unit, :, 1 - zl], 2 * zh + 1 - zl
+            return remote(src, sum3.at[unit], send, done, (tab, 2 * there + core))
+        src, there = sum3.at[unit, 1 - zh], 2 * (1 - zh) + zl
+        return remote(src, sum4.at[unit], send, done, (tab, 2 * there + core))
+
+    def both(act):
+        pl.when(core == 0)(functools.partial(act, 0))
+        pl.when(core == 1)(functools.partial(act, 1))
+
+    def mine_copy(unit):
+        slot = lax.rem(unit, 2)
+        return pltpu.make_async_copy(
+            parts_ref.at[unit, :, :, :, :, core], mine.at[slot], mine_sem.at[slot]
+        )
+
+    def finish(unit):
+        done = sum4[unit].astype(f32) + sum3[unit, zh].astype(f32)
+        top, low = done[: done.shape[0] // 2], done[done.shape[0] // 2 :]
+        each, cut = top.shape
+
+        @pl.when(unit < 4)
+        def _():
+            at = pl.ds(pl.multiple_of(unit * each, each), each)
+            wdown_ref[at, :cut] = top
+            wdown_ref[at, cut:] = low
+
+        @pl.when(jnp.logical_and(unit >= 4, unit < 8))
+        def _():
+            at = pl.multiple_of((unit - 4) * 2 * cut, 2 * cut)
+            wup_ref[:, pl.ds(at, cut)] = top
+            wup_ref[:, pl.ds(pl.multiple_of(at + cut, cut), cut)] = low
+
+        @pl.when(unit == 8)
+        def _():
+            wout_ref[:, :cut] = top
+            wout_ref[:, cut:] = low
+
+    def advance(stage, unit):
+        if stage == 0:
+            landed(sum0.at[unit], srecv_sem.at[0, unit])
+            mine_copy(unit).wait()
+            slot = lax.rem(unit, 2)
+            for a in range(2):
+                for b in range(2):
+                    sum0[unit, a, b] = sum0[unit, a, b] + mine[slot, a, b]
+
+            @pl.when(unit + 2 < UNITS)
+            def _():
+                mine_copy(unit + 2).start()
+
+            both(lambda order: stage_copy(1, unit, order).start())
+        elif stage == 1:
+            landed(sum1.at[unit], srecv_sem.at[1, unit])
+
+            def act(order):
+                own = sum0[unit, :, x] if order == 0 else sum0[unit, y]
+                sum1[unit] = sum1[unit] + own
+                stage_copy(2, unit, order).start()
+
+            both(act)
+        elif stage == 2:
+            landed(sum2.at[unit], srecv_sem.at[2, unit])
+
+            def act(order):
+                sum2[unit] = sum2[unit] + sum1[unit, y if order == 0 else x]
+
+            both(act)
+            stage_copy(3, unit).start()
+        elif stage == 3:
+            landed(sum3.at[unit], srecv_sem.at[3, unit])
+            sum3[unit] = sum3[unit] + sum2[unit, :, zl]
+            stage_copy(4, unit).start()
+        else:
+            landed(sum4.at[unit], srecv_sem.at[4, unit])
+            finish(unit)
+
+    def tick(now):
+        for stage in range(STAGES):
+            at = now - PHASE[stage]
+            unit = (5 * at + 6) // 7
+            due = (at >= 0) & (unit < UNITS) & ((7 * unit) // 5 == at)
+            pl.when(due)(functools.partial(advance, stage, unit))
+
+    for unit in range(UNITS):
+        stage_copy(0, unit).start()
+    for unit in range(2):
+        mine_copy(unit).start()
+
+    def tab_copy(src, dst, sem_at, step):
+        there = lax.rem(tab + step, 4)
+        return remote(
+            src(there), dst(tab), tsend_sem.at[sem_at, there], trecv_sem.at[sem_at, tab], (there, blk)
+        )
+
+    def line_copy(src, dst, sem_at, step):
+        there = lax.rem(blk + step, 8)
+        return remote(
+            src(there), dst(blk), lsend_sem.at[sem_at, there], lrecv_sem.at[sem_at, blk], (tab, there)
+        )
+
+    def small_tab(step):
+        return tab_copy(lambda t: small_ref, lambda t: small_in.at[t], heads, step)
+
+    def small_blk(step):
+        return line_copy(lambda b: small_line, lambda b: small_line_in.at[b], heads, step)
+
+    def slab_tab(head, step):
+        return tab_copy(
+            lambda t: slab.at[head, t], lambda t: slab_in.at[head, t], head, step
+        )
+
+    def slab_blk(head, step):
+        return line_copy(
+            lambda b: line.at[head, b], lambda b: line_in.at[head, b], head, step
+        )
+
+    for step in range(1, 4):
+        small_tab(step).start()
+
+    def pass_small():
+        total = small_ref[...]
+        for step in range(1, 4):
+            there = lax.rem(tab + step, 4)
+            landed(small_in.at[there], trecv_sem.at[heads, there])
+            total += small_in[there]
+        small_line[...] = total
+        for step in range(1, 8):
+            small_blk(step).start()
+
+    def make_slab(head):
+        flat = dqkv[head].reshape(blocks * rows, 3 * HD)
+        grad = jnp.dot(toktv[...], flat, preferred_element_type=f32)
+        sums = jnp.sum(flat.astype(f32), axis=0, keepdims=True)
+        sums = jnp.broadcast_to(sums, (8, 3 * HD))
+        grad = grad.reshape(4, 8, width // 32, 3 * HD)
+        for t in range(4):
+            for b in range(8):
+                slab[head, t, b] = jnp.concatenate([grad[t, b], sums], axis=0).astype(bf16)
+        for step in range(1, 4):
+            slab_tab(head, step).start()
+
+    def pass_slab(head):
+        total = slab[head, tab].astype(f32)
+        for step in range(1, 4):
+            there = lax.rem(tab + step, 4)
+            landed(slab_in.at[head, there], trecv_sem.at[head, there])
+            total += slab_in[head, there].astype(f32)
+        line[head] = total.astype(bf16)
+        line_in[head, blk] = line[head, blk]
+        for step in range(1, 8):
+            slab_blk(head, step).start()
 
     for copy in loads[:4]:
         copy.wait()
@@ -673,13 +951,12 @@
         ktv[head] = qkvv[heads + head].T
 
     def gradient_copy(head, which):
-        return pltpu.make_async_remote_copy(
-            src_ref=dqkv.at[head, which],
-            dst_ref=arrive.at[half, group * heads + head],
-            send_sem=gsend_sem.at[head, which],
-            recv_sem=grecv_sem.at[half, group * heads + head],
-            device_id=(tab, which),
-            device_id_type=MESH,
+        return remote(
+            dqkv.at[head, which],
+            arrive.at[half, group * heads + head],
+            gsend_sem.at[head, which],
+            grecv_sem.at[half, group * heads + head],
+            (tab, which),
         )
 
     def own_gradient(head):
@@ -687,147 +964,483 @@
             dqkv.at[head, blk], arrive.at[half, group * heads + head], own_sem.at[head]
         )
 
-    for head in range(heads):
-
-        @pl.loop(0, 8)
-        def _(step, head=head):
-            which = lax.rem(blk + step, 8)
-            first = pl.multiple_of(which * rows, rows)
-            if head == 0:
-
-                @pl.when(step > 0)
+    @pl.loop(0, heads * TURNS)
+    def _(turn):
+        head, step = turn // TURNS, lax.rem(turn, TURNS)
+        which = lax.rem(chip + step, 4)
+        first = pl.multiple_of(which * tile, tile)
+
+        @pl.when(head == 0)
+        def _():
+            for side in range(2):
+                block = 2 * which + side
+
+                @pl.when(block != blk)
                 def _():
-                    pltpu.make_async_copy(
-                        dov.at[which], dov.at[which], drecv_sem.at[which]
-                    ).wait()
-
-            q = qkvv[head, pl.ds(first, rows)][:, :HD]
-            q_full = qkvv[head, pl.ds(first, rows)]
-            do = dov[which][:, head * HD : (head + 1) * HD]
-            ot = otv[which, head * HD : (head + 1) * HD]
-            delta = jnp.sum(ot * do.astype(jnp.float32).T, axis=0, keepdims=True)
-            st = times_t(qkvv[heads + head], q_full)
-            pt = jnp.exp2(st * scale - lsev[which, head : head + 1])
-            dpt = times_t(qkvv[2 * heads + head][:, :HD], do)
-            dst = (pt * (dpt - delta)).astype(jnp.bfloat16)
-            dv = jnp.dot(pt.astype(jnp.bfloat16), do, preferred_element_type=jnp.float32)
-            dk = jnp.dot(dst, q, preferred_element_type=jnp.float32)
-
-            @pl.when(step == 0)
+                    landed(dov.at[block], drecv_sem.at[block])
+
+                for at in range(heads):
+                    do = dov[block][:, at * HD : (at + 1) * HD]
+                    doh[at, pl.ds(first + side * rows, rows)] = do
+                    ot = otv[which, at * HD : (at + 1) * HD, side * rows : (side + 1) * rows]
+                    deltas[at, which, :1, side * rows : (side + 1) * rows] = jnp.sum(
+                        ot * do.astype(f32).T, axis=0, keepdims=True
+                    )
+
+        @pl.when(step == 0)
+        def _():
+            dkv[...] = jnp.zeros_like(dkv)
+            dvv[...] = jnp.zeros_like(dvv)
+
+        tick(turn)
+
+        q_full = qkvv[head, pl.ds(first, tile)]
+        q = q_full[:, :HD]
+        do = doh[head, pl.ds(first, tile)]
+        delta = deltas[head, which, :1]
+        lse = lsev[which, pl.ds(head, 1)]
+        dqt = jnp.zeros((LANES, tile), f32)
+        for at in range(blocks * rows // piece):
+            cut = pl.ds(at * piece, piece)
+            st = times_t(qkvv[heads + head, cut], q_full)
+            pt = jnp.exp2(st * scale - lse)
+            dpt = times_t(qkvv[2 * heads + head, cut][:, :HD], do)
+            dst = (pt * (dpt - delta)).astype(bf16)
+            dvv[cut] += jnp.dot(pt.astype(bf16), do, preferred_element_type=f32)
+            dkv[cut] += jnp.dot(dst, q, preferred_element_type=f32)
+            dqt += jnp.dot(ktv[head, :, cut], dst, preferred_element_type=f32)
+        dqv[pl.ds(first, tile)] = dqt[:HD].T * shrink
+
+        @pl.when(step == TURNS - 1)
+        def _():
+            @pl.loop(0, 8)
+            def _(at):
+                block = lax.rem(blk + 1 + at, 8)
+                cut = pl.ds(pl.multiple_of(block * rows, rows), rows)
+                dqkv[head, block] = jnp.concatenate(
+                    [dqv[cut], dkv[cut] * shrink, dvv[cut]], axis=1
+                ).astype(bf16)
+
+                @pl.when(at < 7)
+                def _():
+                    gradient_copy(head, block).start()
+
+                @pl.when(at == 7)
+                def _():
+                    own_gradient(head).start()
+
+        @pl.when(jnp.logical_and(head > 0, step == 0))
+        def _():
+            @pl.when(head == 1)
             def _():
-                dvv[...] = dv
-                dkv[...] = dk
-
-            @pl.when(step > 0)
-            def _():
-                dvv[...] += dv
-                dkv[...] += dk
-
-            dqt = jnp.dot(ktv[head], dst, preferred_element_type=jnp.float32)
-            dqv[which] = dqt[:HD].T * (HD**-0.5)
-
-        @pl.loop(0, 8)
-        def _(step, head=head):
-            which = lax.rem(blk + 1 + step, 8)
-            first = pl.multiple_of(which * rows, rows)
-            dqkv[head, which] = jnp.concatenate(
-                [
-                    dqv[which],
-                    dkv[pl.ds(first, rows)] * (HD**-0.5),
-                    dvv[pl.ds(first, rows)],
-                ],
-                axis=1,
-            ).astype(jnp.bfloat16)
-
-            @pl.when(step < 7)
-            def _():
-                gradient_copy(head, which).start()
-
-            @pl.when(step == 7)
-            def _():
-                own_gradient(head).start()
-
-    for copy in loads[4:]:
-        copy.wait()
-    for head in range(heads):
-        flat = dqkv[head].reshape(blocks * rows, 3 * HD)
-        tok = tokv[...].reshape(blocks * rows, tokv.shape[2])
-        wgrad_ref[head] = lax.dot_general(
-            tok, flat, (((0,), (0,)), ((), ())), preferred_element_type=jnp.float32
-        ).astype(jnp.bfloat16)
-        sums_ref[head : head + 1] = jnp.sum(
-            flat.astype(jnp.float32), axis=0, keepdims=True
-        )
-
-    for head in range(heads):
+                loads[4].wait()
+                pass_small()
+
+            make_slab(head - 1)
+
+        @pl.when(jnp.logical_and(head > 0, step == 2))
+        def _():
+            pass_slab(head - 1)
+
+    make_slab(heads - 1)
+    for now in range(heads * TURNS, PHASE[1] + 12):
+        tick(now)
+    loads[5].wait()
+    loads[6].wait()
+
+    @pl.loop(0, heads)
+    def _(head):
         own_gradient(head).wait()
 
         @pl.loop(1, 8)
-        def _(step, head=head):
+        def _(step):
             which = lax.rem(blk + step, 8)
             slot = lax.rem(which, 4) * heads + head
             gradient_copy(head, which).wait_send()
-            pltpu.make_async_copy(
-                arrive.at[which // 4, slot],
-                arrive.at[which // 4, slot],
-                grecv_sem.at[which // 4, slot],
-            ).wait()
+            landed(arrive.at[which // 4, slot], grecv_sem.at[which // 4, slot])
+
+    pass_slab(heads - 1)
 
     for table in range(2):
-
-        def add(at, total, table=table):
-            return total + times_t(arrive[table, at], wv[at])
-
-        total = lax.fori_loop(0, GROUPS * heads, add, prev[table])
-        tgrad_ref[table] = total.astype(jnp.bfloat16)
-
-    @pl.loop(1, 8)
-    def _(step):
-        context_copy(lax.rem(blk + 8 - step, 8)).wait_send()
-
-
-def attend_back(dctx, qkv, ot, lse, full, by_head, pre, heads):
-    blocks, rows, width = full.shape
-    total = blocks * rows
+        for pair in range(GROUPS * heads // 2):
+            left, right = arrive[table, 2 * pair], arrive[table, 2 * pair + 1]
+            for part in range(3):
+                cut = slice(part * HD, (part + 1) * HD)
+                joined[:, pl.ds(part * width + pair * LANES, LANES)] = jnp.concatenate(
+                    [left[:, cut], right[:, cut]], axis=1
+                )
+        at = pl.ds(table * rows, rows)
+        tgrad_ref[table] = (prev[at] + times_t(joined[...], wv[...])).astype(bf16)
+
+    for now in range(PHASE[1] + 12, PHASE[-1] + 12):
+        tick(now)
+
+    def slabs_in(head, at):
+        return [line_in[head, half_at * GROUPS + at].astype(f32) for half_at in range(2)]
+
+    for head in range(heads):
+        for step in range(1, 8):
+            there = lax.rem(blk + step, 8)
+            landed(line_in.at[head, there], lrecv_sem.at[head, there])
+    total = small_line[...]
+    for step in range(1, 8):
+        there = lax.rem(blk + step, 8)
+        landed(small_line_in.at[there], lrecv_sem.at[heads, there])
+        total += small_line_in[there]
+    own = [
+        functools.reduce(jnp.add, slabs_in(at % heads, at // heads))
+        for at in range(GROUPS * heads)
+    ]
+    each = width // 32
+    bias = []
+    for part in range(3):
+        cut = slice(part * HD, (part + 1) * HD)
+        for pair in range(GROUPS * heads // 2):
+            both_heads = jnp.concatenate([own[2 * pair][:, cut], own[2 * pair + 1][:, cut]], axis=1)
+            lanes = slice(part * width + pair * LANES, part * width + (pair + 1) * LANES)
+            wqkv_ref[:, lanes] = both_heads[:each]
+            bias.append(both_heads[each:])
+    pairs = GROUPS * heads // 2
+    bias_q = jnp.concatenate(bias[:pairs], axis=1)
+    bias_v = jnp.concatenate(bias[2 * pairs :], axis=1)
+    bias = jnp.where(tab < 2, bias_q, bias_v)
+
+    row = lax.broadcasted_iota(jnp.int32, (width, LANES), 0)
+    lane = lax.broadcasted_iota(jnp.int32, (width, LANES), 1)
+
+    def take(block, first, count):
+        chosen = jnp.where((row == first + lane) & (lane < count), 1.0, 0.0)
+        return jnp.dot(
+            block, chosen, preferred_element_type=f32, precision=lax.Precision.HIGHEST
+        )
+
+    index = 8 * tab + blk
+    little_ref[0:8] = take(total[:8], each * index, each)
+    at_row = lax.broadcasted_iota(jnp.int32, total.shape, 0) == 6 + tab
+    wide = jnp.sum(jnp.where(at_row, total, 0.0), axis=0, keepdims=True)
+    little_ref[6:7] = take(jnp.broadcast_to(wide, (8, width)), 4 * each * blk, 4 * each)[:1]
+    little_ref[7:8] = take(bias, 2 * each * lax.rem(index, 16), 2 * each)[:1]
+
+    for step in range(1, 8):
+        context_copy(lax.rem(blk + step, 8)).wait_send()
+        small_blk(step).wait_send()
+        for head in range(heads):
+            slab_blk(head, step).wait_send()
+    for step in range(1, 4):
+        small_tab(step).wait_send()
+        for head in range(heads):
+            slab_tab(head, step).wait_send()
+
+    @pl.loop(0, UNITS)
+    def _(unit):
+        for stage in range(STAGES):
+            if stage in (1, 2):
+                both(lambda order, stage=stage: stage_copy(stage, unit, order).wait_send())
+            else:
+                stage_copy(stage, unit).wait_send()
+
+
+def attend_back(dctx, qkv, ot, lse, full_t, qkv_weight, pre, small, parts, heads):
+    width, total = full_t.shape
+    blocks = 8
+    rows = total // blocks
+    each, ff = width // 32, 4 * width
     any_space = pl.BlockSpec(memory_space=pl.ANY)
     vmem = pl.BlockSpec(memory_space=pltpu.VMEM)
     bf16, f32 = jnp.bfloat16, jnp.float32
     dma = pltpu.SemaphoreType.DMA
+    unit = parts.shape[2:]
+    parts = parts.reshape(UNITS, 2, 2, 2, 2, 2, *unit)
+    shape = jax.ShapeDtypeStruct
     return pl.pallas_call(
         functools.partial(attend_back_kernel, heads),
         name="attend_back",
         out_shape=(
-            jax.ShapeDtypeStruct((2, rows, width), bf16),
-            jax.ShapeDtypeStruct((heads, width, 3 * HD), bf16),
-            jax.ShapeDtypeStruct((8, 3 * HD), f32),
+            shape((2, rows, width), bf16),
+            shape((each, 3 * width), f32),
+            shape((each, width), f32),
+            shape((each, ff), f32),
+            shape((4 * each, width), f32),
+            shape((8, LANES), f32),
         ),
-        in_specs=[any_space] * 7,
-        out_specs=(vmem,) * 3,
+        in_specs=[any_space] * 8 + [vmem],
+        out_specs=(vmem,) * 6,
         scratch_shapes=[
             pltpu.VMEM((blocks, rows, heads * HD), bf16),
+            pltpu.VMEM((heads, total, HD), bf16),
+            pltpu.VMEM((heads, 4, 8, 2 * rows), f32),
             pltpu.VMEM((3 * heads, total, LANES), bf16),
-            pltpu.VMEM((blocks, heads * HD, rows), f32),
-            pltpu.VMEM((blocks, 8, rows), f32),
-            pltpu.VMEM((blocks, rows, width), bf16),
-            pltpu.VMEM(by_head.shape, bf16),
-            pltpu.VMEM((2, rows, width), f32),
+            pltpu.VMEM(ot.shape, f32),
+            pltpu.VMEM(lse.shape, f32),
+            pltpu.VMEM((width, total), bf16),
+            pltpu.VMEM(qkv_weight.shape, bf16),
+            pltpu.VMEM((2 * rows, width), f32),
             pltpu.VMEM((heads, LANES, total), bf16),
-            pltpu.VMEM((blocks, rows, HD), f32),
+            pltpu.VMEM((total, HD), f32),
             pltpu.VMEM((total, HD), f32),
             pltpu.VMEM((total, HD), f32),
             pltpu.VMEM((heads, blocks, rows, 3 * HD), bf16),
             pltpu.VMEM((2, GROUPS * heads, rows, 3 * HD), bf16),
+            pltpu.VMEM((rows, 3 * width), bf16),
+            pltpu.VMEM((2, 2, 2, 2, 2, *unit), bf16),
+            pltpu.VMEM((UNITS, 2, 2, 2, 2, *unit), bf16),
+            pltpu.VMEM((UNITS, 2, 2, 2, *unit), bf16),
+            pltpu.VMEM((UNITS, 2, 2, *unit), bf16),
+            pltpu.VMEM((UNITS, 2, *unit), bf16),
+            pltpu.VMEM((UNITS, *unit), bf16),
+            pltpu.VMEM((heads, 4, 8, each + 8, 3 * HD), bf16),
+            pltpu.VMEM((heads, 4, 8, each + 8, 3 * HD), bf16),
+            pltpu.VMEM((heads, 8, each + 8, 3 * HD), bf16),
+            pltpu.VMEM((heads, 8, each + 8, 3 * HD), bf16),
+            pltpu.VMEM((4, 16, width), f32),
+            pltpu.VMEM((16, width), f32),
+            pltpu.VMEM((8, 16, width), f32),
             dma((blocks,)),
             dma((blocks,)),
             dma((heads, blocks)),
             dma((2, GROUPS * heads)),
+            dma((STAGES, UNITS)),
+            dma((STAGES, UNITS)),
+            dma((heads + 1, 4)),
+            dma((heads + 1, 4)),
+            dma((heads + 1, 8)),
+            dma((heads + 1, 8)),
             dma((7,)),
             dma((heads,)),
+            dma((2,)),
         ],
         compiler_params=pltpu.CompilerParams(
-            collective_id=2, has_side_effects=True, vmem_limit_bytes=60 << 20
+            collective_id=2, has_side_effects=True, vmem_limit_bytes=62 << 20
         ),
-    )(dctx, qkv, ot, lse, full, by_head, pre)
+    )(dctx, qkv, ot, lse, full_t, qkv_weight, pre, parts, small)
+
+
+def halves(grad):
+    cut = grad.shape[2] // 2
+    return jnp.concatenate([grad[:, :, :cut], grad[:, :, cut:]], axis=1)
+
+
+def norm_parts(inputs):
+    centred = inputs - jnp.mean(inputs, axis=-1, keepdims=True)
+    inverse = lax.rsqrt(jnp.mean(centred * centred, axis=-1, keepdims=True) + EPSILON)
+    return centred * inverse, inverse
+
+
+def norm_back(grad, normed, inverse, gain):
+    e = grad * gain
+    return inverse * (
+        e
+        - jnp.mean(e, axis=-1, keepdims=True)
+        - normed * jnp.mean(e * normed, axis=-1, keepdims=True)
+    )
+
+
+def column_sum(block):
+    return jnp.sum(block.astype(jnp.float32), axis=0, keepdims=True)
+
+
+def ffn_kernel(
+    tok_ref,
+    ctx_ref,
+    cot_ref,
+    par_ref,
+    outw_ref,
+    upw_hbm,
+    downw_hbm,
+    out_ref,
+    dctx_ref,
+    pre_ref,
+    small_ref,
+    parts_ref,
+    upw,
+    downw,
+    hid,
+    hlow,
+    hlow_t,
+    norm1,
+    slopes,
+    active_t,
+    pre2,
+    gbranch,
+    ghid,
+    stage_d,
+    stage_u,
+    load_sem,
+    stage_sem,
+):
+    f32, bf16 = jnp.float32, jnp.bfloat16
+    tables, groups, rows, cols = ctx_ref.shape
+    width = tok_ref.shape[1]
+    chunks = active_t.shape[0]
+    loads = (
+        pltpu.make_async_copy(upw_hbm, upw, load_sem.at[0]),
+        pltpu.make_async_copy(downw_hbm, downw, load_sem.at[1]),
+    )
+    for copy in loads:
+        copy.start()
+
+    def par(at):
+        return par_ref[at : at + 1]
+
+    inverse1 = []
+    for table in range(tables):
+        cut = pl.ds(table * rows, rows)
+        pre1 = tok_ref[cut].astype(f32) + par(0)
+        for group in range(groups):
+            pre1 += jnp.dot(
+                ctx_ref[table, group],
+                outw_ref[group * cols : (group + 1) * cols],
+                preferred_element_type=f32,
+            )
+        normed, inverse = norm_parts(pre1)
+        inverse1.append(inverse)
+        hidden = normed * par(1) + par(2)
+        low = hidden.astype(bf16)
+        norm1[cut] = normed
+        hid[cut] = hidden
+        hlow[cut] = low
+        hlow_t[:, cut] = low.T
+
+    pre2[...] = hid[...] + par(3)
+    for copy in loads:
+        copy.wait()
+
+    @pl.loop(0, chunks)
+    def _(at):
+        cut = pl.ds(pl.multiple_of(at * width, width), width)
+        upper = jnp.dot(
+            hlow[...], upw[:, cut], preferred_element_type=f32
+        ) + par_ref[pl.ds(24 + at, 1)]
+        cdf = 0.5 + 0.5 * lax.erf(upper * math.sqrt(0.5))
+        act = (upper * cdf).astype(bf16)
+        slopes[at] = cdf + upper * jnp.exp(-0.5 * upper * upper) * (1 / math.sqrt(2 * math.pi))
+        active_t[at] = act.T
+        pre2[...] += jnp.dot(act, downw[cut], preferred_element_type=f32)
+
+    normed, inverse = norm_parts(pre2[...])
+    out_ref[...] = (normed * par(4) + par(5)).astype(bf16)
+    grad = cot_ref[...].astype(f32)
+    small_ref[4:5] = column_sum(grad * normed)
+    small_ref[5:6] = column_sum(grad)
+    gpre2 = norm_back(grad, normed, inverse, par(4))
+    ghid[...] = gpre2
+    low = gpre2.astype(bf16)
+    gbranch[...] = low
+    small_ref[3:4] = column_sum(low)
+
+    each = width // 32
+
+    def down_copies(at):
+        return [
+            pltpu.make_async_copy(
+                stage_d.at[part],
+                parts_ref.at[part, pl.ds(8 * at, 8)],
+                stage_sem.at[part],
+            )
+            for part in range(4)
+        ]
+
+    def up_copy(at):
+        return pltpu.make_async_copy(stage_u, parts_ref.at[4 + at], stage_sem.at[4])
+
+    @pl.loop(0, chunks)
+    def _(at):
+        cut = pl.ds(pl.multiple_of(at * width, width), width)
+        wdown = jnp.dot(active_t[at], gbranch[...], preferred_element_type=f32)
+        wdown = wdown.reshape(8, 4, each, width)
+
+        @pl.when(at > 0)
+        def _():
+            for copy in down_copies(at - 1):
+                copy.wait()
+            up_copy(at - 1).wait()
+
+        for part in range(4):
+            stage_d[part] = halves(wdown[:, part]).astype(bf16)
+        for copy in down_copies(at):
+            copy.start()
+        gact = times_t(gbranch[...], downw[cut])
+        gup = (gact * slopes[at]).astype(bf16)
+        small_ref[pl.ds(6 + at, 1)] = column_sum(gup)
+        ghid[...] += times_t(gup, upw[:, cut])
+        wup = jnp.dot(hlow_t[...], gup, preferred_element_type=f32)
+        stage_u[...] = halves(wup.reshape(32, each, width)).astype(bf16)
+        up_copy(at).start()
+
+    for copy in down_copies(chunks - 1):
+        copy.wait()
+    up_copy(chunks - 1).wait()
+    small = [0.0, 0.0, 0.0]
+    lows = []
+    for table in range(tables):
+        cut = pl.ds(table * rows, rows)
+        grad, normed = ghid[cut], norm1[cut]
+        small[1] += column_sum(grad * normed)
+        small[2] += column_sum(grad)
+        gpre1 = norm_back(grad, normed, inverse1[table], par(1))
+        pre_ref[cut] = gpre1
+        low = gpre1.astype(bf16)
+        small[0] += column_sum(low)
+        lows.append(low)
+        for group in range(groups):
+            dctx_ref[table, group] = times_t(
+                low, outw_ref[group * cols : (group + 1) * cols]
+            ).astype(bf16)
+    for at in range(3):
+        small_ref[at : at + 1] = small[at]
+    small_ref[10:] = jnp.zeros((6, width), f32)
+    for group in range(groups):
+        wout = 0.0
+        for table in range(tables):
+            wout += jnp.dot(ctx_ref[table, group].T, lows[table], preferred_element_type=f32)
+        stage_u[group * 8 : (group + 1) * 8] = halves(wout.reshape(8, each, width)).astype(bf16)
+    last = pltpu.make_async_copy(stage_u, parts_ref.at[8], stage_sem.at[4])
+    last.start()
+    last.wait()
+
+
+def ffn(tokens, ctx, cotangent, params, out_weight, up_weight, down_weight):
+    total, width = tokens.shape
+    chunks = up_weight.shape[1] // width
+    each = width // 32
+    any_space = pl.BlockSpec(memory_space=pl.ANY)
+    vmem = pl.BlockSpec(memory_space=pltpu.VMEM)
+    bf16, f32 = jnp.bfloat16, jnp.float32
+    flops = 18 * total * width * chunks * width + 6 * total * width * width
+    return pl.pallas_call(
+        ffn_kernel,
+        name="ffn",
+        out_shape=(
+            jax.ShapeDtypeStruct((total, width), bf16),
+            jax.ShapeDtypeStruct(ctx.shape, bf16),
+            jax.ShapeDtypeStruct((total, width), f32),
+            jax.ShapeDtypeStruct((16, width), f32),
+            jax.ShapeDtypeStruct((9, 32, 2 * each, width // 2), bf16),
+        ),
+        in_specs=[vmem, vmem, vmem, vmem, vmem, any_space, any_space],
+        out_specs=(vmem, vmem, vmem, vmem, any_space),
+        scratch_shapes=[
+            pltpu.VMEM(up_weight.shape, bf16),
+            pltpu.VMEM(down_weight.shape, bf16),
+            pltpu.VMEM((total, width), f32),
+            pltpu.VMEM((total, width), bf16),
+            pltpu.VMEM((width, total), bf16),
+            pltpu.VMEM((total, width), f32),
+            pltpu.VMEM((chunks, total, width), f32),
+            pltpu.VMEM((chunks, width, total), bf16),
+            pltpu.VMEM((total, width), f32),
+            pltpu.VMEM((total, width), bf16),
+            pltpu.VMEM((total, width), f32),
+            pltpu.VMEM((4, 8, 2 * each, width // 2), bf16),
+            pltpu.VMEM((32, 2 * each, width // 2), bf16),
+            pltpu.SemaphoreType.DMA((2,)),
+            pltpu.SemaphoreType.DMA((5,)),
+        ],
+        compiler_params=pltpu.CompilerParams(vmem_limit_bytes=60 << 20),
+        cost_estimate=pl.CostEstimate(
+            flops=flops, bytes_accessed=40 << 20, transcendentals=total * width * chunks
+        ),
+    )(tokens, ctx, cotangent, params, out_weight, up_weight, down_weight)
 
 
 def scatter_sum(grad):
@@ -859,127 +1472,50 @@
     cotangent,
 ):
     tables, rows, width = tokens.shape
-    f32, bf16 = jnp.float32, jnp.bfloat16
-    all_heads = width // HD
-    heads = all_heads // GROUPS
-    blk = lax.axis_index("blk")
-    group = blk % GROUPS
+    f32 = jnp.float32
+    heads = width // HD // GROUPS
     flat_tokens = tokens.reshape(tables * rows, width)
-
-    by_group = qkv_weight.reshape(width, 3, GROUPS, heads, HD)
-    own = lax.dynamic_index_in_dim(by_group, group, 2, keepdims=False)
-    own_weight = jnp.pad(own, ((0, 0), (0, 0), (0, 0), (0, LANES - HD))).reshape(width, -1)
-    bias_full = jnp.concatenate(
+    six = jnp.stack([out_bias, attn_gain, attn_shift, down_bias, ffn_gain, ffn_shift])
+    params = jnp.concatenate(
         [
-            qkv_bias[:width].astype(f32),
-            jnp.zeros((width,), f32),
-            qkv_bias[width:].astype(f32),
+            six,
+            jnp.zeros((2, width), six.dtype),
+            jnp.broadcast_to(qkv_bias[None, :width], (8, width)),
+            jnp.broadcast_to(qkv_bias[None, width:], (8, width)),
+            up_bias.reshape(-1, width),
+            jnp.zeros((4, width), six.dtype),
         ]
-    ).reshape(3, GROUPS, heads, HD)
-    own_bias = jnp.pad(
-        lax.dynamic_index_in_dim(bias_full, group, 1, keepdims=False),
-        ((0, 0), (0, 0), (0, LANES - HD)),
-    )
-    ones = jnp.zeros((3, 1, LANES), f32).at[0::2, :, HD].set(1.0)
-    own_bias = (own_bias + ones).reshape(1, -1)
-    by_head = (
-        qkv_weight.reshape(width, 3, all_heads, HD)
-        .transpose(2, 0, 1, 3)
-        .reshape(all_heads, width, 3 * HD)
-    )
-
-    ctx, full, qkv, ot, lse = attend(tokens, lengths, own_weight, own_bias, heads)
-
-    context_low = ctx.transpose(0, 2, 1, 3).reshape(tables * rows, width)
-    attended = jnp.dot(context_low, out_weight, preferred_element_type=f32) + out_bias.astype(
-        f32
-    )
-    pre_one = flat_tokens.astype(f32) + attended
-    gain_one = attn_gain.astype(f32)
-    shift_one = attn_shift.astype(f32)
-    hidden = norm_rows(pre_one, gain_one, shift_one)
-    hidden_low = hidden.astype(bf16)
-    upper = jnp.dot(hidden_low, up_weight, preferred_element_type=f32) + up_bias.astype(f32)
-    active = gelu_exact(upper).astype(bf16)
-    pre_two = (
-        hidden
-        + jnp.dot(active, down_weight, preferred_element_type=f32)
-        + down_bias.astype(f32)
-    )
-    gain_two = ffn_gain.astype(f32)
-    shift_two = ffn_shift.astype(f32)
-    layer_out = norm_rows(pre_two, gain_two, shift_two).astype(bf16).reshape(tokens.shape)
-    grad_out = cotangent.reshape(tables * rows, width).astype(f32)
-    _, norm_two_back = jax.vjp(norm_rows, pre_two, gain_two, shift_two)
-    grad_pre_two, ggrad_ffn, sgrad_ffn = norm_two_back(grad_out)
-    grad_branch = grad_pre_two.astype(bf16)
-    wgrad_down = over_rows(active, grad_branch)
-    bgrad_down = jnp.sum(grad_branch, axis=0, dtype=f32)
-    grad_active = times_back(grad_branch, down_weight)
-    _, gelu_back = jax.vjp(gelu_exact, upper)
-    grad_upper = gelu_back(grad_active)[0].astype(bf16)
-    wgrad_up = over_rows(hidden_low, grad_upper)
-    bgrad_up = jnp.sum(grad_upper, axis=0, dtype=f32)
-    grad_hidden = grad_pre_two + times_back(grad_upper, up_weight)
-    _, norm_one_back = jax.vjp(norm_rows, pre_one, gain_one, shift_one)
-    grad_pre_one, ggrad_attn, sgrad_attn = norm_one_back(grad_hidden)
-    grad_attended = grad_pre_one.astype(bf16)
-    wgrad_out = over_rows(context_low, grad_attended)
-    bgrad_out = jnp.sum(grad_attended, axis=0, dtype=f32)
-    grad_context = times_back(grad_attended, out_weight).astype(bf16)
-    dctx = grad_context.reshape(tables, rows, GROUPS, heads * HD).transpose(0, 2, 1, 3)
-
-    token_grad, wgrad_part, sums = attend_back(
-        dctx, qkv, ot, lse, full, by_head, grad_pre_one.reshape(tokens.shape), heads
-    )
-
-    part = lax.psum_scatter(
-        wgrad_part.transpose(1, 0, 2), "tab", scatter_dimension=0, tiled=True
-    )
-    part = lax.all_to_all(
-        part.reshape(8, -1, heads, 3 * HD), "blk", split_axis=0, concat_axis=0, tiled=True
-    )
-    part = part.reshape(2, GROUPS, -1, heads, 3, HD).astype(f32).sum(axis=0)
-    wgrad_qkv = part.transpose(1, 3, 0, 2, 4).reshape(-1, 3 * width)
-
-    sums = sums[:heads].reshape(heads, 3, HD)[:, 0::2].transpose(1, 0, 2)
-    placed = jnp.zeros((2, GROUPS, heads, HD), f32)
-    placed = lax.dynamic_update_slice(placed, sums[:, None], (0, group, 0, 0)).reshape(-1)
-    small = (placed, bgrad_out, ggrad_attn, sgrad_attn, bgrad_up, bgrad_down, ggrad_ffn, sgrad_ffn)
-    small = jnp.concatenate([s.reshape(32, -1) for s in small], axis=1).astype(f32)
-    small = lax.psum_scatter(
-        small.reshape(4, -1), "tab", scatter_dimension=0, tiled=True
-    ).reshape(8, -1)
-    small = lax.psum_scatter(small, "blk", scatter_dimension=0, tiled=True).reshape(-1)
+    ).astype(f32)
+
+    ctx, full_t, qkv, ot, lse = attend(tokens, lengths, params, qkv_weight, heads)
+    layer_out, dctx, pre, small, parts = ffn(
+        flat_tokens,
+        ctx,
+        cotangent.reshape(tables * rows, width),
+        params,
+        out_weight,
+        up_weight,
+        down_weight,
+    )
+    token_grad, wgrad_qkv, wgrad_out, wgrad_up, wgrad_down, little = attend_back(
+        dctx, qkv, ot, lse, full_t, qkv_weight, pre, small, parts, heads
+    )
     each = width // 32
-    cuts = [2 * each, 3 * each, 4 * each, 5 * each]
-    cuts += [cuts[-1] + up_bias.shape[0] // 32]
-    cuts += [cuts[-1] + each, cuts[-1] + 2 * each]
-    (
-        bgrad_qkv,
-        bgrad_out,
-        ggrad_attn,
-        sgrad_attn,
-        bgrad_up,
-        bgrad_down,
-        ggrad_ffn,
-        sgrad_ffn,
-    ) = jnp.split(small, cuts)
     return (
-        layer_out,
+        layer_out.reshape(tokens.shape),
         token_grad,
         wgrad_qkv,
-        bgrad_qkv,
-        scatter_sum(wgrad_out),
-        bgrad_out,
-        ggrad_attn,
-        sgrad_attn,
-        scatter_sum(wgrad_up),
-        bgrad_up,
-        scatter_sum(wgrad_down),
-        bgrad_down,
-        ggrad_ffn,
-        sgrad_ffn,
+        little[7, : 2 * each],
+        wgrad_out,
+        little[0, :each],
+        little[1, :each],
+        little[2, :each],
+        wgrad_up,
+        little[6, : 4 * each],
+        wgrad_down,
+        little[3, :each],
+        little[4, :each],
+        little[5, :each],
     )
 
 

time: 446 us -> 269 us (0.60); the launches traced: 437 us -> 268 us
  waiting for transfers between devices: 85.2 us -> 0 us
  Pallas kernels: 181 us -> 249 us
  matrix products: 57.4 us -> 0 us
  blocking collectives: 42 us -> 0 us
  local copies, waits for them, and re-layouts: 40.3 us -> 18.1 us
  between operations: 15 us -> 0.68 us
  other arithmetic: 11.8 us -> 0.65 us
  starting transfers between devices: 4.89 us -> 0 us
    reduce_scatter x7 -> x0, waiting for transfers between devices: 84.1 us -> none  [the longest x3 39.3 us: scatter_sum(): lax.psum_scatter(lax.psum_scatter(grad.astype(jnp.bfloat16), 'tab', scatt...]
    dot_general x9 -> x0, matrix products: 57.4 us -> none  [the longest x1 20.1 us: shards_direct(): jnp.dot(hidden_low, up_weight, preferred_element_type=f32)]
    unnamed x2 -> x0, blocking collectives: 42 us -> none
    pallas_call x1, Pallas kernels: 102 us -> 139 us  [attend_back(): pl.pallas_call(functools.partial(attend_back_kernel, heads), name='attend...]
    pallas_call x0 -> x1, Pallas kernels: none -> 35.9 us  [ffn(): pl.pallas_call(ffn_kernel, name='ffn', out_shape=(jax.ShapeDtypeStruct((t...]
    reshape x17 -> x1, local copies, waits for them, and re-layouts: 16.6 us -> 0.7 us  [shards_direct(): up_bias.reshape(-1, width)]
    transpose x3 -> x0, local copies, waits for them, and re-layouts: 7.17 us -> none  [the longest x1 4.39 us: shards_direct(): by_head = qkv_weight.reshape(width, 3, all_heads, HD).transpose(2, 0, 1,...]
    convert_element_type x11 -> x1, other arithmetic: 6.85 us -> 0.65 us  [shards_direct(): params = jnp.concatenate([six, jnp.zeros((2, width), six.dtype), jnp.broa...]
  transfers between devices with their start and end apart: 8 -> 0, of which waited for: 4 -> 0; matrix products, arithmetic and copies ran while one was open for 10% -> 0% of each run, Pallas kernels for 23% -> 0%
where the time goes in v2:
time: 269 us; the launch traced here: 268 us
  Pallas kernels  249 us (93%)
  local copies, waits for them, and re-layouts  18.1 us (7%)
    pallas_call x1, Pallas kernels, attend_back(): pl.pallas_call(functools.partial(attend_back_kernel, heads), name='attend...  139 us
    pallas_call x1, Pallas kernels, attend(): pl.pallas_call(functools.partial(attend_kernel, heads), name='attend', ou...  73.7 us
    pallas_call x1, Pallas kernels, ffn(): pl.pallas_call(ffn_kernel, name='ffn', out_shape=(jax.ShapeDtypeStruct((t...  35.9 us
    unnamed x5, local copies, waits for them, and re-layouts  8.6 us

profile of v2, /device:TPU:0, one launch (start us, length us, event | category | flops | bytes accessed | tf_op | source)
XLA Modules:
  0.0 268.2 jit_solution(5146224108779430883)
XLA Ops:
  0.6 0.7 stack.18
  1.3 0.7 stack.19
  2.0 0.7 stack.20
  2.7 0.7 stack.21
  3.4 0.7 stack.22
  4.1 0.7 stack.23
  4.8 0.8 fusion
  5.5 0.7 reshape.46
  6.2 0.1 concatenate.3
  6.3 0.7 convert_element_type.3.par_ref
  7.0 73.7 %attend.1 = (bf16[2,4,256,192]{3,2,1,0:T(8,128)(2,1)}, bf16[768,2048]{1,0:T(8,128)(2,1)}, bf16[9,2048,128]{2,1,0:T(8,128)(2,1)}, f32[4,192,512]{2,1,0:T(8,128)}, f32[4,8,512]{2,1,0:T(8,128)}) custom-call(bf16[2,256,768]{2,1,0:T(8,128)(2,1)} %tok_ref.1, s32[2]{0:T(128)} %len_ref.1, f32[32,768]{1,0:T(8,128)} %convert_element_type.3.par_ref, ...), custom_call_target="tpu_custom_call" | custom-call | tf_op jit(solution)/shard_map/attend/pallas_call | solution.py:601
  80.7 35.9 %ffn.1 = (bf16[512,768]{1,0:T(8,128)(2,1)}, bf16[2,4,256,192]{3,2,1,0:T(8,128)(2,1)}, f32[512,768]{1,0:T(8,128)}, f32[16,768]{1,0:T(8,128)}, bf16[9,32,48,384]{3,2,1,0:T(8,128)(2,1)}) custom-call(bf16[512,768]{1,0:T(8,128)(2,1)} %bitcast.21, bf16[2,4,256,192]{3,2,1,0:T(8,128)(2,1)} %get-tuple-element.30.ctx_ref, bf16[512,768]{1,0:T(8,128)(2,1)} %bitcast.22, ...), custom_call_target="tpu_custom_call" | custom-call | flops 23555211264 | bytes 41943040 | tf_op jit(solution)/shard_map/ffn/pallas_call | solution.py:1410
  116.6 139.2 %attend_back.1 = (bf16[2,256,768]{2,1,0:T(8,128)(2,1)}, f32[24,2304]{1,0:T(8,128)}, f32[24,768]{1,0:T(8,128)}, f32[24,3072]{1,0:T(8,128)}, f32[96,768]{1,0:T(8,128)}, /*index=5*/f32[8,128]{1,0:T(8,128)}) custom-call(bf16[2,4,256,192]{3,2,1,0:T(8,128)(2,1)} %get-tuple-element.32.dctx_ref, bf16[9,2048,128]{2,1,0:T(8,128)(2,1)} %get-tuple-element.33.qkv_ref, ...), custom_call_target="tpu_custom_call" | custom-call | tf_op jit(solution)/shard_map/attend_back/pallas_call | solution.py:1155
  255.8 1.2 slice_bitcast_fusion.7
  257.0 1.4 slice_bitcast_fusion
  258.4 1.2 slice_bitcast_fusion.3
  259.6 2.1 copy.34
  261.7 1.6 copy.35
  263.3 1.5 copy.36
  264.8 1.7 copy.37
  266.5 1.7 copy.38
  (4 shorter events, 0.0 us)

commit v3 on v2

--- a/solution.py
+++ b/solution.py
@@ -332,7 +332,6 @@
 LANES = 128
 LOG2E = math.log2(math.e)
 MESH = pl.DeviceIdType.MESH
-CHUNKS = 2
 
 
 def times_t(left, right):
@@ -356,6 +355,16 @@
         )
 
     pl.semaphore_wait(barrier, 7)
+
+
+def fold(block):
+    cut = block.shape[0] // 2
+    return jnp.concatenate([block[:cut], block[cut:]], axis=1)
+
+
+def unfold(block):
+    cut = block.shape[1] // 2
+    return jnp.concatenate([block[:, :cut], block[:, cut:]], axis=0)
 
 
 def own_window(group, first, rows_ref, out):
@@ -379,9 +388,11 @@
     qkv_ref,
     ot_ref,
     lse_ref,
+    wr_ref,
     tokv,
     toktv,
     wfull,
+    wrv,
     wown,
     bown,
     qkvv,
@@ -389,11 +400,7 @@
     otv,
     lsev,
     csend,
-    send_a,
-    send_b,
-    send_c,
-    send_d,
-    send_e,
+    send_sem,
     recv,
     csend_sem,
     crecv_sem,
@@ -404,7 +411,6 @@
     group = 2 * lax.rem(chip, 2) + core
     rows = tok_ref.shape[1]
     width = tok_ref.shape[2]
-    piece = rows // CHUNKS
     is_near = jnp.logical_or(chip == 1, chip == 2)
     mate = chip + 1 - 2 * lax.rem(chip, 2)
     other_near = 2 - half
@@ -422,36 +428,30 @@
             device_id_type=MESH,
         )
 
-    def own_copies(part):
-        cut = pl.ds(part * piece, piece)
-        here, there = tok_ref.at[half, cut], tok_ref.at[1 - half, cut]
-        dst, done = tokv.at[blk, cut], recv.at[blk, part]
-        return (
-            remote(here, dst, send_a.at[part], done, mate, core),
-            remote(there, dst, send_c.at[part], done, other_near, core),
-            remote(here, dst, send_b.at[part], done, chip, 1 - core),
-        )
-
-    def to_far(slot, part, src_chip):
+    here, there = tok_ref.at[half], tok_ref.at[1 - half]
+    to_mate = remote(here, tokv.at[blk], send_sem.at[0], recv.at[blk], mate, core)
+    to_other = remote(there, tokv.at[blk], send_sem.at[1], recv.at[blk], other_near, core)
+    to_side = remote(here, tokv.at[blk], send_sem.at[2], recv.at[blk], chip, 1 - core)
+
+    def to_far(slot, src_chip):
         which = 2 * src_chip + core
-        ref = tokv.at[which, pl.ds(part * piece, piece)]
-        return remote(ref, ref, send_d.at[slot, part], recv.at[which, part], own_far, core)
-
-    def to_core(slot, part, src_chip):
+        ref = tokv.at[which]
+        return remote(ref, ref, send_sem.at[2 + slot], recv.at[which], own_far, core)
+
+    def to_core(slot, src_chip):
         which = 2 * src_chip + core
-        ref = tokv.at[which, pl.ds(part * piece, piece)]
-        return remote(ref, ref, send_e.at[slot, part], recv.at[which, part], chip, 1 - core)
-
-    def arrived(which, part):
-        ref = tokv.at[which, pl.ds(part * piece, piece)]
-        pltpu.make_async_copy(ref, ref, recv.at[which, part]).wait()
+        ref = tokv.at[which]
+        return remote(ref, ref, send_sem.at[5 + slot], recv.at[which], chip, 1 - core)
+
+    def arrived(which):
+        pltpu.make_async_copy(tokv.at[which], tokv.at[which], recv.at[which]).wait()
 
     load = pltpu.make_async_copy(w_hbm, wfull, local_sem.at[5])
     load.start()
     meet(tab, blk)
-    for part in range(CHUNKS):
-        for copy in own_copies(part):
-            copy.start()
+    pl.when(is_near)(to_other.start)
+    to_mate.start()
+    to_side.start()
     tokv[blk] = tok_ref[half]
 
     lane1 = lax.broadcasted_iota(jnp.int32, (8, LANES), 1)
@@ -492,30 +492,43 @@
         toktv[:, pl.ds(first, rows)] = tok.T
 
     project(blk)
-    for part in range(CHUNKS):
-        arrived(2 * mate + core, part)
-        to_core(0, part, mate).start()
+
+    def half_lanes(part, at):
+        first = part * width + LANES * (at // 2)
+        return wfull[:, first : first + LANES][:, HD * (at % 2) :][:, :HD]
+
+    for head in range(heads):
+        for part in range(3):
+            for pair in range(GROUPS // 2):
+                at = 2 * pair * heads + head
+                wrv[head, :, pl.ds((2 * part + pair) * LANES, LANES)] = jnp.concatenate(
+                    [half_lanes(part, at), half_lanes(part, at + heads)], axis=1
+                )
+    arrived(2 * mate + core)
+    to_core(0, mate).start()
+
+    @pl.when(jnp.logical_not(is_near))
+    def _():
+        to_mate.wait_send()
+        to_other.start()
+
     project(2 * mate + core)
-    for part in range(CHUNKS):
-        arrived(2 * chip + 1 - core, part)
+    arrived(2 * chip + 1 - core)
     project(2 * chip + 1 - core)
-    for part in range(CHUNKS):
-        arrived(2 * mate + 1 - core, part)
+    arrived(2 * mate + 1 - core)
     project(2 * mate + 1 - core)
-    for part in range(CHUNKS):
-        for slot, src_chip in ((1, other_near), (2, other_far)):
-            arrived(2 * src_chip + core, part)
-            pl.when(is_near)(to_far(slot, part, src_chip).start)
-            to_core(slot, part, src_chip).start()
-    for src_chip in (other_near, other_far):
+    for slot, src_chip in ((1, other_near), (2, other_far)):
+        arrived(2 * src_chip + core)
+        pl.when(is_near)(to_far(slot, src_chip).start)
+        to_core(slot, src_chip).start()
         project(2 * src_chip + core)
-        for part in range(CHUNKS):
-            arrived(2 * src_chip + 1 - core, part)
+        arrived(2 * src_chip + 1 - core)
         project(2 * src_chip + 1 - core)
 
     keep = (
         pltpu.make_async_copy(toktv, fullt_ref, local_sem.at[0]),
         pltpu.make_async_copy(qkvv, qkv_ref, local_sem.at[1]),
+        pltpu.make_async_copy(wrv, wr_ref, local_sem.at[6]),
     )
     for copy in keep:
         copy.start()
@@ -548,8 +561,8 @@
             otv[which, head * HD : (head + 1) * HD] = ot[:HD] / total
             lsev[which, head : head + 1] = peak * scale + jnp.log(total) * LOG2E
         out = otv[which].T.astype(jnp.bfloat16)
-        csend[2 * which] = out[:rows]
-        csend[2 * which + 1] = out[rows:]
+        for side in range(2):
+            csend[2 * which + side] = fold(out[side * rows : (side + 1) * rows])
 
         @pl.when(step < 3)
         def _():
@@ -567,13 +580,13 @@
     )
     for copy in more:
         copy.start()
-    for part in range(CHUNKS):
-        for copy in own_copies(part):
-            copy.wait_send()
-        to_core(0, part, mate).wait_send()
-        for slot, src_chip in ((1, other_near), (2, other_far)):
-            pl.when(is_near)(to_far(slot, part, src_chip).wait_send)
-            to_core(slot, part, src_chip).wait_send()
+    pl.when(is_near)(to_mate.wait_send)
+    to_other.wait_send()
+    to_side.wait_send()
+    to_core(0, mate).wait_send()
+    for slot, src_chip in ((1, other_near), (2, other_far)):
+        pl.when(is_near)(to_far(slot, src_chip).wait_send)
+        to_core(slot, src_chip).wait_send()
 
     @pl.loop(1, 8)
     def _(step):
@@ -602,34 +615,32 @@
         functools.partial(attend_kernel, heads),
         name="attend",
         out_shape=(
-            jax.ShapeDtypeStruct((tables, GROUPS, rows, heads * HD), bf16),
+            jax.ShapeDtypeStruct((tables, GROUPS, rows // 2, 2 * heads * HD), bf16),
             jax.ShapeDtypeStruct((width, total), bf16),
             jax.ShapeDtypeStruct((3 * heads, total, LANES), bf16),
             jax.ShapeDtypeStruct((4, heads * HD, 2 * rows), f32),
             jax.ShapeDtypeStruct((4, 8, 2 * rows), f32),
+            jax.ShapeDtypeStruct((heads, width, width), bf16),
         ),
         in_specs=[vmem, pl.BlockSpec(memory_space=pltpu.SMEM), vmem, any_space],
-        out_specs=(any_space,) * 5,
+        out_specs=(any_space,) * 6,
         scratch_shapes=[
             pltpu.VMEM((blocks, rows, width), bf16),
             pltpu.VMEM((width, total), bf16),
             pltpu.VMEM(qkv_weight.shape, bf16),
+            pltpu.VMEM((heads, width, width), bf16),
             pltpu.VMEM((width, 3 * heads * LANES), bf16),
             pltpu.VMEM((8, 3 * heads * LANES), f32),
             pltpu.VMEM((3 * heads, total, LANES), bf16),
             pltpu.VMEM((heads, LANES, total), bf16),
             pltpu.VMEM((4, heads * HD, 2 * rows), f32),
             pltpu.VMEM((4, 8, 2 * rows), f32),
-            pltpu.VMEM((blocks, rows, heads * HD), bf16),
-            dma((CHUNKS,)),
-            dma((CHUNKS,)),
-            dma((CHUNKS,)),
-            dma((3, CHUNKS)),
-            dma((3, CHUNKS)),
-            dma((blocks, CHUNKS)),
+            pltpu.VMEM((blocks, rows // 2, 2 * heads * HD), bf16),
+            dma((8,)),
             dma((blocks,)),
             dma((blocks,)),
-            dma((6,)),
+            dma((blocks,)),
+            dma((7,)),
         ],
         compiler_params=pltpu.CompilerParams(
             collective_id=1, has_side_effects=True, vmem_limit_bytes=60 << 20
@@ -640,7 +651,7 @@
 UNITS = 9
 TURNS = 4
 STAGES = 5
-PHASE = (1, 3, 5, 7, 9)
+PHASE = (2, 5, 7, 9, 11)
 
 
 def attend_back_kernel(
@@ -674,8 +685,14 @@
     dkv,
     dvv,
     dqkv,
-    arrive,
+    qsend,
+    kvsend,
+    arrive_q,
+    arrive_kv,
     joined,
+    xacc,
+    xsend,
+    back,
     mine,
     sum0,
     sum1,
@@ -693,6 +710,8 @@
     drecv_sem,
     gsend_sem,
     grecv_sem,
+    xsend_sem,
+    xrecv_sem,
     ssend_sem,
     srecv_sem,
     tsend_sem,
@@ -700,7 +719,6 @@
     lsend_sem,
     lrecv_sem,
     local_sem,
-    own_sem,
     mine_sem,
 ):
     f32, bf16 = jnp.float32, jnp.bfloat16
@@ -708,7 +726,7 @@
     y, x, zh, zl = tab // 2, lax.rem(tab, 2), chip // 2, lax.rem(chip, 2)
     half = zh
     group = 2 * zl + core
-    blocks, rows = dov.shape[0], dov.shape[1]
+    blocks, rows = dov.shape[0], 2 * dov.shape[1]
     width = toktv.shape[0]
     tile = 2 * rows
     piece = 256
@@ -765,11 +783,18 @@
             (tab, which),
         )
 
-    for step in range(1, 8):
-        which = 2 * lax.rem(chip + 4 - step // 2, 4) + (
-            (1 - core) if step == 1 else (core if step % 2 == 0 else 1 - core)
-        )
-        context_copy(which).start()
+    def chip_at(step):
+        mate = 2 * half + 1 - zl
+        return jnp.where(
+            step < 2,
+            jnp.where(step == 0, chip, mate),
+            jnp.where(step == 2, 2 - half, 3 - 3 * half),
+        )
+
+    context_copy(2 * chip + 1 - core).start()
+    for step in range(1, 4):
+        for side in (core, 1 - core):
+            context_copy(2 * chip_at(step) + side).start()
 
     def stage_copy(stage, unit, order=None):
         send, done = ssend_sem.at[stage, unit], srecv_sem.at[stage, unit]
@@ -871,9 +896,8 @@
 
     def tick(now):
         for stage in range(STAGES):
-            at = now - PHASE[stage]
-            unit = (5 * at + 6) // 7
-            due = (at >= 0) & (unit < UNITS) & ((7 * unit) // 5 == at)
+            unit = now - PHASE[stage]
+            due = (unit >= 0) & (unit < UNITS)
             pl.when(due)(functools.partial(advance, stage, unit))
 
     for unit in range(UNITS):
@@ -923,7 +947,7 @@
             small_blk(step).start()
 
     def make_slab(head):
-        flat = dqkv[head].reshape(blocks * rows, 3 * HD)
+        flat = dqkv[head]
         grad = jnp.dot(toktv[...], flat, preferred_element_type=f32)
         sums = jnp.sum(flat.astype(f32), axis=0, keepdims=True)
         sums = jnp.broadcast_to(sums, (8, 3 * HD))
@@ -950,24 +974,64 @@
     for head in range(heads):
         ktv[head] = qkvv[heads + head].T
 
-    def gradient_copy(head, which):
-        return remote(
-            dqkv.at[head, which],
-            arrive.at[half, group * heads + head],
-            gsend_sem.at[head, which],
-            grecv_sem.at[half, group * heads + head],
-            (tab, which),
-        )
-
-    def own_gradient(head):
-        return pltpu.make_async_copy(
-            dqkv.at[head, blk], arrive.at[half, group * heads + head], own_sem.at[head]
-        )
+    def gradient_copies(head, which, own):
+        slot = group * heads + head
+        pairs = (
+            (qsend.at[head, which], arrive_q.at[slot]),
+            (kvsend.at[head, which], arrive_kv.at[slot]),
+        )
+        for kind, (src, dst) in enumerate(pairs):
+            if own:
+                yield pltpu.make_async_copy(src, dst, grecv_sem.at[kind, slot])
+            else:
+                yield remote(
+                    src,
+                    dst,
+                    gsend_sem.at[kind, head, which],
+                    grecv_sem.at[kind, slot],
+                    (tab, 4 * half + which),
+                )
+
+    def send_gradient(kind, head, which):
+        @pl.when(which == group)
+        def _():
+            list(gradient_copies(head, which, True))[kind].start()
+
+        @pl.when(which != group)
+        def _():
+            list(gradient_copies(head, which, False))[kind].start()
+
+    def absorb(head):
+        for at in range(GROUPS):
+            slot = at * heads + head
+            landed(arrive_q.at[slot], grecv_sem.at[0, slot])
+            landed(arrive_kv.at[slot], grecv_sem.at[1, slot])
+        for pair in range(GROUPS // 2):
+            left, right = 2 * pair * heads + head, (2 * pair + 1) * heads + head
+            lanes = slice(pair * LANES, (pair + 1) * LANES)
+            for side in range(2):
+                cut = slice(side * HD, (side + 1) * HD)
+                joined[side * rows : (side + 1) * rows, lanes] = jnp.concatenate(
+                    [arrive_q[left][:, cut], arrive_q[right][:, cut]], axis=1
+                )
+                lanes_kv = slice((2 * side + 2 + pair) * LANES, (2 * side + 3 + pair) * LANES)
+                joined[:, lanes_kv] = jnp.concatenate(
+                    [arrive_kv[left][:, cut], arrive_kv[right][:, cut]], axis=1
+                )
+
+    def give_back(side, own):
+        src, dst = xsend.at[side], back.at[half]
+        if own:
+            return pltpu.make_async_copy(src, dst, xrecv_sem.at[half])
+        return remote(src, dst, xsend_sem.at[side], xrecv_sem.at[half], (tab, 2 * group + side))
+
+    def is_own(side):
+        return jnp.logical_and(chip == group, core == side)
 
     @pl.loop(0, heads * TURNS)
     def _(turn):
         head, step = turn // TURNS, lax.rem(turn, TURNS)
-        which = lax.rem(chip + step, 4)
+        which = chip_at(step)
         first = pl.multiple_of(which * tile, tile)
 
         @pl.when(head == 0)
@@ -979,8 +1043,9 @@
                 def _():
                     landed(dov.at[block], drecv_sem.at[block])
 
+                dos = unfold(dov[block])
                 for at in range(heads):
-                    do = dov[block][:, at * HD : (at + 1) * HD]
+                    do = dos[:, at * HD : (at + 1) * HD]
                     doh[at, pl.ds(first + side * rows, rows)] = do
                     ot = otv[which, at * HD : (at + 1) * HD, side * rows : (side + 1) * rows]
                     deltas[at, which, :1, side * rows : (side + 1) * rows] = jnp.sum(
@@ -1009,71 +1074,48 @@
             dvv[cut] += jnp.dot(pt.astype(bf16), do, preferred_element_type=f32)
             dkv[cut] += jnp.dot(dst, q, preferred_element_type=f32)
             dqt += jnp.dot(ktv[head, :, cut], dst, preferred_element_type=f32)
-        dqv[pl.ds(first, tile)] = dqt[:HD].T * shrink
+        dq = (dqt[:HD].T * shrink).astype(bf16)
+        dqv[pl.ds(first, tile)] = dq
+        qsend[head, which] = jnp.concatenate([dq[:rows], dq[rows:]], axis=1)
+        send_gradient(0, head, which)
 
         @pl.when(step == TURNS - 1)
         def _():
-            @pl.loop(0, 8)
+            @pl.loop(0, 4)
             def _(at):
-                block = lax.rem(blk + 1 + at, 8)
-                cut = pl.ds(pl.multiple_of(block * rows, rows), rows)
-                dqkv[head, block] = jnp.concatenate(
-                    [dqv[cut], dkv[cut] * shrink, dvv[cut]], axis=1
-                ).astype(bf16)
-
-                @pl.when(at < 7)
-                def _():
-                    gradient_copy(head, block).start()
-
-                @pl.when(at == 7)
-                def _():
-                    own_gradient(head).start()
-
-        @pl.when(jnp.logical_and(head > 0, step == 0))
+                there = lax.rem(group + 1 + at, 4)
+                cut = pl.ds(pl.multiple_of(there * tile, tile), tile)
+                pair = jnp.concatenate([dkv[cut] * shrink, dvv[cut]], axis=1).astype(bf16)
+                kvsend[head, there] = pair
+                send_gradient(1, head, there)
+                dqkv[head, cut] = jnp.concatenate([pair, dqv[cut]], axis=1)
+
+        @pl.when(turn == TURNS)
         def _():
-            @pl.when(head == 1)
-            def _():
-                loads[4].wait()
-                pass_small()
-
-            make_slab(head - 1)
-
-        @pl.when(jnp.logical_and(head > 0, step == 2))
-        def _():
-            pass_slab(head - 1)
-
-    make_slab(heads - 1)
-    for now in range(heads * TURNS, PHASE[1] + 12):
+            pass_small()
+
+    loads[5].wait()
+    for head in range(heads - 1):
+        absorb(head)
+        product = times_t(joined[...], wv[head])
+        xacc[...] = product if head == 0 else xacc[...] + product
+    tick(heads * TURNS)
+    absorb(heads - 1)
+    for side in range(2):
+        at = pl.ds(side * rows, rows)
+        xsend[side] = (xacc[at] + times_t(joined[at], wv[heads - 1])).astype(bf16)
+        pl.when(is_own(side))(give_back(side, True).start)
+        pl.when(jnp.logical_not(is_own(side)))(give_back(side, False).start)
+
+    loads[4].wait()
+    for head in range(heads):
+        make_slab(head)
+        tick(heads * TURNS + 1 + head)
+    for head in range(heads):
+        pass_slab(head)
+    for now in range(heads * TURNS + 1 + heads, PHASE[-1] + UNITS):
         tick(now)
-    loads[5].wait()
     loads[6].wait()
-
-    @pl.loop(0, heads)
-    def _(head):
-        own_gradient(head).wait()
-
-        @pl.loop(1, 8)
-        def _(step):
-            which = lax.rem(blk + step, 8)
-            slot = lax.rem(which, 4) * heads + head
-            gradient_copy(head, which).wait_send()
-            landed(arrive.at[which // 4, slot], grecv_sem.at[which // 4, slot])
-
-    pass_slab(heads - 1)
-
-    for table in range(2):
-        for pair in range(GROUPS * heads // 2):
-            left, right = arrive[table, 2 * pair], arrive[table, 2 * pair + 1]
-            for part in range(3):
-                cut = slice(part * HD, (part + 1) * HD)
-                joined[:, pl.ds(part * width + pair * LANES, LANES)] = jnp.concatenate(
-                    [left[:, cut], right[:, cut]], axis=1
-                )
-        at = pl.ds(table * rows, rows)
-        tgrad_ref[table] = (prev[at] + times_t(joined[...], wv[...])).astype(bf16)
-
-    for now in range(PHASE[1] + 12, PHASE[-1] + 12):
-        tick(now)
 
     def slabs_in(head, at):
         return [line_in[head, half_at * GROUPS + at].astype(f32) for half_at in range(2)]
@@ -1094,7 +1136,7 @@
     each = width // 32
     bias = []
     for part in range(3):
-        cut = slice(part * HD, (part + 1) * HD)
+        cut = slice((part + 2) % 3 * HD, (part + 2) % 3 * HD + HD)
         for pair in range(GROUPS * heads // 2):
             both_heads = jnp.concatenate([own[2 * pair][:, cut], own[2 * pair + 1][:, cut]], axis=1)
             lanes = slice(part * width + pair * LANES, part * width + (pair + 1) * LANES)
@@ -1121,6 +1163,22 @@
     little_ref[6:7] = take(jnp.broadcast_to(wide, (8, width)), 4 * each * blk, 4 * each)[:1]
     little_ref[7:8] = take(bias, 2 * each * lax.rem(index, 16), 2 * each)[:1]
 
+    for table in range(2):
+        landed(back.at[table], xrecv_sem.at[table])
+        tgrad_ref[table] = (
+            prev[pl.ds(table * rows, rows)] + back[table].astype(f32)
+        ).astype(bf16)
+
+    for side in range(2):
+        pl.when(jnp.logical_not(is_own(side)))(give_back(side, False).wait_send)
+
+    @pl.loop(0, heads)
+    def _(head):
+        @pl.loop(1, 4)
+        def _(step):
+            for copy in gradient_copies(head, lax.rem(group + step, 4), False):
+                copy.wait_send()
+
     for step in range(1, 8):
         context_copy(lax.rem(blk + step, 8)).wait_send()
         small_blk(step).wait_send()
@@ -1140,7 +1198,7 @@
                 stage_copy(stage, unit).wait_send()
 
 
-def attend_back(dctx, qkv, ot, lse, full_t, qkv_weight, pre, small, parts, heads):
+def attend_back(dctx, qkv, ot, lse, full_t, by_head, pre, small, parts, heads):
     width, total = full_t.shape
     blocks = 8
     rows = total // blocks
@@ -1166,22 +1224,28 @@
         in_specs=[any_space] * 8 + [vmem],
         out_specs=(vmem,) * 6,
         scratch_shapes=[
-            pltpu.VMEM((blocks, rows, heads * HD), bf16),
+            pltpu.VMEM((blocks, rows // 2, 2 * heads * HD), bf16),
             pltpu.VMEM((heads, total, HD), bf16),
             pltpu.VMEM((heads, 4, 8, 2 * rows), f32),
             pltpu.VMEM((3 * heads, total, LANES), bf16),
             pltpu.VMEM(ot.shape, f32),
             pltpu.VMEM(lse.shape, f32),
             pltpu.VMEM((width, total), bf16),
-            pltpu.VMEM(qkv_weight.shape, bf16),
+            pltpu.VMEM(by_head.shape, bf16),
             pltpu.VMEM((2 * rows, width), f32),
             pltpu.VMEM((heads, LANES, total), bf16),
+            pltpu.VMEM((total, HD), bf16),
             pltpu.VMEM((total, HD), f32),
             pltpu.VMEM((total, HD), f32),
-            pltpu.VMEM((total, HD), f32),
-            pltpu.VMEM((heads, blocks, rows, 3 * HD), bf16),
-            pltpu.VMEM((2, GROUPS * heads, rows, 3 * HD), bf16),
-            pltpu.VMEM((rows, 3 * width), bf16),
+            pltpu.VMEM((heads, total, 3 * HD), bf16),
+            pltpu.VMEM((heads, 4, rows, 2 * HD), bf16),
+            pltpu.VMEM((heads, 4, 2 * rows, 2 * HD), bf16),
+            pltpu.VMEM((GROUPS * heads, rows, 2 * HD), bf16),
+            pltpu.VMEM((GROUPS * heads, 2 * rows, 2 * HD), bf16),
+            pltpu.VMEM((2 * rows, width), bf16),
+            pltpu.VMEM((2 * rows, width), f32),
+            pltpu.VMEM((2, rows, width), bf16),
+            pltpu.VMEM((2, rows, width), bf16),
             pltpu.VMEM((2, 2, 2, 2, 2, *unit), bf16),
             pltpu.VMEM((UNITS, 2, 2, 2, 2, *unit), bf16),
             pltpu.VMEM((UNITS, 2, 2, 2, *unit), bf16),
@@ -1197,8 +1261,10 @@
             pltpu.VMEM((8, 16, width), f32),
             dma((blocks,)),
             dma((blocks,)),
-            dma((heads, blocks)),
+            dma((2, heads, 4)),
             dma((2, GROUPS * heads)),
+            dma((2,)),
+            dma((2,)),
             dma((STAGES, UNITS)),
             dma((STAGES, UNITS)),
             dma((heads + 1, 4)),
@@ -1206,13 +1272,33 @@
             dma((heads + 1, 8)),
             dma((heads + 1, 8)),
             dma((7,)),
-            dma((heads,)),
             dma((2,)),
         ],
         compiler_params=pltpu.CompilerParams(
             collective_id=2, has_side_effects=True, vmem_limit_bytes=62 << 20
         ),
-    )(dctx, qkv, ot, lse, full_t, qkv_weight, pre, parts, small)
+    )(dctx, qkv, ot, lse, full_t, by_head, pre, parts, small)
+
+
+def finish_kernel(whole, *refs):
+    little_ref, outs = refs[whole], refs[whole + 1 :]
+    for src, dst in zip(refs[:whole], outs[:whole]):
+        dst[...] = src[...]
+    for at, dst in enumerate(outs[whole:]):
+        dst[...] = little_ref[at, : dst.shape[0]]
+
+
+def finish(arrays, little, counts):
+    vmem = pl.BlockSpec(memory_space=pltpu.VMEM)
+    shapes = [jax.ShapeDtypeStruct(a.shape, a.dtype) for a in arrays]
+    shapes += [jax.ShapeDtypeStruct((count,), jnp.float32) for count in counts]
+    return pl.pallas_call(
+        functools.partial(finish_kernel, len(arrays)),
+        name="finish",
+        out_shape=tuple(shapes),
+        in_specs=[vmem] * (len(arrays) + 1),
+        out_specs=(vmem,) * len(shapes),
+    )(*arrays, little)
 
 
 def halves(grad):
@@ -1270,6 +1356,7 @@
 ):
     f32, bf16 = jnp.float32, jnp.bfloat16
     tables, groups, rows, cols = ctx_ref.shape
+    rows, cols = 2 * rows, cols // 2
     width = tok_ref.shape[1]
     chunks = active_t.shape[0]
     loads = (
@@ -1288,7 +1375,7 @@
         pre1 = tok_ref[cut].astype(f32) + par(0)
         for group in range(groups):
             pre1 += jnp.dot(
-                ctx_ref[table, group],
+                unfold(ctx_ref[table, group]),
                 outw_ref[group * cols : (group + 1) * cols],
                 preferred_element_type=f32,
             )
@@ -1383,16 +1470,18 @@
         small[0] += column_sum(low)
         lows.append(low)
         for group in range(groups):
-            dctx_ref[table, group] = times_t(
-                low, outw_ref[group * cols : (group + 1) * cols]
-            ).astype(bf16)
+            dctx_ref[table, group] = fold(
+                times_t(low, outw_ref[group * cols : (group + 1) * cols]).astype(bf16)
+            )
     for at in range(3):
         small_ref[at : at + 1] = small[at]
     small_ref[10:] = jnp.zeros((6, width), f32)
     for group in range(groups):
         wout = 0.0
         for table in range(tables):
-            wout += jnp.dot(ctx_ref[table, group].T, lows[table], preferred_element_type=f32)
+            wout += jnp.dot(
+                unfold(ctx_ref[table, group]).T, lows[table], preferred_element_type=f32
+            )
         stage_u[group * 8 : (group + 1) * 8] = halves(wout.reshape(8, each, width)).astype(bf16)
     last = pltpu.make_async_copy(stage_u, parts_ref.at[8], stage_sem.at[4])
     last.start()
@@ -1475,19 +1564,24 @@
     f32 = jnp.float32
     heads = width // HD // GROUPS
     flat_tokens = tokens.reshape(tables * rows, width)
-    six = jnp.stack([out_bias, attn_gain, attn_shift, down_bias, ffn_gain, ffn_shift])
-    params = jnp.concatenate(
-        [
-            six,
-            jnp.zeros((2, width), six.dtype),
-            jnp.broadcast_to(qkv_bias[None, :width], (8, width)),
-            jnp.broadcast_to(qkv_bias[None, width:], (8, width)),
-            up_bias.reshape(-1, width),
-            jnp.zeros((4, width), six.dtype),
-        ]
-    ).astype(f32)
-
-    ctx, full_t, qkv, ot, lse = attend(tokens, lengths, params, qkv_weight, heads)
+    row = lax.broadcasted_iota(jnp.int32, (32, width), 0)
+    params = jnp.zeros((32, width), jnp.bfloat16)
+    spans = [
+        (at, at + 1, vector)
+        for at, vector in enumerate(
+            (out_bias, attn_gain, attn_shift, down_bias, ffn_gain, ffn_shift)
+        )
+    ]
+    spans += [(8, 16, qkv_bias[:width]), (16, 24, qkv_bias[width:])]
+    spans += [
+        (24 + at, 25 + at, up_bias[at * width : (at + 1) * width])
+        for at in range(up_bias.shape[0] // width)
+    ]
+    for first, last, vector in spans:
+        params = jnp.where((row >= first) & (row < last), vector[None], params)
+
+    params = params.astype(f32)
+    ctx, full_t, qkv, ot, lse, by_head = attend(tokens, lengths, params, qkv_weight, heads)
     layer_out, dctx, pre, small, parts = ffn(
         flat_tokens,
         ctx,
@@ -1497,25 +1591,40 @@
         up_weight,
         down_weight,
     )
-    token_grad, wgrad_qkv, wgrad_out, wgrad_up, wgrad_down, little = attend_back(
-        dctx, qkv, ot, lse, full_t, qkv_weight, pre, small, parts, heads
+    *whole, little = attend_back(
+        dctx, qkv, ot, lse, full_t, by_head, pre, small, parts, heads
     )
     each = width // 32
+    (
+        token_grad,
+        wgrad_qkv,
+        wgrad_out,
+        wgrad_up,
+        wgrad_down,
+        bgrad_out,
+        ggrad_attn,
+        sgrad_attn,
+        bgrad_down,
+        ggrad_ffn,
+        sgrad_ffn,
+        bgrad_up,
+        bgrad_qkv,
+    ) = finish(whole, little, [each] * 6 + [4 * each, 2 * each])
     return (
         layer_out.reshape(tokens.shape),
         token_grad,
         wgrad_qkv,
-        little[7, : 2 * each],
+        bgrad_qkv,
         wgrad_out,
-        little[0, :each],
-        little[1, :each],
-        little[2, :each],
+        bgrad_out,
+        ggrad_attn,
+        sgrad_attn,
         wgrad_up,
-        little[6, : 4 * each],
+        bgrad_up,
         wgrad_down,
-        little[3, :each],
-        little[4, :each],
-        little[5, :each],
+        bgrad_down,
+        ggrad_ffn,
+        sgrad_ffn,
     )
 
 

time: 269 us -> 215 us (0.80)
  Pallas kernels: 249 us -> 210 us
  local copies, waits for them, and re-layouts: 18.1 us -> 0.78 us
    pallas_call x1, Pallas kernels: 139 us -> 110 us  [attend_back(): pl.pallas_call(functools.partial(attend_back_kernel, heads), name='attend...]
    pallas_call x1, Pallas kernels: 73.7 us -> 62 us  [attend(): pl.pallas_call(functools.partial(attend_kernel, heads), name='attend', ou...]
    unnamed x5 -> x0, local copies, waits for them, and re-layouts: 8.6 us -> none
    another operation x6 -> x0, local copies, waits for them, and re-layouts: 4.11 us -> none  [shards_direct(): jnp.stack([out_bias, attn_gain, attn_shift, down_bias, ffn_gain, ffn_shift])]
    squeeze x3 -> x0, local copies, waits for them, and re-layouts: 3.8 us -> none  [the longest x1 1.43 us: shards_direct(): little[5, :each]]
where the time goes in v3:
time: 215 us; the launch traced here: 214 us
  Pallas kernels  210 us (98%)
    pallas_call x1, Pallas kernels, attend_back(): pl.pallas_call(functools.partial(attend_back_kernel, heads), name='attend...  110 us
    pallas_call x1, Pallas kernels, attend(): pl.pallas_call(functools.partial(attend_kernel, heads), name='attend', ou...  62 us
    pallas_call x1, Pallas kernels, ffn(): pl.pallas_call(ffn_kernel, name='ffn', out_shape=(jax.ShapeDtypeStruct((t...  35.8 us

profile of v3, /device:TPU:0, one launch (start us, length us, event | category | flops | bytes accessed | tf_op | source)
XLA Modules:
  0.0 213.7 jit_solution(18159912662252060177)
XLA Ops:
  0.7 0.8 fusion
  1.5 1.5 select_convert_fusion.par_ref
  3.0 62.0 %attend.1 = (bf16[2,4,128,384]{3,2,1,0:T(8,128)(2,1)}, bf16[768,2048]{1,0:T(8,128)(2,1)}, bf16[9,2048,128]{2,1,0:T(8,128)(2,1)}, f32[4,192,512]{2,1,0:T(8,128)},...) custom-call(bf16[2,256,768]{2,1,0:T(8,128)(2,1)} %tok_ref.1, s32[2]{0:T(128)} %len_ref.1, ...), custom_call_target="tpu_custom_call" | custom-call | tf_op jit(solution)/shard_map/attend/pallas_call | solution.py:614
  65.0 35.8 %ffn.1 = (bf16[512,768]{1,0:T(8,128)(2,1)}, bf16[2,4,128,384]{3,2,1,0:T(8,128)(2,1)}, f32[512,768]{1,0:T(8,128)}, f32[16,768]{1,0:T(8,128)}, bf16[9,32,48,384]{3,2,1,0:T(8,128)(2,1)}) custom-call(bf16[512,768]{1,0:T(8,128)(2,1)} %bitcast.5, bf16[2,4,128,384]{3,2,1,0:T(8,128)(2,1)} %get-tuple-element.44.ctx_ref, bf16[512,768]{1,0:T(8,128)(2,1)} %bitcast.6, ...), custom_call_target="tpu_custom_call" | custom-call | flops 23555211264 | bytes 41943040 | tf_op jit(solution)/shard_map/ffn/pallas_call | solution.py:1499
  100.9 110.0 %attend_back.1 = (bf16[2,256,768]{2,1,0:T(8,128)(2,1)}, f32[24,2304]{1,0:T(8,128)}, f32[24,768]{1,0:T(8,128)}, f32[24,3072]{1,0:T(8,128)}, f32[96,768]{1,0:T(8,128)}, /*index=5*/f32[8,128]{1,0:T(8,128)}) custom-call(bf16[2,4,128,384]{3,2,1,0:T(8,128)(2,1)} %get-tuple-element.46.dctx_ref, bf16[9,2048,128]{2,1,0:T(8,128)(2,1)} %get-tuple-element.47.qkv_ref, ...), custom_call_target="tpu_custom_call" | custom-call | tf_op jit(solution)/shard_map/attend_back/pallas_call | solution.py:1213
  210.9 2.6 %finish.1 = (bf16[2,256,768]{2,1,0:T(8,128)(2,1)}, f32[24,2304]{1,0:T(8,128)}, f32[24,768]{1,0:T(8,128)}, f32[24,3072]{1,0:T(8,128)}, f32[96,768]{1,0:T(8,128)},...) custom-call(bf16[2,256,768]{2,1,0:T(8,128)(2,1)} %get-tuple-element., ...), custom_call_target="tpu_custom_call" | custom-call | tf_op jit(solution)/shard_map/finish/pallas_call | solution.py:1295
  (6 shorter events, 0.0 us)

commit v4 on v3

--- a/solution.py
+++ b/solution.py
@@ -357,6 +357,60 @@
     pl.semaphore_wait(barrier, 7)
 
 
+def greet_all(tab, blk):
+    barrier = pltpu.get_barrier_semaphore()
+    for step in range(1, 8):
+        pl.semaphore_signal(
+            barrier, inc=1, device_id=(tab, lax.rem(blk + step, 8)), device_id_type=MESH
+        )
+    for step in range(1, 4):
+        pl.semaphore_signal(
+            barrier, inc=1, device_id=(lax.rem(tab + step, 4), blk), device_id_type=MESH
+        )
+    pl.semaphore_wait(barrier, 10)
+
+
+def send_to(src, dst, send_sem, recv_sem, device):
+    return pltpu.make_async_remote_copy(
+        src_ref=src,
+        dst_ref=dst,
+        send_sem=send_sem,
+        recv_sem=recv_sem,
+        device_id=device,
+        device_id_type=MESH,
+    )
+
+
+def landed(ref, sem):
+    pltpu.make_async_copy(ref, ref, sem).wait()
+
+
+def return_rows(src, dst, send_sem, recv_sem, act):
+    tab, _, chip, core = place()
+    half, group = chip // 2, 2 * lax.rem(chip, 2) + core
+    for side in range(2):
+        is_own = jnp.logical_and(chip == group, core == side)
+        own = pltpu.make_async_copy(src.at[side], dst.at[half], recv_sem.at[half])
+        away = send_to(
+            src.at[side],
+            dst.at[half],
+            send_sem.at[side],
+            recv_sem.at[half],
+            (tab, 2 * group + side),
+        )
+        if act == "start":
+            pl.when(is_own)(own.start)
+            pl.when(jnp.logical_not(is_own))(away.start)
+        else:
+            pl.when(jnp.logical_not(is_own))(away.wait_send)
+            landed(dst.at[side], recv_sem.at[side])
+
+
+def by_core(core, act):
+    pl.when(core == 0)(functools.partial(act, 0))
+    pl.when(core == 1)(functools.partial(act, 1))
+
+
 def fold(block):
     cut = block.shape[0] // 2
     return jnp.concatenate([block[:cut], block[cut:]], axis=1)
@@ -383,7 +437,10 @@
     len_ref,
     par_ref,
     w_hbm,
+    cot_hbm,
     ctx_ref,
+    mytok_ref,
+    mycot_ref,
     fullt_ref,
     qkv_ref,
     ot_ref,
@@ -399,11 +456,15 @@
     vtv,
     otv,
     lsev,
+    acc,
+    peaks,
     csend,
     send_sem,
     recv,
     csend_sem,
     crecv_sem,
+    osend_sem,
+    orecv_sem,
     local_sem,
 ):
     tab, blk, chip, core = place()
@@ -491,6 +552,37 @@
             vtv[head, :, pl.ds(first, rows)] = v.T.astype(jnp.bfloat16)
         toktv[:, pl.ds(first, rows)] = tok.T
 
+    def take_keys(tile, head, first_key, count, fresh):
+        queries = pl.ds(pl.multiple_of(tile * 2 * rows, 2 * rows), 2 * rows)
+        keys = pl.ds(pl.multiple_of(first_key, count), count)
+        st = times_t(qkvv[heads + head, keys], qkvv[head, queries])
+        peak = jnp.max(st, axis=0, keepdims=True)
+        if not fresh:
+            before = peaks[tile, pl.ds(head, 1)]
+            peak = jnp.maximum(peak, before)
+        pt = jnp.exp2((st - peak) * scale).astype(jnp.bfloat16)
+        ot = jnp.dot(vtv[head, :, keys], pt, preferred_element_type=jnp.float32)
+        if not fresh:
+            ot += acc[tile, head] * jnp.exp2((before - peak) * scale)
+        acc[tile, head] = ot
+        peaks[tile, pl.ds(head, 1)] = peak
+
+    def meet_keys_of_own_half():
+        @pl.loop(0, 2 * heads)
+        def _(at):
+            tile = jnp.where(at < heads, chip, mate)
+            take_keys(tile, lax.rem(at, heads), half * 4 * rows, 4 * rows, True)
+
+    def meet_keys_of_near():
+        @pl.loop(0, heads)
+        def _(head):
+            take_keys(other_near, head, half * 4 * rows, 4 * rows, True)
+
+        @pl.loop(0, 3 * heads)
+        def _(at):
+            tile = jnp.where(at < heads, chip, jnp.where(at < 2 * heads, mate, other_near))
+            take_keys(tile, lax.rem(at, heads), other_near * 2 * rows, 2 * rows, False)
+
     project(blk)
 
     def half_lanes(part, at):
@@ -517,13 +609,39 @@
     project(2 * chip + 1 - core)
     arrived(2 * mate + 1 - core)
     project(2 * mate + 1 - core)
-    for slot, src_chip in ((1, other_near), (2, other_far)):
+
+    def pass_on(slot, src_chip):
         arrived(2 * src_chip + core)
         pl.when(is_near)(to_far(slot, src_chip).start)
         to_core(slot, src_chip).start()
+
+    def project_chip(src_chip):
         project(2 * src_chip + core)
         arrived(2 * src_chip + 1 - core)
         project(2 * src_chip + 1 - core)
+
+    def owner_of(table):
+        return 2 * table + chip // 2, lax.rem(chip, 2)
+
+    def cotangent_copy(table, own):
+        src, dst = cot_hbm.at[table], mycot_ref.at[core]
+        if own:
+            return pltpu.make_async_copy(src, dst, orecv_sem.at[core])
+        return remote(src, dst, osend_sem.at[table], orecv_sem.at[core], *owner_of(table))
+
+    def is_owner(table):
+        to_chip, to_core = owner_of(table)
+        return jnp.logical_and(to_chip == chip, to_core == core)
+
+    pl.when(is_near)(functools.partial(pass_on, 1, other_near))
+    meet_keys_of_own_half()
+    pl.when(jnp.logical_not(is_near))(functools.partial(pass_on, 1, other_near))
+    pl.when(is_near)(functools.partial(pass_on, 2, other_far))
+    cotangent_copy(1 - half, False).start()
+    project_chip(other_near)
+    meet_keys_of_near()
+    pl.when(jnp.logical_not(is_near))(functools.partial(pass_on, 2, other_far))
+    project_chip(other_far)
 
     keep = (
         pltpu.make_async_copy(toktv, fullt_ref, local_sem.at[0]),
@@ -533,46 +651,60 @@
     for copy in keep:
         copy.start()
 
+    pl.when(is_owner(half))(cotangent_copy(half, True).start)
+    pl.when(jnp.logical_not(is_owner(half)))(cotangent_copy(half, False).start)
+    my_tokens = [
+        pltpu.make_async_copy(
+            tokv.at[2 * group + side], mytok_ref.at[side], local_sem.at[7 + side]
+        )
+        for side in range(2)
+    ]
+    for copy in my_tokens:
+        copy.start()
+
     def context_copy(which):
         return remote(
             csend.at[which],
-            ctx_ref.at[half, group],
+            ctx_ref.at[group],
             csend_sem.at[which],
-            crecv_sem.at[blk],
-            which // 2,
+            crecv_sem.at[group],
+            2 * half + which // 2,
             lax.rem(which, 2),
         )
 
     own_context = pltpu.make_async_copy(
-        csend.at[blk], ctx_ref.at[half, group], local_sem.at[2]
+        csend.at[group], ctx_ref.at[group], local_sem.at[2]
     )
 
     @pl.loop(0, 4)
     def _(step):
-        which = lax.rem(chip + 1 + step, 4)
-        first = pl.multiple_of(which * 2 * rows, 2 * rows)
+        at = jnp.where(is_near, step, 3 - step)
+        which = jnp.where(
+            at < 2, jnp.where(at == 0, chip, mate), jnp.where(at == 2, other_near, other_far)
+        )
+
+        @pl.when(at == 3)
+        def _():
+            @pl.loop(0, heads)
+            def _(head):
+                take_keys(which, head, 0, 8 * rows, True)
+
+        @pl.when(at < 3)
+        def _():
+            @pl.loop(0, heads)
+            def _(head):
+                take_keys(which, head, other_far * 2 * rows, 2 * rows, False)
+
         for head in range(heads):
-            q = qkvv[head, pl.ds(first, 2 * rows)]
-            st = times_t(qkvv[heads + head], q)
-            peak = jnp.max(st, axis=0, keepdims=True)
-            pt = jnp.exp2((st - peak) * scale).astype(jnp.bfloat16)
-            ot = jnp.dot(vtv[head], pt, preferred_element_type=jnp.float32)
+            ot = acc[which, head]
             total = ot[HD : HD + 1]
             otv[which, head * HD : (head + 1) * HD] = ot[:HD] / total
+            peak = peaks[which, head : head + 1]
             lsev[which, head : head + 1] = peak * scale + jnp.log(total) * LOG2E
-        out = otv[which].T.astype(jnp.bfloat16)
-        for side in range(2):
-            csend[2 * which + side] = fold(out[side * rows : (side + 1) * rows])
-
-        @pl.when(step < 3)
-        def _():
-            context_copy(2 * which).start()
-            context_copy(2 * which + 1).start()
-
-        @pl.when(step == 3)
-        def _():
-            context_copy(2 * which + 1 - core).start()
-            own_context.start()
+        csend[which] = fold(otv[which].T.astype(jnp.bfloat16))
+
+        pl.when(which == group)(own_context.start)
+        pl.when(which != group)(context_copy(which).start)
 
     more = (
         pltpu.make_async_copy(otv, ot_ref, local_sem.at[3]),
@@ -588,23 +720,21 @@
         pl.when(is_near)(to_far(slot, src_chip).wait_send)
         to_core(slot, src_chip).wait_send()
 
-    @pl.loop(1, 8)
-    def _(step):
-        which = lax.rem(blk + step, 8)
+    for step in range(1, 4):
+        which = lax.rem(group + step, 4)
         context_copy(which).wait_send()
-        pltpu.make_async_copy(
-            ctx_ref.at[which // 4, lax.rem(which, 4)],
-            ctx_ref.at[which // 4, lax.rem(which, 4)],
-            crecv_sem.at[which],
-        ).wait()
-
+        pltpu.make_async_copy(ctx_ref.at[which], ctx_ref.at[which], crecv_sem.at[which]).wait()
     own_context.wait()
-    for copy in keep + more:
+    pl.when(jnp.logical_not(is_owner(half)))(cotangent_copy(half, False).wait_send)
+    cotangent_copy(1 - half, False).wait_send()
+    for side in range(2):
+        pltpu.make_async_copy(mycot_ref.at[side], mycot_ref.at[side], orecv_sem.at[side]).wait()
+    for copy in [*keep, *more, *my_tokens]:
         copy.wait()
 
 
-def attend(tokens, lengths, params, qkv_weight, heads):
-    tables, rows, width = tokens.shape
+def attend(tokens, lengths, params, qkv_weight, cotangent, heads):
+    _, rows, width = tokens.shape
     blocks = 8
     total = blocks * rows
     any_space = pl.BlockSpec(memory_space=pl.ANY)
@@ -615,15 +745,17 @@
         functools.partial(attend_kernel, heads),
         name="attend",
         out_shape=(
-            jax.ShapeDtypeStruct((tables, GROUPS, rows // 2, 2 * heads * HD), bf16),
+            jax.ShapeDtypeStruct((GROUPS, rows, 2 * heads * HD), bf16),
+            jax.ShapeDtypeStruct((2, rows, width), bf16),
+            jax.ShapeDtypeStruct((2, rows, width), bf16),
             jax.ShapeDtypeStruct((width, total), bf16),
             jax.ShapeDtypeStruct((3 * heads, total, LANES), bf16),
             jax.ShapeDtypeStruct((4, heads * HD, 2 * rows), f32),
             jax.ShapeDtypeStruct((4, 8, 2 * rows), f32),
             jax.ShapeDtypeStruct((heads, width, width), bf16),
         ),
-        in_specs=[vmem, pl.BlockSpec(memory_space=pltpu.SMEM), vmem, any_space],
-        out_specs=(any_space,) * 6,
+        in_specs=[vmem, pl.BlockSpec(memory_space=pltpu.SMEM), vmem, any_space, any_space],
+        out_specs=(any_space,) * 8,
         scratch_shapes=[
             pltpu.VMEM((blocks, rows, width), bf16),
             pltpu.VMEM((width, total), bf16),
@@ -635,23 +767,27 @@
             pltpu.VMEM((heads, LANES, total), bf16),
             pltpu.VMEM((4, heads * HD, 2 * rows), f32),
             pltpu.VMEM((4, 8, 2 * rows), f32),
-            pltpu.VMEM((blocks, rows // 2, 2 * heads * HD), bf16),
+            pltpu.VMEM((4, heads, LANES, 2 * rows), f32),
+            pltpu.VMEM((4, 8, 2 * rows), f32),
+            pltpu.VMEM((GROUPS, rows, 2 * heads * HD), bf16),
             dma((8,)),
             dma((blocks,)),
-            dma((blocks,)),
-            dma((blocks,)),
-            dma((7,)),
+            dma((GROUPS,)),
+            dma((GROUPS,)),
+            dma((2,)),
+            dma((2,)),
+            dma((9,)),
         ],
         compiler_params=pltpu.CompilerParams(
             collective_id=1, has_side_effects=True, vmem_limit_bytes=60 << 20
         ),
-    )(tokens, lengths, params, qkv_weight)
+    )(tokens, lengths, params, qkv_weight, cotangent)
 
 
 UNITS = 9
 TURNS = 4
 STAGES = 5
-PHASE = (2, 5, 7, 9, 11)
+PHASE = ((1, 4, -1), (2, 0, 1), (3, 0, 4), (4, 0, 7))
 
 
 def attend_back_kernel(
@@ -663,6 +799,8 @@
     fullt_ref,
     w_ref,
     pre_ref,
+    down_ref,
+    up_ref,
     parts_ref,
     small_ref,
     tgrad_ref,
@@ -692,7 +830,6 @@
     joined,
     xacc,
     xsend,
-    back,
     mine,
     sum0,
     sum1,
@@ -701,11 +838,13 @@
     sum4,
     slab,
     slab_in,
+    sums,
+    sums_in,
     line,
     line_in,
     small_in,
-    small_line,
-    small_line_in,
+    small_sum,
+    small_pairs,
     dsend_sem,
     drecv_sem,
     gsend_sem,
@@ -726,25 +865,14 @@
     y, x, zh, zl = tab // 2, lax.rem(tab, 2), chip // 2, lax.rem(chip, 2)
     half = zh
     group = 2 * zl + core
-    blocks, rows = dov.shape[0], 2 * dov.shape[1]
+    blocks, rows = 8, dov.shape[1]
     width = toktv.shape[0]
     tile = 2 * rows
     piece = 256
     scale = LOG2E / math.sqrt(HD)
     shrink = HD**-0.5
 
-    def remote(src, dst, send_sem, recv_sem, device):
-        return pltpu.make_async_remote_copy(
-            src_ref=src,
-            dst_ref=dst,
-            send_sem=send_sem,
-            recv_sem=recv_sem,
-            device_id=device,
-            device_id_type=MESH,
-        )
-
-    def landed(ref, sem):
-        pltpu.make_async_copy(ref, ref, sem).wait()
+    remote = send_to
 
     loads = [
         pltpu.make_async_copy(src, dst, local_sem.at[at])
@@ -753,61 +881,48 @@
                 (qkv_ref, qkvv),
                 (ot_ref, otv),
                 (lse_ref, lsev),
-                (dctx_ref.at[half, group], dov.at[blk]),
+                (dctx_ref.at[group], dov.at[group]),
                 (fullt_ref, toktv),
                 (w_ref, wv),
                 (pre_ref, prev),
+                (down_ref, sum1.at[:4]),
+                (up_ref, sum0.at[:4]),
             )
         )
     ]
     for copy in loads:
         copy.start()
 
-    barrier = pltpu.get_barrier_semaphore()
-    for step in range(1, 8):
-        pl.semaphore_signal(
-            barrier, inc=1, device_id=(tab, lax.rem(blk + step, 8)), device_id_type=MESH
-        )
-    for step in range(1, 4):
-        pl.semaphore_signal(
-            barrier, inc=1, device_id=(lax.rem(tab + step, 4), blk), device_id_type=MESH
-        )
-    pl.semaphore_wait(barrier, 10)
+    greet_all(tab, blk)
+
+    def group_at(step):
+        to_chip = jnp.where(step < 2, zl, 1 - zl)
+        return 2 * to_chip + jnp.where(lax.rem(step, 2) == 0, core, 1 - core)
 
     def context_copy(which):
         return remote(
-            dctx_ref.at[which // 4, lax.rem(which, 4)],
-            dov.at[blk],
+            dctx_ref.at[which],
+            dov.at[group],
             dsend_sem.at[which],
-            drecv_sem.at[blk],
-            (tab, which),
-        )
-
-    def chip_at(step):
-        mate = 2 * half + 1 - zl
-        return jnp.where(
-            step < 2,
-            jnp.where(step == 0, chip, mate),
-            jnp.where(step == 2, 2 - half, 3 - 3 * half),
-        )
-
-    context_copy(2 * chip + 1 - core).start()
+            drecv_sem.at[group],
+            (tab, 4 * half + which),
+        )
+
     for step in range(1, 4):
-        for side in (core, 1 - core):
-            context_copy(2 * chip_at(step) + side).start()
+        context_copy(group_at(step)).start()
 
     def stage_copy(stage, unit, order=None):
         send, done = ssend_sem.at[stage, unit], srecv_sem.at[stage, unit]
         if stage == 0:
-            src = parts_ref.at[unit, :, :, :, :, 1 - core]
-            return remote(src, sum0.at[unit], send, done, (tab, 2 * chip + 1 - core))
+            src = parts_ref.at[:, :, :, :, 1 - core]
+            return remote(src, sum0.at[unit - 4], send, done, (tab, 2 * chip + 1 - core))
         if stage == 1 and order == 0:
             return remote(
-                sum0.at[unit, :, 1 - x], sum1.at[unit], send, done, (2 * y + 1 - x, blk)
+                sum0.at[unit - 4, :, 1 - x], sum1.at[unit], send, done, (2 * y + 1 - x, blk)
             )
         if stage == 1:
             return remote(
-                sum0.at[unit, 1 - y], sum1.at[unit], send, done, (2 * (1 - y) + x, blk)
+                sum0.at[unit - 4, 1 - y], sum1.at[unit], send, done, (2 * (1 - y) + x, blk)
             )
         if stage == 2 and order == 0:
             return remote(
@@ -823,15 +938,10 @@
         src, there = sum3.at[unit, 1 - zh], 2 * (1 - zh) + zl
         return remote(src, sum4.at[unit], send, done, (tab, 2 * there + core))
 
-    def both(act):
-        pl.when(core == 0)(functools.partial(act, 0))
-        pl.when(core == 1)(functools.partial(act, 1))
-
-    def mine_copy(unit):
-        slot = lax.rem(unit, 2)
-        return pltpu.make_async_copy(
-            parts_ref.at[unit, :, :, :, :, core], mine.at[slot], mine_sem.at[slot]
-        )
+    both = functools.partial(by_core, core)
+    mine_copy = pltpu.make_async_copy(
+        parts_ref.at[:, :, :, :, core], mine, mine_sem.at[0]
+    )
 
     def finish(unit):
         done = sum4[unit].astype(f32) + sum3[unit, zh].astype(f32)
@@ -857,23 +967,18 @@
 
     def advance(stage, unit):
         if stage == 0:
-            landed(sum0.at[unit], srecv_sem.at[0, unit])
-            mine_copy(unit).wait()
-            slot = lax.rem(unit, 2)
+            landed(sum0.at[unit - 4], srecv_sem.at[0, unit])
+            mine_copy.wait()
             for a in range(2):
                 for b in range(2):
-                    sum0[unit, a, b] = sum0[unit, a, b] + mine[slot, a, b]
-
-            @pl.when(unit + 2 < UNITS)
-            def _():
-                mine_copy(unit + 2).start()
+                    sum0[unit - 4, a, b] = sum0[unit - 4, a, b] + mine[a, b]
 
             both(lambda order: stage_copy(1, unit, order).start())
         elif stage == 1:
             landed(sum1.at[unit], srecv_sem.at[1, unit])
 
             def act(order):
-                own = sum0[unit, :, x] if order == 0 else sum0[unit, y]
+                own = sum0[unit - 4, :, x] if order == 0 else sum0[unit - 4, y]
                 sum1[unit] = sum1[unit] + own
                 stage_copy(2, unit, order).start()
 
@@ -895,15 +1000,25 @@
             finish(unit)
 
     def tick(now):
-        for stage in range(STAGES):
-            unit = now - PHASE[stage]
-            due = (unit >= 0) & (unit < UNITS)
+        pl.when(now == 2)(functools.partial(advance, 0, UNITS - 1))
+
+        @pl.when((now >= 0) & (now < 4))
+        def _():
+            both(lambda order: stage_copy(1, 4 + now, order).start())
+
+        for stage, first, lag in PHASE:
+            unit = now - lag
+            due = (unit >= first) & (unit < UNITS)
             pl.when(due)(functools.partial(advance, stage, unit))
 
-    for unit in range(UNITS):
-        stage_copy(0, unit).start()
-    for unit in range(2):
-        mine_copy(unit).start()
+    stage_copy(0, UNITS - 1).start()
+    mine_copy.start()
+    for copy in loads[7:]:
+        copy.wait()
+
+    @pl.loop(0, 4)
+    def _(at):
+        both(lambda order: stage_copy(2, at, order).start())
 
     def tab_copy(src, dst, sem_at, step):
         there = lax.rem(tab + step, 4)
@@ -920,8 +1035,15 @@
     def small_tab(step):
         return tab_copy(lambda t: small_ref, lambda t: small_in.at[t], heads, step)
 
-    def small_blk(step):
-        return line_copy(lambda b: small_line, lambda b: small_line_in.at[b], heads, step)
+    def small_pair(at):
+        there = (2 * chip + 1 - core, 2 * (2 * zh + 1 - zl) + core, 2 * (2 * (1 - zh) + zl) + core)
+        return remote(
+            small_sum.at[at],
+            small_pairs.at[at],
+            lsend_sem.at[heads, at],
+            lrecv_sem.at[heads, at],
+            (tab, there[at]),
+        )
 
     def slab_tab(head, step):
         return tab_copy(
@@ -936,35 +1058,55 @@
     for step in range(1, 4):
         small_tab(step).start()
 
-    def pass_small():
-        total = small_ref[...]
-        for step in range(1, 4):
-            there = lax.rem(tab + step, 4)
-            landed(small_in.at[there], trecv_sem.at[heads, there])
-            total += small_in[there]
-        small_line[...] = total
-        for step in range(1, 8):
-            small_blk(step).start()
+    def pass_small(at):
+        if at == 0:
+            total = small_ref[...]
+            for step in range(1, 4):
+                there = lax.rem(tab + step, 4)
+                landed(small_in.at[there], trecv_sem.at[heads, there])
+                total += small_in[there]
+        else:
+            landed(small_pairs.at[at - 1], lrecv_sem.at[heads, at - 1])
+            total = small_sum[at - 1] + small_pairs[at - 1]
+        small_sum[at] = total
+        if at < 3:
+            small_pair(at).start()
+
+    def sums_tab(head, step):
+        return tab_copy(
+            lambda t: sums.at[head], lambda t: sums_in.at[head, t], heads + 1 + head, step
+        )
 
     def make_slab(head):
         flat = dqkv[head]
+        sums[head] = jnp.broadcast_to(
+            jnp.sum(flat.astype(f32), axis=0, keepdims=True), (8, 3 * HD)
+        )
         grad = jnp.dot(toktv[...], flat, preferred_element_type=f32)
-        sums = jnp.sum(flat.astype(f32), axis=0, keepdims=True)
-        sums = jnp.broadcast_to(sums, (8, 3 * HD))
-        grad = grad.reshape(4, 8, width // 32, 3 * HD)
-        for t in range(4):
-            for b in range(8):
-                slab[head, t, b] = jnp.concatenate([grad[t, b], sums], axis=0).astype(bf16)
+        each = width // 32
+        slab[head, :, :4] = grad[:, : 2 * HD].reshape(4, 4, 2 * each, 2 * HD).astype(bf16)
+        q = grad[:, 2 * HD :].reshape(16, 2, each, HD)
+        q = jnp.concatenate([q[:, 0], q[:, 1]], axis=2)
+        slab[head, :, 4:] = q.reshape(4, 2, 2 * each, 2 * HD).astype(bf16)
         for step in range(1, 4):
             slab_tab(head, step).start()
+            sums_tab(head, step).start()
 
     def pass_slab(head):
         total = slab[head, tab].astype(f32)
+        sums_total = sums[head]
         for step in range(1, 4):
             there = lax.rem(tab + step, 4)
             landed(slab_in.at[head, there], trecv_sem.at[head, there])
+            landed(sums_in.at[head, there], trecv_sem.at[heads + 1 + head, there])
             total += slab_in[head, there].astype(f32)
-        line[head] = total.astype(bf16)
+            sums_total += sums_in[head, there]
+        each = width // 32
+        for b in range(8):
+            kv = total[b // 2, b % 2 * each :][:each]
+            q = total[4 + b // 4, b // 2 % 2 * each :][:each, b % 2 * HD :][:, :HD]
+            rows_b = jnp.concatenate([jnp.concatenate([kv, q], axis=1), sums_total], axis=0)
+            line[head, b] = rows_b.astype(bf16)
         line_in[head, blk] = line[head, blk]
         for step in range(1, 8):
             slab_blk(head, step).start()
@@ -1019,38 +1161,24 @@
                     [arrive_kv[left][:, cut], arrive_kv[right][:, cut]], axis=1
                 )
 
-    def give_back(side, own):
-        src, dst = xsend.at[side], back.at[half]
-        if own:
-            return pltpu.make_async_copy(src, dst, xrecv_sem.at[half])
-        return remote(src, dst, xsend_sem.at[side], xrecv_sem.at[half], (tab, 2 * group + side))
-
-    def is_own(side):
-        return jnp.logical_and(chip == group, core == side)
-
     @pl.loop(0, heads * TURNS)
     def _(turn):
         head, step = turn // TURNS, lax.rem(turn, TURNS)
-        which = chip_at(step)
+        which = group_at(step)
         first = pl.multiple_of(which * tile, tile)
 
         @pl.when(head == 0)
         def _():
-            for side in range(2):
-                block = 2 * which + side
-
-                @pl.when(block != blk)
-                def _():
-                    landed(dov.at[block], drecv_sem.at[block])
-
-                dos = unfold(dov[block])
-                for at in range(heads):
-                    do = dos[:, at * HD : (at + 1) * HD]
-                    doh[at, pl.ds(first + side * rows, rows)] = do
-                    ot = otv[which, at * HD : (at + 1) * HD, side * rows : (side + 1) * rows]
-                    deltas[at, which, :1, side * rows : (side + 1) * rows] = jnp.sum(
-                        ot * do.astype(f32).T, axis=0, keepdims=True
-                    )
+            @pl.when(step > 0)
+            def _():
+                landed(dov.at[which], drecv_sem.at[which])
+
+            dos = unfold(dov[which])
+            for at in range(heads):
+                do = dos[:, at * HD : (at + 1) * HD]
+                doh[at, pl.ds(first, tile)] = do
+                ot = otv[which, at * HD : (at + 1) * HD]
+                deltas[at, which, :1] = jnp.sum(ot * do.astype(f32).T, axis=0, keepdims=True)
 
         @pl.when(step == 0)
         def _():
@@ -1092,7 +1220,19 @@
 
         @pl.when(turn == TURNS)
         def _():
-            pass_small()
+            loads[4].wait()
+            pass_small(0)
+
+        for at in range(1, 4):
+            pl.when(turn == TURNS + at)(functools.partial(pass_small, at))
+
+        @pl.when(jnp.logical_and(head > 0, step == 0))
+        def _():
+            make_slab(head - 1)
+
+        @pl.when(jnp.logical_and(head > 0, step == 3))
+        def _():
+            pass_slab(head - 1)
 
     loads[5].wait()
     for head in range(heads - 1):
@@ -1101,21 +1241,17 @@
         xacc[...] = product if head == 0 else xacc[...] + product
     tick(heads * TURNS)
     absorb(heads - 1)
+    loads[6].wait()
     for side in range(2):
         at = pl.ds(side * rows, rows)
-        xsend[side] = (xacc[at] + times_t(joined[at], wv[heads - 1])).astype(bf16)
-        pl.when(is_own(side))(give_back(side, True).start)
-        pl.when(jnp.logical_not(is_own(side)))(give_back(side, False).start)
-
-    loads[4].wait()
-    for head in range(heads):
-        make_slab(head)
-        tick(heads * TURNS + 1 + head)
-    for head in range(heads):
-        pass_slab(head)
-    for now in range(heads * TURNS + 1 + heads, PHASE[-1] + UNITS):
+        total = prev[at] + xacc[at] + times_t(joined[at], wv[heads - 1])
+        xsend[side] = total.astype(bf16)
+    return_rows(xsend, tgrad_ref, xsend_sem, xrecv_sem, "start")
+
+    make_slab(heads - 1)
+    for now in range(heads * TURNS + 1, PHASE[-1][2] + UNITS):
         tick(now)
-    loads[6].wait()
+    pass_slab(heads - 1)
 
     def slabs_in(head, at):
         return [line_in[head, half_at * GROUPS + at].astype(f32) for half_at in range(2)]
@@ -1124,11 +1260,7 @@
         for step in range(1, 8):
             there = lax.rem(blk + step, 8)
             landed(line_in.at[head, there], lrecv_sem.at[head, there])
-    total = small_line[...]
-    for step in range(1, 8):
-        there = lax.rem(blk + step, 8)
-        landed(small_line_in.at[there], lrecv_sem.at[heads, there])
-        total += small_line_in[there]
+    total = small_sum[3]
     own = [
         functools.reduce(jnp.add, slabs_in(at % heads, at // heads))
         for at in range(GROUPS * heads)
@@ -1163,14 +1295,9 @@
     little_ref[6:7] = take(jnp.broadcast_to(wide, (8, width)), 4 * each * blk, 4 * each)[:1]
     little_ref[7:8] = take(bias, 2 * each * lax.rem(index, 16), 2 * each)[:1]
 
-    for table in range(2):
-        landed(back.at[table], xrecv_sem.at[table])
-        tgrad_ref[table] = (
-            prev[pl.ds(table * rows, rows)] + back[table].astype(f32)
-        ).astype(bf16)
-
-    for side in range(2):
-        pl.when(jnp.logical_not(is_own(side)))(give_back(side, False).wait_send)
+    return_rows(xsend, tgrad_ref, xsend_sem, xrecv_sem, "wait")
+    for step in range(1, 4):
+        context_copy(group_at(step)).wait_send()
 
     @pl.loop(0, heads)
     def _(head):
@@ -1180,25 +1307,30 @@
                 copy.wait_send()
 
     for step in range(1, 8):
-        context_copy(lax.rem(blk + step, 8)).wait_send()
-        small_blk(step).wait_send()
         for head in range(heads):
             slab_blk(head, step).wait_send()
+    for at in range(3):
+        small_pair(at).wait_send()
     for step in range(1, 4):
         small_tab(step).wait_send()
         for head in range(heads):
             slab_tab(head, step).wait_send()
+            sums_tab(head, step).wait_send()
+
+    stage_copy(0, UNITS - 1).wait_send()
 
     @pl.loop(0, UNITS)
     def _(unit):
-        for stage in range(STAGES):
-            if stage in (1, 2):
-                both(lambda order, stage=stage: stage_copy(stage, unit, order).wait_send())
-            else:
-                stage_copy(stage, unit).wait_send()
-
-
-def attend_back(dctx, qkv, ot, lse, full_t, by_head, pre, small, parts, heads):
+        @pl.when(unit >= 4)
+        def _():
+            both(lambda order: stage_copy(1, unit, order).wait_send())
+
+        both(lambda order: stage_copy(2, unit, order).wait_send())
+        stage_copy(3, unit).wait_send()
+        stage_copy(4, unit).wait_send()
+
+
+def attend_back(dctx, qkv, ot, lse, full_t, by_head, pre, small, down, up, parts, heads):
     width, total = full_t.shape
     blocks = 8
     rows = total // blocks
@@ -1207,8 +1339,7 @@
     vmem = pl.BlockSpec(memory_space=pltpu.VMEM)
     bf16, f32 = jnp.bfloat16, jnp.float32
     dma = pltpu.SemaphoreType.DMA
-    unit = parts.shape[2:]
-    parts = parts.reshape(UNITS, 2, 2, 2, 2, 2, *unit)
+    unit = parts.shape[-2:]
     shape = jax.ShapeDtypeStruct
     return pl.pallas_call(
         functools.partial(attend_back_kernel, heads),
@@ -1221,10 +1352,10 @@
             shape((4 * each, width), f32),
             shape((8, LANES), f32),
         ),
-        in_specs=[any_space] * 8 + [vmem],
-        out_specs=(vmem,) * 6,
+        in_specs=[any_space] * 10 + [vmem],
+        out_specs=(any_space,) + (vmem,) * 5,
         scratch_shapes=[
-            pltpu.VMEM((blocks, rows // 2, 2 * heads * HD), bf16),
+            pltpu.VMEM((GROUPS, rows, 2 * heads * HD), bf16),
             pltpu.VMEM((heads, total, HD), bf16),
             pltpu.VMEM((heads, 4, 8, 2 * rows), f32),
             pltpu.VMEM((3 * heads, total, LANES), bf16),
@@ -1245,39 +1376,40 @@
             pltpu.VMEM((2 * rows, width), bf16),
             pltpu.VMEM((2 * rows, width), f32),
             pltpu.VMEM((2, rows, width), bf16),
-            pltpu.VMEM((2, rows, width), bf16),
-            pltpu.VMEM((2, 2, 2, 2, 2, *unit), bf16),
-            pltpu.VMEM((UNITS, 2, 2, 2, 2, *unit), bf16),
+            pltpu.VMEM((2, 2, 2, 2, *unit), bf16),
+            pltpu.VMEM((UNITS - 4, 2, 2, 2, 2, *unit), bf16),
             pltpu.VMEM((UNITS, 2, 2, 2, *unit), bf16),
             pltpu.VMEM((UNITS, 2, 2, *unit), bf16),
             pltpu.VMEM((UNITS, 2, *unit), bf16),
             pltpu.VMEM((UNITS, *unit), bf16),
-            pltpu.VMEM((heads, 4, 8, each + 8, 3 * HD), bf16),
-            pltpu.VMEM((heads, 4, 8, each + 8, 3 * HD), bf16),
+            pltpu.VMEM((heads, 4, 6, 2 * each, 2 * HD), bf16),
+            pltpu.VMEM((heads, 4, 6, 2 * each, 2 * HD), bf16),
+            pltpu.VMEM((heads, 8, 3 * HD), f32),
+            pltpu.VMEM((heads, 4, 8, 3 * HD), f32),
             pltpu.VMEM((heads, 8, each + 8, 3 * HD), bf16),
             pltpu.VMEM((heads, 8, each + 8, 3 * HD), bf16),
             pltpu.VMEM((4, 16, width), f32),
-            pltpu.VMEM((16, width), f32),
-            pltpu.VMEM((8, 16, width), f32),
-            dma((blocks,)),
-            dma((blocks,)),
+            pltpu.VMEM((4, 16, width), f32),
+            pltpu.VMEM((3, 16, width), f32),
+            dma((GROUPS,)),
+            dma((GROUPS,)),
             dma((2, heads, 4)),
             dma((2, GROUPS * heads)),
             dma((2,)),
             dma((2,)),
             dma((STAGES, UNITS)),
             dma((STAGES, UNITS)),
-            dma((heads + 1, 4)),
-            dma((heads + 1, 4)),
+            dma((2 * heads + 1, 4)),
+            dma((2 * heads + 1, 4)),
             dma((heads + 1, 8)),
             dma((heads + 1, 8)),
-            dma((7,)),
-            dma((2,)),
+            dma((9,)),
+            dma((1,)),
         ],
         compiler_params=pltpu.CompilerParams(
             collective_id=2, has_side_effects=True, vmem_limit_bytes=62 << 20
         ),
-    )(dctx, qkv, ot, lse, full_t, by_head, pre, parts, small)
+    )(dctx, qkv, ot, lse, full_t, by_head, pre, down, up, parts, small)
 
 
 def finish_kernel(whole, *refs):
@@ -1333,10 +1465,12 @@
     outw_ref,
     upw_hbm,
     downw_hbm,
-    out_ref,
+    layer_ref,
     dctx_ref,
     pre_ref,
     small_ref,
+    down_ref,
+    up_ref,
     parts_ref,
     upw,
     downw,
@@ -1349,16 +1483,27 @@
     pre2,
     gbranch,
     ghid,
-    stage_d,
-    stage_u,
+    out,
+    dparts,
+    uparts,
+    sum0,
+    sum1,
     load_sem,
-    stage_sem,
+    keep_sem,
+    osend_sem,
+    orecv_sem,
+    ssend_sem,
+    srecv_sem,
 ):
     f32, bf16 = jnp.float32, jnp.bfloat16
-    tables, groups, rows, cols = ctx_ref.shape
-    rows, cols = 2 * rows, cols // 2
+    groups, rows, cols = ctx_ref.shape
+    cols = cols // 2
+    sides = 2
     width = tok_ref.shape[1]
     chunks = active_t.shape[0]
+    each = width // 32
+    tab, blk, chip, core = place()
+    y, x = tab // 2, lax.rem(tab, 2)
     loads = (
         pltpu.make_async_copy(upw_hbm, upw, load_sem.at[0]),
         pltpu.make_async_copy(downw_hbm, downw, load_sem.at[1]),
@@ -1366,16 +1511,19 @@
     for copy in loads:
         copy.start()
 
+    greet_all(tab, blk)
+
     def par(at):
         return par_ref[at : at + 1]
 
     inverse1 = []
-    for table in range(tables):
+    contexts = [unfold(ctx_ref[group]) for group in range(groups)]
+    for table in range(sides):
         cut = pl.ds(table * rows, rows)
         pre1 = tok_ref[cut].astype(f32) + par(0)
         for group in range(groups):
             pre1 += jnp.dot(
-                unfold(ctx_ref[table, group]),
+                contexts[group][table * rows : (table + 1) * rows],
                 outw_ref[group * cols : (group + 1) * cols],
                 preferred_element_type=f32,
             )
@@ -1405,7 +1553,8 @@
         pre2[...] += jnp.dot(act, downw[cut], preferred_element_type=f32)
 
     normed, inverse = norm_parts(pre2[...])
-    out_ref[...] = (normed * par(4) + par(5)).astype(bf16)
+    out[...] = (normed * par(4) + par(5)).astype(bf16).reshape(out.shape)
+    return_rows(out, layer_ref, osend_sem, orecv_sem, "start")
     grad = cot_ref[...].astype(f32)
     small_ref[4:5] = column_sum(grad * normed)
     small_ref[5:6] = column_sum(grad)
@@ -1415,51 +1564,63 @@
     gbranch[...] = low
     small_ref[3:4] = column_sum(low)
 
-    each = width // 32
-
-    def down_copies(at):
-        return [
-            pltpu.make_async_copy(
-                stage_d.at[part],
-                parts_ref.at[part, pl.ds(8 * at, 8)],
-                stage_sem.at[part],
+    def core_copy(unit, src):
+        return send_to(
+            src.at[:, :, :, :, 1 - core],
+            sum0.at[unit],
+            ssend_sem.at[0, unit],
+            srecv_sem.at[0, unit],
+            (tab, 2 * chip + 1 - core),
+        )
+
+    def axis_copy(unit, order):
+        if order == 0:
+            src, there = sum0.at[unit, :, 1 - x], 2 * y + 1 - x
+        else:
+            src, there = sum0.at[unit, 1 - y], 2 * (1 - y) + x
+        return send_to(
+            src, sum1.at[unit], ssend_sem.at[1, unit], srecv_sem.at[1, unit], (there, blk)
+        )
+
+    def add_core(unit, parts):
+        landed(sum0.at[unit], srecv_sem.at[0, unit])
+        for a in range(2):
+            for b in range(2):
+                sum0[unit, a, b] = sum0[unit, a, b] + parts[a, b, :, :, core]
+
+    @pl.loop(0, chunks)
+    def _(at):
+        wdown = jnp.dot(active_t[at], gbranch[...], preferred_element_type=f32)
+        wdown = wdown.reshape(8, 4, each, width)
+        for part in range(4):
+            dparts[part, at // 2, lax.rem(at, 2)] = (
+                halves(wdown[:, part]).astype(bf16).reshape(dparts.shape[3:])
             )
-            for part in range(4)
-        ]
-
-    def up_copy(at):
-        return pltpu.make_async_copy(stage_u, parts_ref.at[4 + at], stage_sem.at[4])
+
+    for unit in range(4):
+        core_copy(unit, dparts.at[unit]).start()
 
     @pl.loop(0, chunks)
     def _(at):
         cut = pl.ds(pl.multiple_of(at * width, width), width)
-        wdown = jnp.dot(active_t[at], gbranch[...], preferred_element_type=f32)
-        wdown = wdown.reshape(8, 4, each, width)
-
-        @pl.when(at > 0)
+
+        @pl.when(jnp.logical_or(at == 1, at == 2))
         def _():
-            for copy in down_copies(at - 1):
-                copy.wait()
-            up_copy(at - 1).wait()
-
-        for part in range(4):
-            stage_d[part] = halves(wdown[:, part]).astype(bf16)
-        for copy in down_copies(at):
-            copy.start()
+            for unit in (2 * at - 2, 2 * at - 1):
+                add_core(unit, dparts.at[unit])
+                by_core(core, lambda order, unit=unit: axis_copy(unit, order).start())
+
         gact = times_t(gbranch[...], downw[cut])
         gup = (gact * slopes[at]).astype(bf16)
         small_ref[pl.ds(6 + at, 1)] = column_sum(gup)
         ghid[...] += times_t(gup, upw[:, cut])
         wup = jnp.dot(hlow_t[...], gup, preferred_element_type=f32)
-        stage_u[...] = halves(wup.reshape(32, each, width)).astype(bf16)
-        up_copy(at).start()
-
-    for copy in down_copies(chunks - 1):
-        copy.wait()
-    up_copy(chunks - 1).wait()
+        uparts[at] = halves(wup.reshape(32, each, width)).astype(bf16).reshape(uparts.shape[1:])
+        core_copy(4 + at, uparts.at[at]).start()
+
     small = [0.0, 0.0, 0.0]
     lows = []
-    for table in range(tables):
+    for table in range(sides):
         cut = pl.ds(table * rows, rows)
         grad, normed = ghid[cut], norm1[cut]
         small[1] += column_sum(grad * normed)
@@ -1469,29 +1630,47 @@
         low = gpre1.astype(bf16)
         small[0] += column_sum(low)
         lows.append(low)
-        for group in range(groups):
-            dctx_ref[table, group] = fold(
-                times_t(low, outw_ref[group * cols : (group + 1) * cols]).astype(bf16)
-            )
+    low = jnp.concatenate(lows, axis=0)
     for at in range(3):
         small_ref[at : at + 1] = small[at]
     small_ref[10:] = jnp.zeros((6, width), f32)
+    wouts = []
     for group in range(groups):
-        wout = 0.0
-        for table in range(tables):
-            wout += jnp.dot(
-                unfold(ctx_ref[table, group]).T, lows[table], preferred_element_type=f32
-            )
-        stage_u[group * 8 : (group + 1) * 8] = halves(wout.reshape(8, each, width)).astype(bf16)
-    last = pltpu.make_async_copy(stage_u, parts_ref.at[8], stage_sem.at[4])
-    last.start()
-    last.wait()
+        dctx_ref[group] = fold(
+            times_t(low, outw_ref[group * cols : (group + 1) * cols]).astype(bf16)
+        )
+        wout = jnp.dot(unfold(ctx_ref[group]).T, low, preferred_element_type=f32)
+        wouts.append(halves(wout.reshape(8, each, width)).astype(bf16))
+    for unit in range(4):
+        core_copy(unit, dparts.at[unit]).wait_send()
+    dparts[0] = jnp.concatenate(wouts, axis=0).reshape(dparts.shape[1:])
+    keep = [pltpu.make_async_copy(dparts.at[0], parts_ref, keep_sem.at[0])]
+
+    @pl.loop(0, 4)
+    def _(at):
+        add_core(4 + at, uparts.at[at])
+        landed(sum1.at[at], srecv_sem.at[1, at])
+
+        def act(order):
+            sum1[at] = sum1[at] + (sum0[at, :, x] if order == 0 else sum0[at, y])
+            axis_copy(at, order).wait_send()
+
+        by_core(core, act)
+        core_copy(4 + at, uparts.at[at]).wait_send()
+
+    keep.append(pltpu.make_async_copy(sum1, down_ref, keep_sem.at[1]))
+    keep.append(pltpu.make_async_copy(sum0.at[4:], up_ref, keep_sem.at[2]))
+    for copy in keep:
+        copy.start()
+    return_rows(out, layer_ref, osend_sem, orecv_sem, "wait")
+    for copy in keep:
+        copy.wait()
 
 
 def ffn(tokens, ctx, cotangent, params, out_weight, up_weight, down_weight):
     total, width = tokens.shape
     chunks = up_weight.shape[1] // width
-    each = width // 32
+    unit = (2 * (width // 32), width // 2)
     any_space = pl.BlockSpec(memory_space=pl.ANY)
     vmem = pl.BlockSpec(memory_space=pltpu.VMEM)
     bf16, f32 = jnp.bfloat16, jnp.float32
@@ -1500,14 +1679,16 @@
         ffn_kernel,
         name="ffn",
         out_shape=(
-            jax.ShapeDtypeStruct((total, width), bf16),
+            jax.ShapeDtypeStruct((2, total // 2, width), bf16),
             jax.ShapeDtypeStruct(ctx.shape, bf16),
             jax.ShapeDtypeStruct((total, width), f32),
             jax.ShapeDtypeStruct((16, width), f32),
-            jax.ShapeDtypeStruct((9, 32, 2 * each, width // 2), bf16),
+            jax.ShapeDtypeStruct((4, 2, 2, 2, *unit), bf16),
+            jax.ShapeDtypeStruct((4, 2, 2, 2, 2, *unit), bf16),
+            jax.ShapeDtypeStruct((2, 2, 2, 2, 2, *unit), bf16),
         ),
         in_specs=[vmem, vmem, vmem, vmem, vmem, any_space, any_space],
-        out_specs=(vmem, vmem, vmem, vmem, any_space),
+        out_specs=(any_space, vmem, vmem, vmem, any_space, any_space, any_space),
         scratch_shapes=[
             pltpu.VMEM(up_weight.shape, bf16),
             pltpu.VMEM(down_weight.shape, bf16),
@@ -1520,27 +1701,25 @@
             pltpu.VMEM((total, width), f32),
             pltpu.VMEM((total, width), bf16),
             pltpu.VMEM((total, width), f32),
-            pltpu.VMEM((4, 8, 2 * each, width // 2), bf16),
-            pltpu.VMEM((32, 2 * each, width // 2), bf16),
+            pltpu.VMEM((2, total // 2, width), bf16),
+            pltpu.VMEM((4, 2, 2, 2, 2, 2, *unit), bf16),
+            pltpu.VMEM((4, 2, 2, 2, 2, 2, *unit), bf16),
+            pltpu.VMEM((8, 2, 2, 2, 2, *unit), bf16),
+            pltpu.VMEM((4, 2, 2, 2, *unit), bf16),
             pltpu.SemaphoreType.DMA((2,)),
-            pltpu.SemaphoreType.DMA((5,)),
+            pltpu.SemaphoreType.DMA((3,)),
+            pltpu.SemaphoreType.DMA((2,)),
+            pltpu.SemaphoreType.DMA((2,)),
+            pltpu.SemaphoreType.DMA((2, 8)),
+            pltpu.SemaphoreType.DMA((2, 8)),
         ],
-        compiler_params=pltpu.CompilerParams(vmem_limit_bytes=60 << 20),
+        compiler_params=pltpu.CompilerParams(
+            collective_id=3, has_side_effects=True, vmem_limit_bytes=63 << 20
+        ),
         cost_estimate=pl.CostEstimate(
             flops=flops, bytes_accessed=40 << 20, transcendentals=total * width * chunks
         ),
     )(tokens, ctx, cotangent, params, out_weight, up_weight, down_weight)
-
-
-def scatter_sum(grad):
-    return lax.psum_scatter(
-        lax.psum_scatter(
-            grad.astype(jnp.bfloat16), "tab", scatter_dimension=0, tiled=True
-        ),
-        "blk",
-        scatter_dimension=0,
-        tiled=True,
-    ).astype(jnp.float32)
 
 
 def shards_direct(
@@ -1563,7 +1742,6 @@
     tables, rows, width = tokens.shape
     f32 = jnp.float32
     heads = width // HD // GROUPS
-    flat_tokens = tokens.reshape(tables * rows, width)
     row = lax.broadcasted_iota(jnp.int32, (32, width), 0)
     params = jnp.zeros((32, width), jnp.bfloat16)
     spans = [
@@ -1581,22 +1759,26 @@
         params = jnp.where((row >= first) & (row < last), vector[None], params)
 
     params = params.astype(f32)
-    ctx, full_t, qkv, ot, lse, by_head = attend(tokens, lengths, params, qkv_weight, heads)
-    layer_out, dctx, pre, small, parts = ffn(
-        flat_tokens,
+    ctx, my_tokens, my_cotangent, full_t, qkv, ot, lse, by_head = attend(
+        tokens, lengths, params, qkv_weight, cotangent, heads
+    )
+    layer_out, dctx, pre, small, down, up, parts = ffn(
+        my_tokens.reshape(tables * rows, width),
         ctx,
-        cotangent.reshape(tables * rows, width),
+        my_cotangent.reshape(tables * rows, width),
         params,
         out_weight,
         up_weight,
         down_weight,
     )
     *whole, little = attend_back(
-        dctx, qkv, ot, lse, full_t, by_head, pre, small, parts, heads
+        dctx, qkv, ot, lse, full_t, by_head, pre, small, down, up, parts, heads
     )
     each = width // 32
+    whole.insert(1, layer_out)
     (
         token_grad,
+        layer_out,
         wgrad_qkv,
         wgrad_out,
         wgrad_up,
@@ -1611,7 +1793,7 @@
         bgrad_qkv,
     ) = finish(whole, little, [each] * 6 + [4 * each, 2 * each])
     return (
-        layer_out.reshape(tokens.shape),
+        layer_out,
         token_grad,
         wgrad_qkv,
         bgrad_qkv,

time: 215 us -> 206 us (0.958)
  Pallas kernels: 210 us -> 203 us
    pallas_call x1, Pallas kernels: 110 us -> 101 us  [attend_back(): pl.pallas_call(functools.partial(attend_back_kernel, heads), name='attend...]
    pallas_call x1, Pallas kernels: 35.8 us -> 40.8 us  [ffn(): pl.pallas_call(ffn_kernel, name='ffn', out_shape=(jax.ShapeDtypeStruct((2...]
    pallas_call x1, Pallas kernels: 62 us -> 57.7 us  [attend(): pl.pallas_call(functools.partial(attend_kernel, heads), name='attend', ou...]
where the time goes in v4:
time: 206 us
  Pallas kernels  203 us (99%)
    pallas_call x1, Pallas kernels, attend_back(): pl.pallas_call(functools.partial(attend_back_kernel, heads), name='attend...  101 us
    pallas_call x1, Pallas kernels, attend(): pl.pallas_call(functools.partial(attend_kernel, heads), name='attend', ou...  57.7 us
    pallas_call x1, Pallas kernels, ffn(): pl.pallas_call(ffn_kernel, name='ffn', out_shape=(jax.ShapeDtypeStruct((2...  40.8 us

profile of v4, /device:TPU:0, one launch (start us, length us, event | category | flops | bytes accessed | tf_op | source)
XLA Modules:
  0.0 205.9 jit_solution(3361202651571629104)
XLA Ops:
  0.7 0.8 fusion
  1.5 1.5 select_convert_fusion.par_ref
  3.0 57.7 %attend.1 = (bf16[4,256,384]{2,1,0:T(8,128)(2,1)}, bf16[2,256,768]{2,1,0:T(8,128)(2,1)}, bf16[2,256,768]{2,1,0:T(8,128)(2,1)}, bf16[768,2048]{1,0:T(8,128)(2,1)}...) custom-call(bf16[2,256,768]{2,1,0:T(8,128)(2,1)} %tok_ref.1, ...), custom_call_target="tpu_custom_call" | custom-call | tf_op jit(solution)/shard_map/attend/pallas_call | solution.py:744
  60.8 40.8 %ffn.1 = (bf16[2,256,768]{2,1,0:T(8,128)(2,1)}, bf16[4,256,384]{2,1,0:T(8,128)(2,1)}, f32[512,768]{1,0:T(8,128)}, f32[16,768]{1,0:T(8,128)}, bf16[4,2,2,2,48,384...) custom-call(bf16[512,768]{1,0:T(8,128)(2,1)} %bitcast.2, ...), custom_call_target="tpu_custom_call" | custom-call | flops 23555211264 | bytes 41943040 | tf_op jit(solution)/shard_map/ffn/pallas_call | solution.py:1678
  101.5 101.0 %attend_back.1 = (bf16[2,256,768]{2,1,0:T(8,128)(2,1)}, f32[24,2304]{1,0:T(8,128)}, f32[24,768]{1,0:T(8,128)}, f32[24,3072]{1,0:T(8,128)}, f32[96,768]{1,0:T(8,128)}, /*index=5*/f32[8,128]{1,0:T(8,128)}) custom-call(bf16[4,256,384]{2,1,0:T(8,128)(2,1)} %get-tuple-element.52.dctx_ref, bf16[9,2048,128]{2,1,0:T(8,128)(2,1)} %get-tuple-element.53.qkv_ref, ...), custom_call_target="tpu_custom_call" | custom-call | tf_op jit(solution)/shard_map/attend_back/pallas_call | solution.py:1344
  202.6 3.1 %finish.1 = (bf16[2,256,768]{2,1,0:T(8,128)(2,1)}, bf16[2,256,768]{2,1,0:T(8,128)(2,1)}, f32[24,2304]{1,0:T(8,128)}, f32[24,768]{1,0:T(8,128)}, f32[24,3072]{1,0...) custom-call(bf16[2,256,768]{2,1,0:T(8,128)(2,1)} %get-tuple-element., ...), custom_call_target="tpu_custom_call" | custom-call | tf_op jit(solution)/shard_map/finish/pallas_call | solution.py:1427
  (6 shorter events, 0.0 us)
